TPU v7x, 32 devices: a whole 2x2x4 slice. The times are simulated.
32 devices in a mesh: dp: 4 (over y, x), expert: 8 (over z, core).
Axes of the slice: x: 2, y: 2, z: 4, core: 2. Of those that a mesh axis runs over, the one named last changes fastest.
Arguments:
- tokens: bfloat16 [2048, 4096], P(('dp', 'expert')), may hold values from -6 to 6
- grads_out: bfloat16 [2048, 4096], P(('dp', 'expert')), may hold values from -6 to 6
- routes: int32 [2048, 2], P(('dp', 'expert')), may hold values from 0 to 31, all different within a row; in each aligned block of 64 rows (0 to 63, 64 to 127, ...) at most 4 rows name the same one
- route_weights: float32 [2048, 2], P(('dp', 'expert')), may hold values from 0.2 to 1
- depth_filter: float32 [32, 5, 512], P('expert'), may hold values from -2.5 to 2.5
- point_weight: bfloat16 [512, 32, 1024], P('dp', 'expert'), may hold values from -0.25 to 0.25
Outputs:
- mixed: bfloat16 [2048, 4096], P(('dp', 'expert'))
- token_grads: bfloat16 [2048, 4096], P(('dp', 'expert'))
- point_grads: float32 [512, 32, 1024], P('dp', 'expert')
- depth_grads: float32 [32, 5, 512], P('expert')
Inputs may be any that keep to these rules, and one draw needn't show every extreme that they name: `routes`: the two experts of a frame differ; among the 64 frames of one device no expert is named more than 4 times.
All inputs are finite; a program needn't handle non-finite values.
Results may differ from a plain program's by a relative error of at most 0.0095.
Values may be sent and summed in bfloat16 or wider, within the bound.
No kernel may reach another device: no remote copies, remote signals or barrier semaphores. Data moves between devices by JAX's collectives and lax.ppermute only.
A program may use at most 64 MiB of HBM per device.

v0:
```python
import jax
import jax.numpy as jnp
from jax import lax
from jax.sharding import PartitionSpec as P

KERNEL_TAPS = 5
DILATION_STEP = 2
CAP = 4


def shifted_input(field, tap_offset):
    width = field.shape[-2]
    pads = [(0, 0)] * (field.ndim - 2) + [(abs(tap_offset), abs(tap_offset)), (0, 0)]
    padded = jnp.pad(field, pads)
    begin = abs(tap_offset) + tap_offset
    return lax.slice_in_dim(padded, begin, begin + width, axis=field.ndim - 2)


def shards(tokens, grads_out, routes, route_weights, depth_filter, point_weight):
    tok_count = tokens.shape[0]
    dev_count = lax.axis_size("expert")
    exp_local = depth_filter.shape[0]
    exp_total = exp_local * dev_count
    slot_count = 2 * tok_count
    frame_width = tokens.shape[1]
    channels = point_weight.shape[2] // 2
    bins = frame_width // channels
    route_flat = routes.reshape(slot_count)
    onehot = (route_flat[:, None] == jnp.arange(exp_total, dtype=jnp.int32)[None, :]).astype(
        jnp.int32
    )
    ranks = jnp.sum((jnp.cumsum(onehot, axis=0) - 1) * onehot, axis=1)
    slot_ids = route_flat * CAP + ranks
    placing = (slot_ids[None, :] == jnp.arange(exp_total * CAP, dtype=jnp.int32)[:, None]).astype(
        jnp.bfloat16
    )
    tokens_twice = jnp.repeat(tokens, 2, axis=0)
    cotan_twice = (
        route_weights.reshape(slot_count, 1) * jnp.repeat(grads_out, 2, axis=0).astype(jnp.float32)
    ).astype(jnp.bfloat16)
    send_frames = jnp.dot(placing, tokens_twice, preferred_element_type=jnp.float32).astype(
        jnp.bfloat16
    )
    send_cotan = jnp.dot(placing, cotan_twice, preferred_element_type=jnp.float32).astype(
        jnp.bfloat16
    )
    send_frames = send_frames.reshape(dev_count, exp_local * CAP, frame_width)
    send_cotan = send_cotan.reshape(dev_count, exp_local * CAP, frame_width)

    def to_local(buffer):
        shaped = buffer.reshape(dev_count, exp_local, CAP, bins, channels)
        return jnp.transpose(shaped, (1, 0, 2, 3, 4)).reshape(
            exp_local, dev_count * CAP, bins, channels
        )

    def to_source(buffer):
        shaped = buffer.reshape(exp_local, dev_count, CAP, frame_width)
        return jnp.transpose(shaped, (1, 0, 2, 3)).reshape(dev_count, exp_local * CAP, frame_width)

    recv_frames, recv_cotan = (
        lax.all_to_all(send_frames, "expert", split_axis=0, concat_axis=0, tiled=True),
        lax.all_to_all(send_cotan, "expert", split_axis=0, concat_axis=0, tiled=True),
    )
    input_frames = to_local(recv_frames).astype(jnp.float32)
    hidden_state = jnp.zeros(input_frames.shape, jnp.float32)
    for tap_index in range(KERNEL_TAPS):
        hidden_state = hidden_state + depth_filter[:, tap_index][:, None, None, :] * shifted_input(
            input_frames, DILATION_STEP * (tap_index - KERNEL_TAPS // 2)
        )
    hidden_state = hidden_state.astype(jnp.bfloat16)
    full_filter = lax.all_gather(point_weight, "dp", axis=0, tiled=True)
    preact = jnp.einsum(
        "erpc,ceo->erpo", hidden_state, full_filter, preferred_element_type=jnp.float32
    )
    value_half = preact[..., :channels]
    gate_sig = jax.nn.sigmoid(preact[..., channels:])
    expert_out = (value_half * gate_sig).astype(jnp.bfloat16)
    cotan = to_local(recv_cotan).astype(jnp.float32)
    dpre = jnp.concatenate(
        [cotan * gate_sig, cotan * value_half * gate_sig * (1.0 - gate_sig)], axis=-1
    ).astype(jnp.bfloat16)
    dhidden = jnp.einsum("erpo,ceo->erpc", dpre, full_filter, preferred_element_type=jnp.float32)
    frame_grad = jnp.zeros(input_frames.shape, jnp.float32)
    tap_grads = []
    for tap_index in range(KERNEL_TAPS):
        tap_offset = DILATION_STEP * (tap_index - KERNEL_TAPS // 2)
        frame_grad = frame_grad + depth_filter[:, tap_index][:, None, None, :] * shifted_input(
            dhidden, -tap_offset
        )
        tap_grads.append(jnp.sum(dhidden * shifted_input(input_frames, tap_offset), axis=(1, 2)))
    frame_grad = frame_grad.astype(jnp.bfloat16)
    depth_grads = lax.psum(jnp.stack(tap_grads, axis=1).astype(jnp.bfloat16), "dp").astype(
        jnp.float32
    )
    point_grads = lax.psum_scatter(
        jnp.einsum("erpc,erpo->ceo", hidden_state, dpre, preferred_element_type=jnp.float32).astype(
            jnp.bfloat16
        ),
        "dp",
        scatter_dimension=0,
        tiled=True,
    ).astype(jnp.float32)
    back_out, back_grad = (
        lax.all_to_all(to_source(expert_out), "expert", split_axis=0, concat_axis=0, tiled=True),
        lax.all_to_all(to_source(frame_grad), "expert", split_axis=0, concat_axis=0, tiled=True),
    )
    back_out = back_out.reshape(exp_total * CAP, frame_width)
    back_grad = back_grad.reshape(exp_total * CAP, frame_width)
    slot_out = jnp.dot(placing.T, back_out, preferred_element_type=jnp.float32).reshape(
        tok_count, 2, frame_width
    )
    slot_grad = jnp.dot(placing.T, back_grad, preferred_element_type=jnp.float32).reshape(
        tok_count, 2, frame_width
    )
    mixed = jnp.sum(route_weights[:, :, None] * slot_out, axis=1).astype(jnp.bfloat16)
    token_grads = jnp.sum(slot_grad, axis=1).astype(jnp.bfloat16)
    return (mixed, token_grads, point_grads, depth_grads)


def solution(mesh):
    placed = (
        P(("dp", "expert"), None),
        P(("dp", "expert"), None),
        P(("dp", "expert"), None),
        P(("dp", "expert"), None),
        P("expert", None, None),
        P("dp", "expert", None),
    )
    return jax.shard_map(
        shards,
        mesh=mesh,
        in_specs=placed,
        out_specs=(
            P(("dp", "expert"), None),
            P(("dp", "expert"), None),
            P("dp", "expert", None),
            P("expert", None, None),
        ),
        check_vma=False,
    )
```

profile of v0, /device:TPU:0, one launch (start us, length us, event | category | flops | bytes accessed | tf_op | source)
XLA Modules:
  0.0 179.3 jit_solution(13614706876543647294)
XLA Ops:
  7.2 2.6 %copy.51 = bf16[128,4,1024]{2,0,1:T(8,128)(2,1)} copy(bf16[128,4,1024]{2,1,0:T(4,128)(2,1)} %param.11) | data formatting | bytes 2097152 | tf_op args[5]
  10.1 1.0 broadcast_in_dim.4
  12.0 1.4 convolution_convert_fusion.1
  13.4 6.3 %all-to-all-start = ((bf16[8,16,4096]{2,1,0:T(8,128)(2,1)}), bf16[8,16,4096]{2,1,0:T(8,128)(2,1)S(1)}, u32[]{:S(2)}, u32[]{:S(2)}) async-start(bf16[8,16,4096]{2,1,0:T(8,128)(2,1)} %bitcast.2), calls=%async_computation | async-start | bytes 2097152 | tf_op jit(solution)/shard_map/all_to_all | solution.py:61
  19.8 2.1 %broadcast_in_dim.5 = f32[64,2,4096]{2,1,0:T(2,128)S(1)} broadcast(bf16[64,4096]{1,0:T(8,128)(2,1)} %param.7), dimensions={0,2} | broadcast | bytes 2621440 | tf_op jit(solution)/shard_map/broadcast_in_dim | solution.py:39
  21.9 2.4 %convert_element_type.97 = f32[128,4096]{1,0:T(8,128)} reshape(f32[64,2,4096]{2,1,0:T(2,128)S(1)} %broadcast_in_dim.5) | data formatting | bytes 4194304 | tf_op jit(solution)/shard_map/convert_element_type | solution.py:39
  24.6 3.1 %convolution_convert_fusion = bf16[128,4096]{1,0:T(8,128)(2,1)} fusion(f32[128,4096]{1,0:T(8,128)} %convert_element_type.97, f32[128]{0:T(128)S(1)} %mul.169, s32[128]{0:T(128)S(1)} %multiply_add_fusion.1), kind=kOutput, calls=%fused_computation.10 | convolution fusion | flops 135806976 | bytes 3146752 | tf_op jit(solution)/shard_map/dot_general | solution.py:44
  27.7 18.6 %all-to-all-done = bf16[8,16,4096]{2,1,0:T(8,128)(2,1)S(1)} async-done(((bf16[8,16,4096]{2,1,0:T(8,128)(2,1)}), bf16[8,16,4096]{2,1,0:T(8,128)(2,1)S(1)}, u32[]{:S(2)}, u32[]{:S(2)}) %all-to-all-start) | async-done | bytes 1048608 | tf_op jit(solution)/shard_map/all_to_all | solution.py:61
  46.3 4.2 %all-to-all-start.2 = ((bf16[8,16,4096]{2,1,0:T(8,128)(2,1)}), bf16[8,16,4096]{2,1,0:T(8,128)(2,1)}, u32[]{:S(2)}, u32[]{:S(2)}) async-start(bf16[8,16,4096]{2,1,0:T(8,128)(2,1)} %bitcast.16), calls=%async_computation.2 | async-start | bytes 2097152 | tf_op jit(solution)/shard_map/all_to_all | solution.py:62
  51.5 25.7 %all-to-all-done.2 = bf16[8,16,4096]{2,1,0:T(8,128)(2,1)} async-done(((bf16[8,16,4096]{2,1,0:T(8,128)(2,1)}), bf16[8,16,4096]{2,1,0:T(8,128)(2,1)}, u32[]{:S(2)}, u32[]{:S(2)}) %all-to-all-start.2) | async-done | bytes 1048608 | tf_op jit(solution)/shard_map/all_to_all | solution.py:62
  77.2 1.6 copy.66
  78.8 1.5 copy.55
  80.3 1.2 add_convert_fusion
  81.6 3.6 %fusion.2 = f32[4,32,8,1024]{3,2,1,0:T(8,128)S(1)} fusion(bf16[4,32,8,512]{3,2,1,0:T(8,128)(2,1)S(1)} %add_convert_fusion, bf16[512,4,1024]{2,0,1:T(8,128)(2,1)} %all-gather.2.cloned.1.call-done), kind=kOutput, calls=%fused_computation.14 | convolution fusion | flops 1073741824 | bytes 9437184 | tf_op jit(solution)/shard_map/erpc,ceo->erpo/dot_general | solution.py:72
  85.2 2.1 %multiply_convert_fusion.1 = (bf16[4,32,8,512]{3,2,1,0:T(8,128)(2,1)S(1)}, bf16[4,32,8,512]{3,2,1,0:T(8,128)(2,1)S(1)}, bf16[4,32,8,512]{3,2,1,0:T(8,128)(2,1)}) fusion(f32[4,32,8,512]{3,2,1,0:T(8,128)S(1)} %bitcast.82, f32[4,32,8,1024]{3,2,1,0:T(8,128)S(1)} %fusion.2), kind=kLoop, calls=%fused_computation.36 | loop fusion | flops 6291456 | bytes 9437184 | tf_op jit(solution)/shard_map/convert.16
  87.3 3.3 %bitcast_convert_fusion = bf16[4,1024,512]{2,1,0:T(8,128)(2,1)} fusion(bf16[4,32,8,512]{3,2,1,0:T(8,128)(2,1)S(1)} %add_convert_fusion, bf16[4,32,8,512]{3,2,1,0:T(8,128)(2,1)S(1)} %get-tuple-element.26, bf16[4,32,8,512]{3,2,1,0:T(8,128)(2,1)S(1)} %get-tuple-element.25), kind=kOutput, calls=%fused_computation | convolution fusion | flops 1080033280 | bytes 7340032 | tf_op jit(solution)/shard_map/erpc,erpo->ceo/dot_general | solution.py:96
  90.6 6.5 %copy.63 = bf16[512,4096]{1,0:T(8,128)(2,1)} copy(bf16[512,4096]{0,1:T(8,128)(2,1)} %bitcast.85) | data formatting | bytes 8388608
  97.1 1.2 copy-done.3
  98.3 3.8 %fusion = f32[4,32,8,512]{3,2,1,0:T(8,128)S(1)} fusion(bf16[512,4,1024]{2,0,1:T(8,128)(2,1)} %all-gather.2.cloned.1.call-done, bf16[4,32,8,512]{3,2,1,0:T(8,128)(2,1)} %copy-done.4, bf16[4,32,8,512]{3,2,1,0:T(8,128)(2,1)S(1)} %copy-done.3), kind=kOutput, calls=%fused_computation.12 | convolution fusion | flops 1077936128 | bytes 8388608 | tf_op jit(solution)/shard_map/erpo,ceo->erpc/dot_general | solution.py:82
  102.1 2.5 %multiply_reduce_fusion = (bf16[4,512]{1,0:T(4,128)(2,1)S(1)}, bf16[4,512]{1,0:T(4,128)(2,1)S(1)}, bf16[4,512]{1,0:T(4,128)(2,1)S(1)}, bf16[4,512]{1,0:T(4,128)(...) fusion(f32[4,32,8,512]{3,2,1,0:T(8,128)S(1)} %fusion, f32[4,32,8,512]{3,2,1,0:T(8,128)S(1)} %bitcast.79, ...), kind=kLoop, calls=%fused_computation.30 | loop fusion | flops 10475520 | bytes 5304320 | tf_op jit(solution)/shard_map/reduce_sum | solution.py:90
  106.1 1.6 copy.57
  107.6 3.8 %all-to-all-start.3 = ((bf16[8,16,4096]{2,1,0:T(8,128)(2,1)}), bf16[8,16,4096]{2,1,0:T(8,128)(2,1)S(1)}, u32[]{:S(2)}, u32[]{:S(2)}) async-start(bf16[8,16,4096]{2,1,0:T(8,128)(2,1)} %copy.57), calls=%async_computation.3 | async-start | bytes 2097152 | tf_op jit(solution)/shard_map/all_to_all | solution.py:105
  111.4 0.8 reshape.97
  112.8 1.6 copy.53
  114.4 23.3 %all-to-all-done.3 = bf16[8,16,4096]{2,1,0:T(8,128)(2,1)S(1)} async-done(((bf16[8,16,4096]{2,1,0:T(8,128)(2,1)}), bf16[8,16,4096]{2,1,0:T(8,128)(2,1)S(1)}, u32[]{:S(2)}, u32[]{:S(2)}) %all-to-all-start.3) | async-done | bytes 1048608 | tf_op jit(solution)/shard_map/all_to_all | solution.py:105
  137.7 3.6 %all-to-all-start.1 = ((bf16[8,16,4096]{2,1,0:T(8,128)(2,1)}), bf16[8,16,4096]{2,1,0:T(8,128)(2,1)S(1)}, u32[]{:S(2)}, u32[]{:S(2)}) async-start(bf16[8,16,4096]{2,1,0:T(8,128)(2,1)} %copy.53), calls=%async_computation.1 | async-start | bytes 2097152 | tf_op jit(solution)/shard_map/all_to_all | solution.py:104
  141.6 16.2 %psum.7 = bf16[4,5,512]{2,0,1:T(4,128)(2,1)S(1)} all-reduce(bf16[4,5,512]{2,0,1:T(4,128)(2,1)S(1)} %constant_dynamic-update-slice_fusion), channel_id=1, replica_groups=mesh['dp'=4,'expert'=8] {'dp'}, use_global_device_ids=true, to_apply=%region_10.11 | all-reduce | flops 10240 | bytes 40960 | tf_op jit(solution)/shard_map/psum | solution.py:92
  158.4 1.3 convolution_reduce_fusion
  159.7 8.1 %all-to-all-done.1 = bf16[8,16,4096]{2,1,0:T(8,128)(2,1)S(1)} async-done(((bf16[8,16,4096]{2,1,0:T(8,128)(2,1)}), bf16[8,16,4096]{2,1,0:T(8,128)(2,1)S(1)}, u32[]{:S(2)}, u32[]{:S(2)}) %all-to-all-start.1) | async-done | bytes 1048608 | tf_op jit(solution)/shard_map/all_to_all | solution.py:104
  167.8 1.3 fusion.16
  169.1 1.6 copy.64
  170.7 1.8 copy.58
  (47 shorter events, 5.2 us)
Async XLA Ops:
  7.2 2.7 %copy-start.8 = (s32[64,2]{0,1:T(2,128)S(1)}, s32[64,2]{0,1:T(2,128)}, u32[]{:S(2)}) copy-start(s32[64,2]{0,1:T(2,128)} %param.8) | copy-start | bytes 1540
  7.2 2.9 %copy-start.5 = (bf16[64,4096]{1,0:T(8,128)(2,1)S(1)}, bf16[64,4096]{1,0:T(8,128)(2,1)}, u32[]{:S(2)}) copy-start(bf16[64,4096]{1,0:T(8,128)(2,1)} %param.6) | copy-start | bytes 1572868
  7.2 74.4 %all-gather.2.cloned.1.call-start = ((), (), s32[]{:S(2)}) async-start(), calls=%async_computation.5 | async-start | bytes 5242880 | tf_op jit(solution)/shard_map/all_gather | solution.py:71
  13.4 32.9 %all-to-all-start = ((bf16[8,16,4096]{2,1,0:T(8,128)(2,1)}), bf16[8,16,4096]{2,1,0:T(8,128)(2,1)S(1)}, u32[]{:S(2)}, u32[]{:S(2)}) async-start(bf16[8,16,4096]{2,1,0:T(8,128)(2,1)} %bitcast.2), calls=%async_computation | async-start | bytes 2097152 | tf_op jit(solution)/shard_map/all_to_all | solution.py:61
  21.9 2.5 %copy-start.7 = (f32[64,2]{0,1:T(2,128)S(1)}, f32[64,2]{0,1:T(2,128)}, u32[]{:S(2)}) copy-start(f32[64,2]{0,1:T(2,128)} %param.9) | copy-start | bytes 1540
  24.6 26.2 %copy-start.6 = (f32[4,5,512]{2,0,1:T(4,128)S(1)}, f32[4,5,512]{2,0,1:T(4,128)}, u32[]{:S(2)}) copy-start(f32[4,5,512]{2,0,1:T(4,128)} %param.10) | copy-start | bytes 122884
  46.3 30.8 %all-to-all-start.2 = ((bf16[8,16,4096]{2,1,0:T(8,128)(2,1)}), bf16[8,16,4096]{2,1,0:T(8,128)(2,1)}, u32[]{:S(2)}, u32[]{:S(2)}) async-start(bf16[8,16,4096]{2,1,0:T(8,128)(2,1)} %bitcast.16), calls=%async_computation.2 | async-start | bytes 2097152 | tf_op jit(solution)/shard_map/all_to_all | solution.py:62
  50.6 118.5 %reduce-scatter.4.cloned.1.call-start = ((), (), s32[]{:S(2)}) async-start(), calls=%async_computation.6 | async-start | bytes 5242880
  81.6 3.6 %copy-start = (f32[4,8,4,8,512]{4,3,2,1,0:T(8,128)S(1)}, f32[4,8,4,8,512]{4,3,2,1,0:T(8,128)}, u32[]{:S(2)}) copy-start(f32[4,8,4,8,512]{4,3,2,1,0:T(8,128)} %copy.55) | copy-start | bytes 6291460
  87.3 3.3 %copy-start.2 = (bf16[4,32,8,512]{3,2,1,0:T(8,128)(2,1)}, bf16[4,32,8,512]{3,2,1,0:T(8,128)(2,1)S(1)}, u32[]{:S(2)}) copy-start(bf16[4,32,8,512]{3,2,1,0:T(8,128)(2,1)S(1)} %get-tuple-element.25) | copy-start | bytes 3145732
  87.3 3.3 %copy-start.4 = (bf16[4,32,8,512]{3,2,1,0:T(8,128)(2,1)}, bf16[4,32,8,512]{3,2,1,0:T(8,128)(2,1)S(1)}, u32[]{:S(2)}) copy-start(bf16[4,32,8,512]{3,2,1,0:T(8,128)(2,1)S(1)} %get-tuple-element.26) | copy-start | bytes 3145732
  97.1 1.2 copy-start.3
  106.0 5.4 %copy-start.1 = (bf16[4,32,8,512]{3,2,1,0:T(8,128)(2,1)S(1)}, bf16[4,32,8,512]{3,2,1,0:T(8,128)(2,1)}, u32[]{:S(2)}) copy-start(bf16[4,32,8,512]{3,2,1,0:T(8,128)(2,1)} %get-tuple-element.27) | copy-start | bytes 3145732
  107.6 30.1 %all-to-all-start.3 = ((bf16[8,16,4096]{2,1,0:T(8,128)(2,1)}), bf16[8,16,4096]{2,1,0:T(8,128)(2,1)S(1)}, u32[]{:S(2)}, u32[]{:S(2)}) async-start(bf16[8,16,4096]{2,1,0:T(8,128)(2,1)} %copy.57), calls=%async_computation.3 | async-start | bytes 2097152 | tf_op jit(solution)/shard_map/all_to_all | solution.py:105
  137.7 30.1 %all-to-all-start.1 = ((bf16[8,16,4096]{2,1,0:T(8,128)(2,1)}), bf16[8,16,4096]{2,1,0:T(8,128)(2,1)S(1)}, u32[]{:S(2)}, u32[]{:S(2)}) async-start(bf16[8,16,4096]{2,1,0:T(8,128)(2,1)} %copy.53), calls=%async_computation.1 | async-start | bytes 2097152 | tf_op jit(solution)/shard_map/all_to_all | solution.py:104
Sparse Core Ops, SparseCore 0:
  9.9 55.3 all-gather.1
  97.2 51.7 reduce-scatter.3
where the time goes:
time: 180 us; the launch traced here: 179 us
  waiting for transfers between devices  75.8 us (42%)
  local copies, waits for them, and re-layouts  30.1 us (17%)
  starting transfers between devices  18.2 us (10%)
  matrix products  17.8 us (10%)
  blocking collectives  16.2 us (9%)
  between operations  14.3 us (8%)
  other arithmetic  6.93 us (4%)
    all_to_all x1, waiting for transfers between devices, shards(): lax.all_to_all(send_cotan, 'expert', split_axis=0, concat_axis=0, tiled=T...  25.7 us
    all_to_all x1, waiting for transfers between devices, shards(): lax.all_to_all(to_source(frame_grad), 'expert', split_axis=0, concat_axis...  23.3 us
    all_to_all x1, waiting for transfers between devices, shards(): lax.all_to_all(send_frames, 'expert', split_axis=0, concat_axis=0, tiled=...  18.6 us
    psum x1, blocking collectives, shards(): lax.psum(jnp.stack(tap_grads, axis=1).astype(jnp.bfloat16), 'dp')  16.2 us
    unnamed x30, local copies, waits for them, and re-layouts  15.9 us
    all_to_all x1, waiting for transfers between devices, shards(): lax.all_to_all(to_source(expert_out), 'expert', split_axis=0, concat_axis...  8.08 us
    all_to_all x1, starting transfers between devices, shards(): lax.all_to_all(send_frames, 'expert', split_axis=0, concat_axis=0, tiled=...  6.33 us
    all_to_all x1, starting transfers between devices, shards(): lax.all_to_all(send_cotan, 'expert', split_axis=0, concat_axis=0, tiled=T...  4.24 us
  transfers between devices with their start and end apart: 6, of which 4 were waited for; matrix products, arithmetic and copies ran while one was open for 18% of the time, Pallas kernels for 0%

commit v1 on v0

v1 whole, which is shorter than its diff:
```python
import functools

import jax
import jax.numpy as jnp
from jax import lax
from jax.experimental import pallas as pl
from jax.experimental.pallas import tpu as pltpu
from jax.sharding import PartitionSpec as P

KERNEL_TAPS = 5
DILATION_STEP = 2
CAP = 4
CHUNK = 2
ROWS = 2 * CHUNK * CAP
PAD = 8
OFFSETS = tuple(DILATION_STEP * (j - KERNEL_TAPS // 2) for j in range(KERNEL_TAPS))
F32 = jnp.float32
BF16 = jnp.bfloat16


def params():
    return pltpu.CompilerParams(vmem_limit_bytes=56 * 1024 * 1024)


def dot(a, b, dims=((1,), (0,))):
    return lax.dot_general(a, b, (dims, ((), ())), preferred_element_type=F32)


def column(row):
    size = row.shape[1]
    diagonal = lax.broadcasted_iota(jnp.int32, (size, size), 0) == lax.broadcasted_iota(
        jnp.int32, (size, size), 1
    )
    return jnp.sum(jnp.where(diagonal, row, jnp.zeros_like(row)), axis=1, keepdims=True)


def dispatch_kernel(devs, chunks, chunk, me_ref, routes_ref, weights_ref, tokens_ref, grads_ref, *refs):
    table_ref, pieces, select_ref = refs[0], refs[1:-1], refs[-1]
    toks, width = tokens_ref.shape
    slots = devs * ROWS
    experts = devs * chunks * CHUNK

    @pl.when(pl.program_id(0) == 0)
    def _():
        me = me_ref[0]
        first = column(routes_ref[0:1, :])
        second = column(routes_ref[1:2, :])
        lane_expert = lax.broadcasted_iota(jnp.int32, (toks, experts), 1)
        hit_first = (first == lane_expert).astype(F32)
        hit_second = (second == lane_expert).astype(F32)
        earlier = (
            lax.broadcasted_iota(jnp.int32, (toks, toks), 1)
            < lax.broadcasted_iota(jnp.int32, (toks, toks), 0)
        ).astype(BF16)
        counts = dot(earlier, (hit_first + hit_second).astype(BF16))
        rank_first = jnp.sum(counts * hit_first, axis=1, keepdims=True).astype(jnp.int32)
        rank_second = jnp.sum(counts * hit_second, axis=1, keepdims=True).astype(jnp.int32)
        slot_first = first * CAP + rank_first
        slot_second = second * CAP + rank_second
        lane = lax.broadcasted_iota(jnp.int32, (1, slots), 1)
        piece = lane // ROWS
        within = lane % ROWS
        far = devs // 2
        relative = jnp.where(piece < far, 2 * piece, 2 * (piece - far) + 1)
        is_frame = within // (CHUNK * CAP) == 0
        wanted = ((me ^ relative) * chunks + chunk) * (CHUNK * CAP) + within % (CHUNK * CAP)
        one = lambda mask: jnp.where(mask, 1.0, 0.0).astype(BF16)
        frame_wanted = jnp.where(is_frame, wanted, -1)
        cotan_wanted = jnp.where(is_frame, -1, wanted)
        frame_first = one(slot_first == frame_wanted)
        frame_second = one(slot_second == frame_wanted)
        cotan_first = one(slot_first == cotan_wanted)
        cotan_second = one(slot_second == cotan_wanted)
        table_ref[0:toks] = frame_first
        table_ref[toks : 2 * toks] = frame_second
        table_ref[2 * toks : 3 * toks] = cotan_first + cotan_second
        select_ref[0:toks] = frame_first + frame_second
        select_ref[toks : 2 * toks] = cotan_first
        select_ref[2 * toks : 3 * toks] = cotan_second

    weight_first = column(weights_ref[0:1, :])
    weight_second = column(weights_ref[1:2, :])
    step = min(512, width)
    for begin in range(0, width, step):
        lanes = slice(begin, begin + step)
        grads = grads_ref[:, lanes].astype(F32)
        stacked = jnp.concatenate(
            [
                tokens_ref[:, lanes],
                (weight_first * grads).astype(BF16),
                (weight_second * grads).astype(BF16),
            ],
            axis=0,
        )
        placed = dot(select_ref[...], stacked, ((0,), (0,)))
        begin_row = 0
        for ref in pieces:
            rows = ref.shape[0]
            ref[:, lanes] = placed[begin_row : begin_row + rows].astype(BF16)
            begin_row += rows


def sorting(devs, side):
    total = devs * ROWS
    block = devs * CAP
    row = lax.broadcasted_iota(jnp.int32, (total, total), side)
    expert = row // (2 * block)
    tensor = (row // block) % 2
    device = (row // CAP) % devs
    source = device * ROWS + (tensor * CHUNK + expert) * CAP + row % CAP
    other = lax.broadcasted_iota(jnp.int32, (total, total), 1 - side)
    return jnp.where(source == other, 1.0, 0.0).astype(BF16)


def bits_of(size, expert):
    bits = [1 << k for k in range(size.bit_length() - 1)]
    return bits if expert % 2 == 0 else bits[::-1]


def halving(size, expert):
    rounds, held = [], list(range(size))
    for bit in bits_of(size, expert):
        rounds.append(([r for r in held if r & bit], [r for r in held if not r & bit]))
        held = rounds[-1][1]
    return rounds


def chunk_kernel(devs, held, chunk, *refs):
    me_ref, filter_ref = refs[0], refs[1]
    refs = refs[2:]
    far = devs // 2
    (own_ref, swapped_ref, *far_refs), refs = refs[: far + 1], refs[far + 1 :]
    weight_refs, refs = refs[: len(held)], refs[len(held) :]
    backs, refs = refs[:far], refs[far:]
    reduce_refs, refs = refs[: 2 * CHUNK], refs[2 * CHUNK :]
    matrix, rows_f32, hidden, preact, dpre, dhidden, grad, results = refs
    shards_n = sum(map(len, held)) // CHUNK
    width = own_ref.shape[1]
    channels = matrix.shape[1]
    bins = width // channels
    block = devs * CAP
    total = devs * ROWS
    local = channels // shards_n
    for ref, blocks in zip(weight_refs, held):
        for index, (expert, place, relative) in enumerate(blocks):
            begin = pl.multiple_of((me_ref[0] ^ place if relative else place) * local, local)
            matrix[expert, pl.ds(begin, local), :] = ref[index * local : (index + 1) * local]

    sort = sorting(devs, 0)
    for p in range(bins):
        lanes = slice(p * channels, (p + 1) * channels)
        stacked = [ref[:, lanes] for ref in (own_ref, swapped_ref, *far_refs)]
        rows_f32[:, lanes] = dot(sort, jnp.concatenate(stacked, axis=0))

    for expert in range(CHUNK):
        frames = slice(expert * 2 * block, expert * 2 * block + block)
        cotans = slice(expert * 2 * block + block, (expert + 1) * 2 * block)
        taps = [filter_ref[chunk * CHUNK + expert, j : j + 1, :] for j in range(KERNEL_TAPS)]
        bin_lanes = lambda p: slice(p * channels, (p + 1) * channels)
        bin_rows = lambda p: slice(p * block, (p + 1) * block)
        for p in range(bins):
            acc = None
            for j, off in enumerate(OFFSETS):
                if 0 <= p + off < bins:
                    term = taps[j] * rows_f32[frames, bin_lanes(p + off)]
                    acc = term if acc is None else acc + term
            hidden[bin_rows(p), :] = acc.astype(BF16)
        preact[...] = dot(hidden[...], matrix[expert])
        for p in range(bins):
            value = preact[bin_rows(p), 0:channels]
            sig = 1.0 / (1.0 + jnp.exp(-preact[bin_rows(p), channels : 2 * channels]))
            cotan = rows_f32[cotans, bin_lanes(p)]
            results[frames, bin_lanes(p)] = (value * sig).astype(BF16)
            dpre[bin_rows(p), 0:channels] = (cotan * sig).astype(BF16)
            dpre[bin_rows(p), channels : 2 * channels] = (
                cotan * value * sig * (1.0 - sig)
            ).astype(BF16)
        dhidden[...] = dot(dpre[...], matrix[expert], ((1,), (1,)))
        grad[...] = dot(hidden[...], dpre[...], ((0,), (0,))).astype(BF16)
        rounds = halving(shards_n, expert)[0]
        for ref, relatives in zip(reduce_refs[2 * expert : 2 * expert + 2], rounds):
            for index, relative in enumerate(relatives):
                begin = pl.multiple_of((me_ref[0] ^ relative) * local, local)
                row = index * (local + PAD)
                ref[row : row + local, :] = grad[pl.ds(begin, local), :]
        for q in range(bins):
            acc = None
            for j, off in enumerate(OFFSETS):
                if 0 <= q - off < bins:
                    term = taps[j] * dhidden[bin_rows(q - off), :]
                    acc = term if acc is None else acc + term
            results[cotans, bin_lanes(q)] = acc.astype(BF16)
        lines = []
        for j, off in enumerate(OFFSETS):
            acc = None
            for p in range(bins):
                if 0 <= p + off < bins:
                    term = dhidden[bin_rows(p), :] * rows_f32[frames, bin_lanes(p + off)]
                    acc = term if acc is None else acc + term
            lines.append(jnp.sum(acc, axis=0, keepdims=True))
        tail = jnp.concatenate(lines + [jnp.zeros((PAD - KERNEL_TAPS, channels), F32)], axis=0)
        tail = jnp.concatenate([tail, jnp.zeros_like(tail)], axis=1).astype(BF16)
        for ref in reduce_refs[2 * expert : 2 * expert + 2]:
            for row in range(local, ref.shape[0], local + PAD):
                ref[row : row + PAD, :] = tail
    unsort = sorting(devs, 1)
    for p in range(bins):
        lanes = slice(p * channels, (p + 1) * channels)
        placed = dot(unsort, results[:, lanes])
        for r, ref in enumerate(backs):
            ref[:, lanes] = placed[2 * r * ROWS : 2 * (r + 1) * ROWS].astype(BF16)


def combine_kernel(chunks, weights_ref, *refs):
    tables, pieces, (mixed_ref, grads_ref) = refs[:chunks], refs[chunks:-2], refs[-2:]
    each = len(pieces) // chunks
    toks, width = mixed_ref.shape
    weight_first = column(weights_ref[0:1, :])
    weight_second = column(weights_ref[1:2, :])
    step = min(512, width)
    for begin in range(0, width, step):
        lanes = slice(begin, begin + step)
        placed = None
        for index, table_ref in enumerate(tables):
            stacked = [ref[:, lanes] for ref in pieces[index * each : (index + 1) * each]]
            part = dot(table_ref[...], jnp.concatenate(stacked, axis=0))
            placed = part if placed is None else placed + part
        mixed_ref[:, lanes] = (
            weight_first * placed[0:toks] + weight_second * placed[toks : 2 * toks]
        ).astype(BF16)
        grads_ref[:, lanes] = placed[2 * toks : 3 * toks].astype(BF16)


VMEM = pl.BlockSpec(memory_space=pltpu.VMEM)
SMEM = pl.BlockSpec(memory_space=pltpu.SMEM)
COSTS = (2, 3, 2)
LATE = False
PLANE = 4
WINDOW = 3


def cost(work):
    return pl.CostEstimate(flops=work * 10**9, transcendentals=0, bytes_accessed=8 * 1024 * 1024)


def flip(value, axis, bits):
    return lax.ppermute(value, axis, [(k, k ^ bits) for k in range(lax.axis_size(axis))])


def after(value, *others):
    return lax.optimization_barrier((value, *others))[0]


def shards(tokens, grads_out, routes, route_weights, depth_filter, point_weight):
    toks, width = tokens.shape
    devs = lax.axis_size("expert")
    shards_n = lax.axis_size("dp")
    exp_local = depth_filter.shape[0]
    chunks = exp_local // CHUNK
    local, _, out_channels = point_weight.shape
    channels = local * shards_n
    bins = width // channels
    block = devs * CAP
    total = devs * ROWS
    far = devs // 2
    order = sorted(range(1, far), reverse=True)
    me = lax.axis_index("expert").astype(jnp.int32).reshape(1)
    me_dp = lax.axis_index("dp").astype(jnp.int32).reshape(1)
    routes = routes.T
    route_weights = route_weights.T

    whole = lambda *shape: pl.BlockSpec(shape, lambda i: (0,) * len(shape))
    piece = jax.ShapeDtypeStruct((ROWS, width), BF16)
    tables, sent = [], []
    for chunk in range(chunks):
        table, *pieces = pl.pallas_call(
            functools.partial(dispatch_kernel, devs, chunks, chunk),
            grid=(1,),
            out_shape=[jax.ShapeDtypeStruct((3 * toks, total), BF16)]
            + [piece] * far
            + [jax.ShapeDtypeStruct((far * ROWS, width), BF16)],
            in_specs=[SMEM, whole(2, toks), whole(2, toks), whole(toks, width), whole(toks, width)],
            out_specs=[whole(3 * toks, total)]
            + [whole(ROWS, width)] * far
            + [whole(far * ROWS, width)],
            scratch_shapes=[pltpu.VMEM((3 * toks, total), BF16)],
            compiler_params=params(),
            cost_estimate=cost(COSTS[0]),
            name="dispatch",
        )(me, routes, route_weights, tokens, grads_out)
        tables.append(table)
        sent.append(pieces)

    line = []

    def along_line(pieces):
        moved = {0: pieces[0]}
        for r in order:
            value = pieces[r]
            if len(line) >= WINDOW:
                value = after(value, line[-WINDOW])
            line.append(flip(value, "expert", 2 * r))
            moved[r] = line[-1]
        return [moved[r] for r in range(far)]

    plane = []

    def in_plane(value, bit):
        if len(plane) >= PLANE:
            value = after(value, plane[-PLANE])
        plane.append(flip(value, "dp", bit))
        return plane[-1]

    def gather(parts):
        held = [(part, [0]) for part in parts]
        for turn in range(shards_n.bit_length() - 1):
            bits = [bits_of(shards_n, expert)[turn] for expert in range(CHUNK)]
            came = [in_plane(value, bit) for (value, _), bit in zip(held, bits)]
            new = [
                (other, [place ^ bit for place in places])
                for (_, places), other, bit in zip(held, came, bits)
            ]
            if 2 * len(held[0][1]) == shards_n:
                return [
                    (value, [(expert, place, True) for place in places])
                    for expert in range(CHUNK)
                    for value, places in (held[expert], new[expert])
                ]
            held = [
                (jnp.concatenate([old, other], axis=0), places + more)
                for (old, places), (other, more) in zip(held, new)
            ]

    def scatter(pairs):
        rounds = [halving(shards_n, expert) for expert in range(CHUNK)]
        size = local + PAD
        for turn in range(len(rounds[0])):
            came = [
                in_plane(send, bits_of(shards_n, expert)[turn])
                for expert, (send, _) in enumerate(pairs)
            ]
            if turn + 1 == len(rounds[0]):
                return [
                    keep.astype(F32) + other.astype(F32)
                    for (_, keep), other in zip(pairs, came)
                ]
            new = []
            for expert, ((_, keep), other) in enumerate(zip(pairs, came)):
                places = rounds[expert][turn][1]
                total = lambda r: (
                    keep[places.index(r) * size : (places.index(r) + 1) * size].astype(F32)
                    + other[places.index(r) * size : (places.index(r) + 1) * size].astype(F32)
                ).astype(BF16)
                new.append(
                    [
                        jnp.concatenate([total(r) for r in relatives], axis=0)
                        for relatives in rounds[expert][turn + 1]
                    ]
                )
            pairs = new

    weights = jnp.transpose(after(point_weight, tables[0]), (1, 0, 2))
    arrived = []
    for *own, relayed in sent:
        relayed = flip(relayed, "expert", 1)
        pairs = [
            jnp.concatenate([own[r], relayed[r * ROWS : (r + 1) * ROWS]], axis=0)
            for r in range(1, far)
        ]
        arrived.append([own[0], relayed] + along_line([own[0]] + pairs)[1:])
    gathered = [
        gather(
            [
                after(weights[chunk * CHUNK + expert], arrived[chunk][1])
                for expert in range(CHUNK)
            ]
        )
        for chunk in range(chunks)
    ]
    half = jax.ShapeDtypeStruct((shards_n // 2 * (local + PAD), out_channels), BF16)
    backs = []
    reduced = []
    for chunk in range(chunks):
        full, held = zip(*gathered[chunk])
        pair = jax.ShapeDtypeStruct((2 * ROWS, width), BF16)
        outs = [pair] * far + [half] * (2 * CHUNK)
        outs = pl.pallas_call(
            functools.partial(chunk_kernel, devs, held, chunk),
            out_shape=outs,
            grid=(1,),
            in_specs=[SMEM, whole(*depth_filter.shape)]
            + [whole(ROWS, width)] * 2
            + [whole(*value.shape) for value in (*arrived[chunk][2:], *full)],
            out_specs=[whole(*value.shape) for value in outs],
            scratch_shapes=[
                pltpu.VMEM((CHUNK, channels, out_channels), BF16),
                pltpu.VMEM((total, width), F32),
                pltpu.VMEM((bins * block, channels), BF16),
                pltpu.VMEM((bins * block, out_channels), F32),
                pltpu.VMEM((bins * block, out_channels), BF16),
                pltpu.VMEM((bins * block, channels), F32),
                pltpu.VMEM((channels, out_channels), BF16),
                pltpu.VMEM((total, width), BF16),
            ],
            compiler_params=params(),
            cost_estimate=cost(COSTS[1]),
            name="experts",
        )(me_dp, depth_filter, *arrived[chunk], *full)
        results, to_reduce = list(outs[:far]), outs[far:]
        reduced += scatter(list(zip(to_reduce[::2], to_reduce[1::2])))
        if LATE and chunk + 1 == chunks:
            results[1] = after(results[1], *reduced)
        near = along_line(results)
        swapped = flip(jnp.concatenate([value[ROWS:] for value in near], axis=0), "expert", 1)
        backs += near + [swapped]

    mixed, token_grads = pl.pallas_call(
        functools.partial(combine_kernel, chunks),
        grid=(1,),
        out_shape=[jax.ShapeDtypeStruct((toks, width), BF16)] * 2,
        in_specs=[whole(2, toks)]
        + [whole(3 * toks, total)] * chunks
        + ([whole(ROWS, width)] * far + [whole(far * ROWS, width)]) * chunks,
        out_specs=[whole(toks, width)] * 2,
        compiler_params=params(),
        cost_estimate=cost(COSTS[2]),
        name="combine",
    )(route_weights, *tables, *backs)
    point_grads = jnp.stack([value[:local] for value in reduced], axis=1)
    depth_grads = jnp.stack(
        [value[local : local + KERNEL_TAPS, :channels] for value in reduced], axis=0
    )
    return (mixed, token_grads, point_grads, depth_grads)


def solution(mesh):
    placed = (
        P(("dp", "expert"), None),
        P(("dp", "expert"), None),
        P(("dp", "expert"), None),
        P(("dp", "expert"), None),
        P("expert", None, None),
        P("dp", "expert", None),
    )
    return jax.shard_map(
        shards,
        mesh=mesh,
        in_specs=placed,
        out_specs=(
            P(("dp", "expert"), None),
            P(("dp", "expert"), None),
            P("dp", "expert", None),
            P("expert", None, None),
        ),
        check_vma=False,
    )
```

time: 180 us -> 148 us (0.82)
  starting transfers between devices: 18.2 us -> 43.1 us
  Pallas kernels: 0 us -> 23 us
  local copies, waits for them, and re-layouts: 30.1 us -> 9.82 us
  matrix products: 17.8 us -> 0 us
  blocking collectives: 16.2 us -> 0 us
  between operations: 14.3 us -> 1.41 us
  waiting for transfers between devices: 75.8 us -> 69.4 us
  other arithmetic: 6.93 us -> 1.17 us
    all_to_all x4 -> x0, waiting for transfers between devices: 75.7 us -> none  [the longest x1 25.7 us: shards(): lax.all_to_all(send_cotan, 'expert', split_axis=0, concat_axis=0, tiled=T...]
    ppermute x0 -> x32, waiting for transfers between devices: none -> 69.4 us  [flip(): lax.ppermute(value, axis, [(k, k ^ bits) for k in range(lax.axis_size(axi...]
    ppermute x0 -> x32, starting transfers between devices: none -> 43.1 us  [flip(): lax.ppermute(value, axis, [(k, k ^ bits) for k in range(lax.axis_size(axi...]
    pallas_call x0 -> x5, Pallas kernels: none -> 23 us  [the longest x2 13.5 us: shards(): pl.pallas_call(functools.partial(chunk_kernel, devs, held, chunk), out_sh...]
    all_to_all x4 -> x0, starting transfers between devices: 17.9 us -> none  [the longest x1 6.33 us: shards(): lax.all_to_all(send_frames, 'expert', split_axis=0, concat_axis=0, tiled=...]
    dot_general x7 -> x0, matrix products: 17.8 us -> none  [the longest x1 3.8 us: shards(): jnp.einsum('erpo,ceo->erpc', dpre, full_filter, preferred_element_type=jn...]
    psum x1 -> x0, blocking collectives: 16.2 us -> none  [shards(): lax.psum(jnp.stack(tap_grads, axis=1).astype(jnp.bfloat16), 'dp')]
    unnamed x30 -> x83, local copies, waits for them, and re-layouts: 15.9 us -> 7.27 us
  transfers between devices with their start and end apart: 6 -> 32, of which waited for: 4 -> 10; matrix products, arithmetic and copies ran while one was open for 18% -> 3% of each run, Pallas kernels for 0% -> 14%
where the time goes in v1:
time: 148 us
  waiting for transfers between devices  69.4 us (47%)
  starting transfers between devices  43.1 us (29%)
  Pallas kernels  23 us (16%)
  local copies, waits for them, and re-layouts  9.82 us (7%)
    ppermute x32, waiting for transfers between devices, flip(): lax.ppermute(value, axis, [(k, k ^ bits) for k in range(lax.axis_size(axi...  69.4 us
    ppermute x32, starting transfers between devices, flip(): lax.ppermute(value, axis, [(k, k ^ bits) for k in range(lax.axis_size(axi...  43.1 us
    pallas_call x2, Pallas kernels, shards(): pl.pallas_call(functools.partial(chunk_kernel, devs, held, chunk), out_sh...  13.5 us
    unnamed x83, local copies, waits for them, and re-layouts  7.27 us
    pallas_call x2, Pallas kernels, shards(): pl.pallas_call(functools.partial(dispatch_kernel, devs, chunks, chunk), g...  5.96 us
    pallas_call x1, Pallas kernels, shards(): pl.pallas_call(functools.partial(combine_kernel, chunks), grid=(1,), out_...  3.54 us
  transfers between devices with their start and end apart: 32, of which 10 were waited for; matrix products, arithmetic and copies ran while one was open for 3% of the time, Pallas kernels for 14%

profile of v1, /device:TPU:0, one launch (start us, length us, event | category | flops | bytes accessed | tf_op | source)
XLA Modules:
  0.0 147.9 jit_solution(2011167395634147418)
XLA Ops:
  0.6 3.0 %dispatch.2 = (bf16[192,128]{1,0:T(8,128)(2,1)}, bf16[16,4096]{1,0:T(8,128)(2,1)}, bf16[16,4096]{1,0:T(8,128)(2,1)}, bf16[16,4096]{1,0:T(8,128)(2,1)}, bf16[16,4...) custom-call(s32[1]{0:T(128)} %bitcast.1.me_ref, s32[2,64]{1,0:T(2,128)} %bitcast.32, f32[2,64]{1,0:T(2,128)} %bitcast.34, ...), custom_call_target="tpu_custom_call" | custom-call | flops 2000000000 | bytes 8388608 | tf_op jit(solution)/shard_map/dispatch/pallas_call | solution.py:276
  4.1 3.0 %dispatch.3 = (bf16[192,128]{1,0:T(8,128)(2,1)}, bf16[16,4096]{1,0:T(8,128)(2,1)}, bf16[16,4096]{1,0:T(8,128)(2,1)}, bf16[16,4096]{1,0:T(8,128)(2,1)}, bf16[16,4...) custom-call(s32[1]{0:T(128)} %bitcast.1.me_ref, s32[2,64]{1,0:T(2,128)} %bitcast.33, f32[2,64]{1,0:T(2,128)} %bitcast.35, ...), custom_call_target="tpu_custom_call" | custom-call | flops 2000000000 | bytes 8388608 | tf_op jit(solution)/shard_map/dispatch/pallas_call | solution.py:276
  8.6 2.7 %collective-permute-start.6 = (bf16[128,1024]{1,0:T(8,128)(2,1)S(1)}, bf16[128,1024]{1,0:T(8,128)(2,1)S(1)}, u32[]{:S(2)}, u32[]{:S(2)}) collective-permute-start(bf16[128,1024]{1,0:T(8,128)(2,1)S(1)} %get-tuple-element.69), channel_id=1, source_target_pairs={{0,16},{8,24},{16,0},{24,8},{1,17},{9,25},{17,1},{25,9},{2,18},{10... | collective-permute-start | bytes 786440 | tf_op jit(solution)/shard_map/ppermute | solution.py:247
  11.3 1.5 %collective-permute-start.4 = (bf16[128,1024]{1,0:T(8,128)(2,1)S(1)}, bf16[128,1024]{1,0:T(8,128)(2,1)S(1)}, u32[]{:S(2)}, u32[]{:S(2)}) collective-permute-start(bf16[128,1024]{1,0:T(8,128)(2,1)S(1)} %get-tuple-element.68), channel_id=1, source_target_pairs={{0,8},{8,0},{16,24},{24,16},{1,9},{9,1},{17,25},{25,17},{2,10},{10... | collective-permute-start | bytes 786440 | tf_op jit(solution)/shard_map/ppermute | solution.py:247
  12.8 1.6 %collective-permute-start.1 = (bf16[32,4096]{1,0:T(8,128)(2,1)S(1)}, bf16[32,4096]{1,0:T(8,128)(2,1)S(1)}, u32[]{:S(2)}, u32[]{:S(2)}) collective-permute-start(bf16[32,4096]{1,0:T(8,128)(2,1)S(1)} %pad_maximum_fusion.3), channel_id=1, source_target_pairs={{0,2},{1,3},{2,0},{3,1},{4,6},{5,7},{6,4},{7,5},{8,10},{9,11},{10,... | collective-permute-start | bytes 786440 | tf_op jit(solution)/shard_map/ppermute | solution.py:247
  14.5 2.7 %collective-permute-start.2 = (bf16[32,4096]{1,0:T(8,128)(2,1)S(1)}, bf16[32,4096]{1,0:T(8,128)(2,1)S(1)}, u32[]{:S(2)}, u32[]{:S(2)}) collective-permute-start(bf16[32,4096]{1,0:T(8,128)(2,1)S(1)} %pad_maximum_fusion.4), channel_id=1, source_target_pairs={{0,4},{1,5},{2,6},{3,7},{4,0},{5,1},{6,2},{7,3},{8,12},{9,13},{10,... | collective-permute-start | bytes 786440 | tf_op jit(solution)/shard_map/ppermute | solution.py:247
  18.2 1.8 %collective-permute-start.7 = (bf16[256,1024]{1,0:T(8,128)(2,1)S(1)}, bf16[256,1024]{1,0:T(8,128)(2,1)S(1)}, u32[]{:S(2)}, u32[]{:S(2)}) collective-permute-start(bf16[256,1024]{1,0:T(8,128)(2,1)S(1)} %constant_dynamic-update-slice_fusion.2.refs_9_), channel_id=1, source_target_pairs={{0,8},{8,0},{16,24},{24,16},{1,9},{9,1},{17,25},{25,17},{2,10},{10... | collective-permute-start | bytes 1572872 | tf_op jit(solution)/shard_map/ppermute | solution.py:247
  20.0 1.6 %collective-permute-start.5 = (bf16[256,1024]{1,0:T(8,128)(2,1)S(1)}, bf16[256,1024]{1,0:T(8,128)(2,1)S(1)}, u32[]{:S(2)}, u32[]{:S(2)}) collective-permute-start(bf16[256,1024]{1,0:T(8,128)(2,1)S(1)} %constant_dynamic-update-slice_fusion.refs_7_), channel_id=1, source_target_pairs={{0,16},{8,24},{16,0},{24,8},{1,17},{9,25},{17,1},{25,9},{2,18},{10... | collective-permute-start | bytes 1572872 | tf_op jit(solution)/shard_map/ppermute | solution.py:247
  21.7 14.2 %collective-permute-done.2.refs_5_ = bf16[32,4096]{1,0:T(8,128)(2,1)S(1)} collective-permute-done((bf16[32,4096]{1,0:T(8,128)(2,1)S(1)}, bf16[32,4096]{1,0:T(8,128)(2,1)S(1)}, u32[]{:S(2)}, u32[]{:S(2)}) %collective-permute-start.2) | collective-permute-done | bytes 262176 | tf_op jit(solution)/shard_map/ppermute | solution.py:247
  37.2 5.3 %collective-permute-start.11 = (bf16[32,4096]{1,0:T(8,128)(2,1)S(1)}, bf16[32,4096]{1,0:T(8,128)(2,1)S(1)}, u32[]{:S(2)}, u32[]{:S(2)}) collective-permute-start(bf16[32,4096]{1,0:T(8,128)(2,1)S(1)} %pad_maximum_fusion.7), channel_id=1, source_target_pairs={{0,4},{1,5},{2,6},{3,7},{4,0},{5,1},{6,2},{7,3},{8,12},{9,13},{10,... | collective-permute-start | bytes 786440 | tf_op jit(solution)/shard_map/ppermute | solution.py:247
  42.4 1.3 collective-permute-start.13
  44.6 6.6 %experts.2 = (bf16[32,4096]{1,0:T(8,128)(2,1)}, bf16[32,4096]{1,0:T(8,128)(2,1)}, bf16[32,4096]{1,0:T(8,128)(2,1)}, bf16[32,4096]{1,0:T(8,128)(2,1)}, bf16[272,1...) custom-call(s32[1]{0:T(128)} %bitcast.3.refs_0_, ...), custom_call_target="tpu_custom_call" | custom-call | flops 3000000000 | bytes 8388608 | tf_op jit(solution)/shard_map/experts/pallas_call | solution.py:387
  51.2 5.4 %collective-permute-done.13.refs_6_ = bf16[32,4096]{1,0:T(8,128)(2,1)S(1)} collective-permute-done((bf16[32,4096]{1,0:T(8,128)(2,1)S(1)}, bf16[32,4096]{1,0:T(8,128)(2,1)S(1)}, u32[]{:S(2)}, u32[]{:S(2)}) %collective-permute-start.13) | collective-permute-done | bytes 262176 | tf_op jit(solution)/shard_map/ppermute | solution.py:247
  56.7 2.4 %collective-permute-start.14 = (bf16[32,4096]{1,0:T(8,128)(2,1)}, bf16[32,4096]{1,0:T(8,128)(2,1)S(1)}, u32[]{:S(2)}, u32[]{:S(2)}) collective-permute-start(bf16[32,4096]{1,0:T(8,128)(2,1)} %get-tuple-element.83), channel_id=1, source_target_pairs={{0,6},{1,7},{2,4},{3,5},{4,2},{5,3},{6,0},{7,1},{8,14},{9,15},{10,... | collective-permute-start | bytes 786440 | tf_op jit(solution)/shard_map/ppermute | solution.py:247
  59.1 6.7 %collective-permute-done.11.refs_5_ = bf16[32,4096]{1,0:T(8,128)(2,1)S(1)} collective-permute-done((bf16[32,4096]{1,0:T(8,128)(2,1)S(1)}, bf16[32,4096]{1,0:T(8,128)(2,1)S(1)}, u32[]{:S(2)}, u32[]{:S(2)}) %collective-permute-start.11) | collective-permute-done | bytes 262176 | tf_op jit(solution)/shard_map/ppermute | solution.py:247
  65.8 6.4 %collective-permute-start.12 = (bf16[32,4096]{1,0:T(8,128)(2,1)}, bf16[32,4096]{1,0:T(8,128)(2,1)S(1)}, u32[]{:S(2)}, u32[]{:S(2)}) collective-permute-start(bf16[32,4096]{1,0:T(8,128)(2,1)} %get-tuple-element.79), channel_id=1, source_target_pairs={{0,4},{1,5},{2,6},{3,7},{4,0},{5,1},{6,2},{7,3},{8,12},{9,13},{10,... | collective-permute-start | bytes 786440 | tf_op jit(solution)/shard_map/ppermute | solution.py:247
  72.3 1.2 collective-permute-start.17
  74.9 1.6 %collective-permute-start.24 = (bf16[272,1024]{1,0:T(8,128)(2,1)}, bf16[272,1024]{1,0:T(8,128)(2,1)S(1)}, u32[]{:S(2)}, u32[]{:S(2)}) collective-permute-start(bf16[272,1024]{1,0:T(8,128)(2,1)} %get-tuple-element.102), channel_id=1, source_target_pairs={{0,8},{8,0},{16,24},{24,16},{1,9},{9,1},{17,25},{25,17},{2,10},{10... | collective-permute-start | bytes 1671176 | tf_op jit(solution)/shard_map/ppermute | solution.py:247
  76.5 12.2 %collective-permute-done.12.refs_4_ = bf16[32,4096]{1,0:T(8,128)(2,1)S(1)} collective-permute-done((bf16[32,4096]{1,0:T(8,128)(2,1)}, bf16[32,4096]{1,0:T(8,128)(2,1)S(1)}, u32[]{:S(2)}, u32[]{:S(2)}) %collective-permute-start.12) | collective-permute-done | bytes 262176 | tf_op jit(solution)/shard_map/ppermute | solution.py:247
  88.7 1.1 collective-permute-start.26
  91.0 6.9 %experts.3 = (bf16[32,4096]{1,0:T(8,128)(2,1)}, bf16[32,4096]{1,0:T(8,128)(2,1)}, bf16[32,4096]{1,0:T(8,128)(2,1)}, bf16[32,4096]{1,0:T(8,128)(2,1)}, bf16[272,1...) custom-call(s32[1]{0:T(128)} %bitcast.3.refs_0_, ...), custom_call_target="tpu_custom_call" | custom-call | flops 3000000000 | bytes 8388608 | tf_op jit(solution)/shard_map/experts/pallas_call | solution.py:387
  97.9 1.2 collective-permute-start.22
  100.0 3.3 %collective-permute-start.20 = (bf16[32,4096]{1,0:T(8,128)(2,1)}, bf16[32,4096]{1,0:T(8,128)(2,1)S(1)}, u32[]{:S(2)}, u32[]{:S(2)}) collective-permute-start(bf16[32,4096]{1,0:T(8,128)(2,1)} %get-tuple-element.93), channel_id=1, source_target_pairs={{0,2},{1,3},{2,0},{3,1},{4,6},{5,7},{6,4},{7,5},{8,10},{9,11},{10,... | collective-permute-start | bytes 786440 | tf_op jit(solution)/shard_map/ppermute | solution.py:247
  103.4 1.0 collective-permute-start.25
  104.5 4.7 %collective-permute-done.22.refs_10_ = bf16[32,4096]{1,0:T(8,128)(2,1)S(1)} collective-permute-done((bf16[32,4096]{1,0:T(8,128)(2,1)}, bf16[32,4096]{1,0:T(8,128)(2,1)S(1)}, u32[]{:S(2)}, u32[]{:S(2)}) %collective-permute-start.22) | collective-permute-done | bytes 262176 | tf_op jit(solution)/shard_map/ppermute | solution.py:247
  109.7 11.9 %collective-permute-done.21.refs_9_ = bf16[32,4096]{1,0:T(8,128)(2,1)S(1)} collective-permute-done((bf16[32,4096]{1,0:T(8,128)(2,1)}, bf16[32,4096]{1,0:T(8,128)(2,1)S(1)}, u32[]{:S(2)}, u32[]{:S(2)}) %collective-permute-start.21) | collective-permute-done | bytes 262176 | tf_op jit(solution)/shard_map/ppermute | solution.py:247
  122.2 1.0 collective-permute-start.30
  123.7 12.1 %collective-permute-done.28 = bf16[272,1024]{1,0:T(8,128)(2,1)S(1)} collective-permute-done((bf16[272,1024]{1,0:T(8,128)(2,1)S(1)}, bf16[272,1024]{1,0:T(8,128)(2,1)S(1)}, u32[]{:S(2)}, u32[]{:S(2)}) %collective-permute-start.28) | collective-permute-done | bytes 557088 | tf_op jit(solution)/shard_map/ppermute | solution.py:247
  135.9 1.0 collective-permute-start.29
  138.8 3.5 %combine.1 = (bf16[64,4096]{1,0:T(8,128)(2,1)}, bf16[64,4096]{1,0:T(8,128)(2,1)}) custom-call(f32[2,64]{1,0:T(2,128)} %bitcast.36, bf16[192,128]{1,0:T(8,128)(2,1)} %get-tuple-element.60.refs_0_, bf16[192,128]{1,0:T(8,128)(2,1)} %get-tuple-element.61.refs_1_, bf16[32,4096]{1,0:T(8,128)(2,1)} %get-tuple-element.70.refs_2_, bf16[32,4096]{1,0:T(8,128)(2,1)} %copy-done.19, ...), custom_call_target="tpu_custom_call" | custom-call | flops 2000000000 | bytes 8388608 | tf_op jit(solution)/shard_map/combine/pallas_call | solution.py:417
  142.4 0.9 collective-permute-done.29
  145.2 2.7 %copy.13 = f32[128,4,1024]{2,1,0:T(4,128)} copy(f32[128,4,1024]{2,0,1:T(8,128)S(1)} %pad_maximum_fusion) | data formatting | bytes 4194304
  (162 shorter events, 14.0 us)
Async XLA Ops:
  3.6 4.9 %collective-permute-start = (bf16[64,4096]{1,0:T(8,128)(2,1)}, bf16[64,4096]{1,0:T(8,128)(2,1)S(1)}, u32[]{:S(2)}, u32[]{:S(2)}) collective-permute-start(bf16[64,4096]{1,0:T(8,128)(2,1)} %get-tuple-element.63), channel_id=1, source_target_pairs={{0,1},{1,0},{2,3},{3,2},{4,5},{5,4},{6,7},{7,6},{8,9},{9,8},{10,11... | collective-permute-start | bytes 1572872 | tf_op jit(solution)/shard_map/ppermute | solution.py:247
  7.1 10.1 %collective-permute-start.8 = (bf16[64,4096]{1,0:T(8,128)(2,1)}, bf16[64,4096]{1,0:T(8,128)(2,1)S(1)}, u32[]{:S(2)}, u32[]{:S(2)}) collective-permute-start(bf16[64,4096]{1,0:T(8,128)(2,1)} %get-tuple-element.73), channel_id=1, source_target_pairs={{0,1},{1,0},{2,3},{3,2},{4,5},{5,4},{6,7},{7,6},{8,9},{9,8},{10,11... | collective-permute-start | bytes 1572872 | tf_op jit(solution)/shard_map/ppermute | solution.py:247
  8.6 9.6 %collective-permute-start.6 = (bf16[128,1024]{1,0:T(8,128)(2,1)S(1)}, bf16[128,1024]{1,0:T(8,128)(2,1)S(1)}, u32[]{:S(2)}, u32[]{:S(2)}) collective-permute-start(bf16[128,1024]{1,0:T(8,128)(2,1)S(1)} %get-tuple-element.69), channel_id=1, source_target_pairs={{0,16},{8,24},{16,0},{24,8},{1,17},{9,25},{17,1},{25,9},{2,18},{10... | collective-permute-start | bytes 786440 | tf_op jit(solution)/shard_map/ppermute | solution.py:247
  11.3 8.7 %collective-permute-start.4 = (bf16[128,1024]{1,0:T(8,128)(2,1)S(1)}, bf16[128,1024]{1,0:T(8,128)(2,1)S(1)}, u32[]{:S(2)}, u32[]{:S(2)}) collective-permute-start(bf16[128,1024]{1,0:T(8,128)(2,1)S(1)} %get-tuple-element.68), channel_id=1, source_target_pairs={{0,8},{8,0},{16,24},{24,16},{1,9},{9,1},{17,25},{25,17},{2,10},{10... | collective-permute-start | bytes 786440 | tf_op jit(solution)/shard_map/ppermute | solution.py:247
  12.8 24.4 %collective-permute-start.1 = (bf16[32,4096]{1,0:T(8,128)(2,1)S(1)}, bf16[32,4096]{1,0:T(8,128)(2,1)S(1)}, u32[]{:S(2)}, u32[]{:S(2)}) collective-permute-start(bf16[32,4096]{1,0:T(8,128)(2,1)S(1)} %pad_maximum_fusion.3), channel_id=1, source_target_pairs={{0,2},{1,3},{2,0},{3,1},{4,6},{5,7},{6,4},{7,5},{8,10},{9,11},{10,... | collective-permute-start | bytes 786440 | tf_op jit(solution)/shard_map/ppermute | solution.py:247
  14.5 21.4 %collective-permute-start.2 = (bf16[32,4096]{1,0:T(8,128)(2,1)S(1)}, bf16[32,4096]{1,0:T(8,128)(2,1)S(1)}, u32[]{:S(2)}, u32[]{:S(2)}) collective-permute-start(bf16[32,4096]{1,0:T(8,128)(2,1)S(1)} %pad_maximum_fusion.4), channel_id=1, source_target_pairs={{0,4},{1,5},{2,6},{3,7},{4,0},{5,1},{6,2},{7,3},{8,12},{9,13},{10,... | collective-permute-start | bytes 786440 | tf_op jit(solution)/shard_map/ppermute | solution.py:247
  17.2 19.3 %collective-permute-start.3 = (bf16[32,4096]{1,0:T(8,128)(2,1)S(1)}, bf16[32,4096]{1,0:T(8,128)(2,1)S(1)}, u32[]{:S(2)}, u32[]{:S(2)}) collective-permute-start(bf16[32,4096]{1,0:T(8,128)(2,1)S(1)} %pad_maximum_fusion.5), channel_id=1, source_target_pairs={{0,6},{1,7},{2,4},{3,5},{4,2},{5,3},{6,0},{7,1},{8,14},{9,15},{10,... | collective-permute-start | bytes 786440 | tf_op jit(solution)/shard_map/ppermute | solution.py:247
  18.2 24.3 %collective-permute-start.7 = (bf16[256,1024]{1,0:T(8,128)(2,1)S(1)}, bf16[256,1024]{1,0:T(8,128)(2,1)S(1)}, u32[]{:S(2)}, u32[]{:S(2)}) collective-permute-start(bf16[256,1024]{1,0:T(8,128)(2,1)S(1)} %constant_dynamic-update-slice_fusion.2.refs_9_), channel_id=1, source_target_pairs={{0,8},{8,0},{16,24},{24,16},{1,9},{9,1},{17,25},{25,17},{2,10},{10... | collective-permute-start | bytes 1572872 | tf_op jit(solution)/shard_map/ppermute | solution.py:247
  20.0 23.8 %collective-permute-start.5 = (bf16[256,1024]{1,0:T(8,128)(2,1)S(1)}, bf16[256,1024]{1,0:T(8,128)(2,1)S(1)}, u32[]{:S(2)}, u32[]{:S(2)}) collective-permute-start(bf16[256,1024]{1,0:T(8,128)(2,1)S(1)} %constant_dynamic-update-slice_fusion.refs_7_), channel_id=1, source_target_pairs={{0,16},{8,24},{16,0},{24,8},{1,17},{9,25},{17,1},{25,9},{2,18},{10... | collective-permute-start | bytes 1572872 | tf_op jit(solution)/shard_map/ppermute | solution.py:247
  35.9 36.3 %collective-permute-start.16 = (bf16[128,1024]{1,0:T(8,128)(2,1)S(1)}, bf16[128,1024]{1,0:T(8,128)(2,1)S(1)}, u32[]{:S(2)}, u32[]{:S(2)}) collective-permute-start(bf16[128,1024]{1,0:T(8,128)(2,1)S(1)} %get-tuple-element.86), channel_id=1, source_target_pairs={{0,8},{8,0},{16,24},{24,16},{1,9},{9,1},{17,25},{25,17},{2,10},{10... | collective-permute-start | bytes 786440 | tf_op jit(solution)/shard_map/ppermute | solution.py:247
  36.5 35.8 %collective-permute-start.18 = (bf16[128,1024]{1,0:T(8,128)(2,1)S(1)}, bf16[128,1024]{1,0:T(8,128)(2,1)S(1)}, u32[]{:S(2)}, u32[]{:S(2)}) collective-permute-start(bf16[128,1024]{1,0:T(8,128)(2,1)S(1)} %get-tuple-element.89), channel_id=1, source_target_pairs={{0,16},{8,24},{16,0},{24,8},{1,17},{9,25},{17,1},{25,9},{2,18},{10... | collective-permute-start | bytes 786440 | tf_op jit(solution)/shard_map/ppermute | solution.py:247
  37.2 28.6 %collective-permute-start.11 = (bf16[32,4096]{1,0:T(8,128)(2,1)S(1)}, bf16[32,4096]{1,0:T(8,128)(2,1)S(1)}, u32[]{:S(2)}, u32[]{:S(2)}) collective-permute-start(bf16[32,4096]{1,0:T(8,128)(2,1)S(1)} %pad_maximum_fusion.7), channel_id=1, source_target_pairs={{0,4},{1,5},{2,6},{3,7},{4,0},{5,1},{6,2},{7,3},{8,12},{9,13},{10,... | collective-permute-start | bytes 786440 | tf_op jit(solution)/shard_map/ppermute | solution.py:247
  42.4 14.2 %collective-permute-start.13 = (bf16[32,4096]{1,0:T(8,128)(2,1)S(1)}, bf16[32,4096]{1,0:T(8,128)(2,1)S(1)}, u32[]{:S(2)}, u32[]{:S(2)}) collective-permute-start(bf16[32,4096]{1,0:T(8,128)(2,1)S(1)} %pad_maximum_fusion.8), channel_id=1, source_target_pairs={{0,6},{1,7},{2,4},{3,5},{4,2},{5,3},{6,0},{7,1},{8,14},{9,15},{10,... | collective-permute-start | bytes 786440 | tf_op jit(solution)/shard_map/ppermute | solution.py:247
  43.8 28.4 %collective-permute-start.9 = (bf16[32,4096]{1,0:T(8,128)(2,1)S(1)}, bf16[32,4096]{1,0:T(8,128)(2,1)S(1)}, u32[]{:S(2)}, u32[]{:S(2)}) collective-permute-start(bf16[32,4096]{1,0:T(8,128)(2,1)S(1)} %pad_maximum_fusion.6), channel_id=1, source_target_pairs={{0,2},{1,3},{2,0},{3,1},{4,6},{5,7},{6,4},{7,5},{8,10},{9,11},{10,... | collective-permute-start | bytes 786440 | tf_op jit(solution)/shard_map/ppermute | solution.py:247
  56.7 18.2 %collective-permute-start.14 = (bf16[32,4096]{1,0:T(8,128)(2,1)}, bf16[32,4096]{1,0:T(8,128)(2,1)S(1)}, u32[]{:S(2)}, u32[]{:S(2)}) collective-permute-start(bf16[32,4096]{1,0:T(8,128)(2,1)} %get-tuple-element.83), channel_id=1, source_target_pairs={{0,6},{1,7},{2,4},{3,5},{4,2},{5,3},{6,0},{7,1},{8,14},{9,15},{10,... | collective-permute-start | bytes 786440 | tf_op jit(solution)/shard_map/ppermute | solution.py:247
  65.8 22.9 %collective-permute-start.12 = (bf16[32,4096]{1,0:T(8,128)(2,1)}, bf16[32,4096]{1,0:T(8,128)(2,1)S(1)}, u32[]{:S(2)}, u32[]{:S(2)}) collective-permute-start(bf16[32,4096]{1,0:T(8,128)(2,1)} %get-tuple-element.79), channel_id=1, source_target_pairs={{0,4},{1,5},{2,6},{3,7},{4,0},{5,1},{6,2},{7,3},{8,12},{9,13},{10,... | collective-permute-start | bytes 786440 | tf_op jit(solution)/shard_map/ppermute | solution.py:247
  72.2 17.6 %collective-permute-start.10 = (bf16[32,4096]{1,0:T(8,128)(2,1)}, bf16[32,4096]{1,0:T(8,128)(2,1)S(1)}, u32[]{:S(2)}, u32[]{:S(2)}) collective-permute-start(bf16[32,4096]{1,0:T(8,128)(2,1)} %get-tuple-element.75), channel_id=1, source_target_pairs={{0,2},{1,3},{2,0},{3,1},{4,6},{5,7},{6,4},{7,5},{8,10},{9,11},{10,... | collective-permute-start | bytes 786440 | tf_op jit(solution)/shard_map/ppermute | solution.py:247
  72.3 17.7 %collective-permute-start.17 = (bf16[256,1024]{1,0:T(8,128)(2,1)S(1)}, bf16[256,1024]{1,0:T(8,128)(2,1)S(1)}, u32[]{:S(2)}, u32[]{:S(2)}) collective-permute-start(bf16[256,1024]{1,0:T(8,128)(2,1)S(1)} %constant_dynamic-update-slice_fusion.4.refs_7_), channel_id=1, source_target_pairs={{0,16},{8,24},{16,0},{24,8},{1,17},{9,25},{17,1},{25,9},{2,18},{10... | collective-permute-start | bytes 1572872 | tf_op jit(solution)/shard_map/ppermute | solution.py:247
  73.5 16.5 %collective-permute-start.19 = (bf16[256,1024]{1,0:T(8,128)(2,1)S(1)}, bf16[256,1024]{1,0:T(8,128)(2,1)S(1)}, u32[]{:S(2)}, u32[]{:S(2)}) collective-permute-start(bf16[256,1024]{1,0:T(8,128)(2,1)S(1)} %constant_dynamic-update-slice_fusion.6.refs_9_), channel_id=1, source_target_pairs={{0,8},{8,0},{16,24},{24,16},{1,9},{9,1},{17,25},{25,17},{2,10},{10... | collective-permute-start | bytes 1572872 | tf_op jit(solution)/shard_map/ppermute | solution.py:247
  74.9 25.1 %collective-permute-start.24 = (bf16[272,1024]{1,0:T(8,128)(2,1)}, bf16[272,1024]{1,0:T(8,128)(2,1)S(1)}, u32[]{:S(2)}, u32[]{:S(2)}) collective-permute-start(bf16[272,1024]{1,0:T(8,128)(2,1)} %get-tuple-element.102), channel_id=1, source_target_pairs={{0,8},{8,0},{16,24},{24,16},{1,9},{9,1},{17,25},{25,17},{2,10},{10... | collective-permute-start | bytes 1671176 | tf_op jit(solution)/shard_map/ppermute | solution.py:247
  88.7 14.7 %collective-permute-start.26 = (bf16[272,1024]{1,0:T(8,128)(2,1)}, bf16[272,1024]{1,0:T(8,128)(2,1)S(1)}, u32[]{:S(2)}, u32[]{:S(2)}) collective-permute-start(bf16[272,1024]{1,0:T(8,128)(2,1)} %get-tuple-element.106), channel_id=1, source_target_pairs={{0,16},{8,24},{16,0},{24,8},{1,17},{9,25},{17,1},{25,9},{2,18},{10... | collective-permute-start | bytes 1671176 | tf_op jit(solution)/shard_map/ppermute | solution.py:247
  89.9 47.9 %collective-permute-start.15 = (bf16[64,4096]{1,0:T(8,128)(2,1)S(1)}, bf16[64,4096]{1,0:T(8,128)(2,1)S(1)}, u32[]{:S(2)}, u32[]{:S(2)}) collective-permute-start(bf16[64,4096]{1,0:T(8,128)(2,1)S(1)} %pad_maximum_fusion.1), channel_id=1, source_target_pairs={{0,1},{1,0},{2,3},{3,2},{4,5},{5,4},{6,7},{7,6},{8,9},{9,8},{10,11... | collective-permute-start | bytes 1572872 | tf_op jit(solution)/shard_map/ppermute | solution.py:247
  97.9 11.3 %collective-permute-start.22 = (bf16[32,4096]{1,0:T(8,128)(2,1)}, bf16[32,4096]{1,0:T(8,128)(2,1)S(1)}, u32[]{:S(2)}, u32[]{:S(2)}) collective-permute-start(bf16[32,4096]{1,0:T(8,128)(2,1)} %get-tuple-element.97), channel_id=1, source_target_pairs={{0,6},{1,7},{2,4},{3,5},{4,2},{5,3},{6,0},{7,1},{8,14},{9,15},{10,... | collective-permute-start | bytes 786440 | tf_op jit(solution)/shard_map/ppermute | solution.py:247
  99.1 22.5 %collective-permute-start.21 = (bf16[32,4096]{1,0:T(8,128)(2,1)}, bf16[32,4096]{1,0:T(8,128)(2,1)S(1)}, u32[]{:S(2)}, u32[]{:S(2)}) collective-permute-start(bf16[32,4096]{1,0:T(8,128)(2,1)} %get-tuple-element.95), channel_id=1, source_target_pairs={{0,4},{1,5},{2,6},{3,7},{4,0},{5,1},{6,2},{7,3},{8,12},{9,13},{10,... | collective-permute-start | bytes 786440 | tf_op jit(solution)/shard_map/ppermute | solution.py:247
  100.0 22.1 %collective-permute-start.20 = (bf16[32,4096]{1,0:T(8,128)(2,1)}, bf16[32,4096]{1,0:T(8,128)(2,1)S(1)}, u32[]{:S(2)}, u32[]{:S(2)}) collective-permute-start(bf16[32,4096]{1,0:T(8,128)(2,1)} %get-tuple-element.93), channel_id=1, source_target_pairs={{0,2},{1,3},{2,0},{3,1},{4,6},{5,7},{6,4},{7,5},{8,10},{9,11},{10,... | collective-permute-start | bytes 786440 | tf_op jit(solution)/shard_map/ppermute | solution.py:247
  103.4 19.8 %collective-permute-start.25 = (bf16[136,1024]{1,0:T(8,128)(2,1)S(1)}, bf16[136,1024]{1,0:T(8,128)(2,1)S(1)}, u32[]{:S(2)}, u32[]{:S(2)}) collective-permute-start(bf16[136,1024]{1,0:T(8,128)(2,1)S(1)} %add_convert_fusion.6), channel_id=1, source_target_pairs={{0,16},{8,24},{16,0},{24,8},{1,17},{9,25},{17,1},{25,9},{2,18},{10... | collective-permute-start | bytes 835592 | tf_op jit(solution)/shard_map/ppermute | solution.py:247
  109.2 14.3 %collective-permute-start.27 = (bf16[136,1024]{1,0:T(8,128)(2,1)S(1)}, bf16[136,1024]{1,0:T(8,128)(2,1)S(1)}, u32[]{:S(2)}, u32[]{:S(2)}) collective-permute-start(bf16[136,1024]{1,0:T(8,128)(2,1)S(1)} %add_convert_fusion.4), channel_id=1, source_target_pairs={{0,8},{8,0},{16,24},{24,16},{1,9},{9,1},{17,25},{25,17},{2,10},{10... | collective-permute-start | bytes 835592 | tf_op jit(solution)/shard_map/ppermute | solution.py:247
  121.6 14.2 %collective-permute-start.28 = (bf16[272,1024]{1,0:T(8,128)(2,1)S(1)}, bf16[272,1024]{1,0:T(8,128)(2,1)S(1)}, u32[]{:S(2)}, u32[]{:S(2)}) collective-permute-start(bf16[272,1024]{1,0:T(8,128)(2,1)S(1)} %copy-done.25), channel_id=1, source_target_pairs={{0,8},{8,0},{16,24},{24,16},{1,9},{9,1},{17,25},{25,17},{2,10},{10... | collective-permute-start | bytes 1671176 | tf_op jit(solution)/shard_map/ppermute | solution.py:247
  122.2 14.8 %collective-permute-start.30 = (bf16[272,1024]{1,0:T(8,128)(2,1)S(1)}, bf16[272,1024]{1,0:T(8,128)(2,1)S(1)}, u32[]{:S(2)}, u32[]{:S(2)}) collective-permute-start(bf16[272,1024]{1,0:T(8,128)(2,1)S(1)} %copy-done.24), channel_id=1, source_target_pairs={{0,16},{8,24},{16,0},{24,8},{1,17},{9,25},{17,1},{25,9},{2,18},{10... | collective-permute-start | bytes 1671176 | tf_op jit(solution)/shard_map/ppermute | solution.py:247
  123.2 14.6 %collective-permute-start.23 = (bf16[64,4096]{1,0:T(8,128)(2,1)S(1)}, bf16[64,4096]{1,0:T(8,128)(2,1)S(1)}, u32[]{:S(2)}, u32[]{:S(2)}) collective-permute-start(bf16[64,4096]{1,0:T(8,128)(2,1)S(1)} %pad_maximum_fusion.2), channel_id=1, source_target_pairs={{0,1},{1,0},{2,3},{3,2},{4,5},{5,4},{6,7},{7,6},{8,9},{9,8},{10,11... | collective-permute-start | bytes 1572872 | tf_op jit(solution)/shard_map/ppermute | solution.py:247
  135.9 7.4 %collective-permute-start.29 = (bf16[136,1024]{1,0:T(8,128)(2,1)S(1)}, bf16[136,1024]{1,0:T(8,128)(2,1)S(1)}, u32[]{:S(2)}, u32[]{:S(2)}) collective-permute-start(bf16[136,1024]{1,0:T(8,128)(2,1)S(1)} %add_convert_fusion.2), channel_id=1, source_target_pairs={{0,16},{8,24},{16,0},{24,8},{1,17},{9,25},{17,1},{25,9},{2,18},{10... | collective-permute-start | bytes 835592 | tf_op jit(solution)/shard_map/ppermute | solution.py:247
  137.0 7.2 %collective-permute-start.31 = (bf16[136,1024]{1,0:T(8,128)(2,1)S(1)}, bf16[136,1024]{1,0:T(8,128)(2,1)S(1)}, u32[]{:S(2)}, u32[]{:S(2)}) collective-permute-start(bf16[136,1024]{1,0:T(8,128)(2,1)S(1)} %add_convert_fusion), channel_id=1, source_target_pairs={{0,8},{8,0},{16,24},{24,16},{1,9},{9,1},{17,25},{25,17},{2,10},{10... | collective-permute-start | bytes 835592 | tf_op jit(solution)/shard_map/ppermute | solution.py:247
  (38 other events, 401.5 us)

commit v2 on v1

--- a/solution.py
+++ b/solution.py
@@ -117,14 +117,6 @@
     return bits if expert % 2 == 0 else bits[::-1]
 
 
-def halving(size, expert):
-    rounds, held = [], list(range(size))
-    for bit in bits_of(size, expert):
-        rounds.append(([r for r in held if r & bit], [r for r in held if not r & bit]))
-        held = rounds[-1][1]
-    return rounds
-
-
 def chunk_kernel(devs, held, chunk, *refs):
     me_ref, filter_ref = refs[0], refs[1]
     refs = refs[2:]
@@ -132,9 +124,9 @@
     (own_ref, swapped_ref, *far_refs), refs = refs[: far + 1], refs[far + 1 :]
     weight_refs, refs = refs[: len(held)], refs[len(held) :]
     backs, refs = refs[:far], refs[far:]
-    reduce_refs, refs = refs[: 2 * CHUNK], refs[2 * CHUNK :]
+    shards_n = sum(map(len, held)) // CHUNK
+    reduce_refs, refs = refs[:shards_n], refs[shards_n:]
     matrix, rows_f32, hidden, preact, dpre, dhidden, grad, results = refs
-    shards_n = sum(map(len, held)) // CHUNK
     width = own_ref.shape[1]
     channels = matrix.shape[1]
     bins = width // channels
@@ -177,12 +169,9 @@
             ).astype(BF16)
         dhidden[...] = dot(dpre[...], matrix[expert], ((1,), (1,)))
         grad[...] = dot(hidden[...], dpre[...], ((0,), (0,))).astype(BF16)
-        rounds = halving(shards_n, expert)[0]
-        for ref, relatives in zip(reduce_refs[2 * expert : 2 * expert + 2], rounds):
-            for index, relative in enumerate(relatives):
-                begin = pl.multiple_of((me_ref[0] ^ relative) * local, local)
-                row = index * (local + PAD)
-                ref[row : row + local, :] = grad[pl.ds(begin, local), :]
+        for relative, ref in enumerate(reduce_refs):
+            begin = pl.multiple_of((me_ref[0] ^ relative) * local, local)
+            ref[expert * local : (expert + 1) * local, :] = grad[pl.ds(begin, local), :]
         for q in range(bins):
             acc = None
             for j, off in enumerate(OFFSETS):
@@ -199,10 +188,9 @@
                     acc = term if acc is None else acc + term
             lines.append(jnp.sum(acc, axis=0, keepdims=True))
         tail = jnp.concatenate(lines + [jnp.zeros((PAD - KERNEL_TAPS, channels), F32)], axis=0)
-        tail = jnp.concatenate([tail, jnp.zeros_like(tail)], axis=1).astype(BF16)
-        for ref in reduce_refs[2 * expert : 2 * expert + 2]:
-            for row in range(local, ref.shape[0], local + PAD):
-                ref[row : row + PAD, :] = tail
+        lanes = slice(expert * channels, (expert + 1) * channels)
+        for ref in reduce_refs:
+            ref[CHUNK * local : CHUNK * local + PAD, lanes] = tail.astype(BF16)
     unsort = sorting(devs, 1)
     for p in range(bins):
         lanes = slice(p * channels, (p + 1) * channels)
@@ -234,8 +222,13 @@
 VMEM = pl.BlockSpec(memory_space=pltpu.VMEM)
 SMEM = pl.BlockSpec(memory_space=pltpu.SMEM)
 COSTS = (2, 3, 2)
-LATE = False
-PLANE = 4
+LATE = 1
+PLANE = 2
+AG1_FIRST = True
+D1_AFTER = "gather0last"
+K_AFTER = ["gather1first", ""]
+R_AFTER = ['gather1last', 'sums0']
+R_LAST = ["", ""]
 WINDOW = 3
 
 
@@ -304,18 +297,27 @@
         return [moved[r] for r in range(far)]
 
     plane = []
-
-    def in_plane(value, bit):
+    steps = {}
+    rounds_n = shards_n.bit_length() - 1
+
+    def in_plane(value, bit, step):
         if len(plane) >= PLANE:
             value = after(value, plane[-PLANE])
         plane.append(flip(value, "dp", bit))
+        steps.setdefault(step, []).append(plane[-1])
         return plane[-1]
 
-    def gather(parts):
+    def wait(value, name):
+        names = [n for n in (name or "").split() if n]
+        others = [v for n in names for v in steps[n]]
+        return after(value, *others) if others else value
+
+    def gather(parts, chunk):
         held = [(part, [0]) for part in parts]
         for turn in range(shards_n.bit_length() - 1):
             bits = [bits_of(shards_n, expert)[turn] for expert in range(CHUNK)]
-            came = [in_plane(value, bit) for (value, _), bit in zip(held, bits)]
+            step = f"gather{chunk}" + ("first" if turn == 0 else "last")
+            came = [in_plane(value, bit, step) for (value, _), bit in zip(held, bits)]
             new = [
                 (other, [place ^ bit for place in places])
                 for (_, places), other, bit in zip(held, came, bits)
@@ -331,59 +333,39 @@
                 for (old, places), (other, more) in zip(held, new)
             ]
 
-    def scatter(pairs):
-        rounds = [halving(shards_n, expert) for expert in range(CHUNK)]
-        size = local + PAD
-        for turn in range(len(rounds[0])):
-            came = [
-                in_plane(send, bits_of(shards_n, expert)[turn])
-                for expert, (send, _) in enumerate(pairs)
-            ]
-            if turn + 1 == len(rounds[0]):
-                return [
-                    keep.astype(F32) + other.astype(F32)
-                    for (_, keep), other in zip(pairs, came)
-                ]
-            new = []
-            for expert, ((_, keep), other) in enumerate(zip(pairs, came)):
-                places = rounds[expert][turn][1]
-                total = lambda r: (
-                    keep[places.index(r) * size : (places.index(r) + 1) * size].astype(F32)
-                    + other[places.index(r) * size : (places.index(r) + 1) * size].astype(F32)
-                ).astype(BF16)
-                new.append(
-                    [
-                        jnp.concatenate([total(r) for r in relatives], axis=0)
-                        for relatives in rounds[expert][turn + 1]
-                    ]
-                )
-            pairs = new
-
     weights = jnp.transpose(after(point_weight, tables[0]), (1, 0, 2))
-    arrived = []
-    for *own, relayed in sent:
+    def dispatched(chunk):
+        *own, relayed = sent[chunk]
         relayed = flip(relayed, "expert", 1)
         pairs = [
             jnp.concatenate([own[r], relayed[r * ROWS : (r + 1) * ROWS]], axis=0)
             for r in range(1, far)
         ]
-        arrived.append([own[0], relayed] + along_line([own[0]] + pairs)[1:])
-    gathered = [
-        gather(
-            [
-                after(weights[chunk * CHUNK + expert], arrived[chunk][1])
-                for expert in range(CHUNK)
-            ]
-        )
-        for chunk in range(chunks)
-    ]
-    half = jax.ShapeDtypeStruct((shards_n // 2 * (local + PAD), out_channels), BF16)
+        if chunk > 0:
+            pairs = [wait(value, D1_AFTER) for value in pairs]
+        return [own[0], relayed] + along_line([own[0]] + pairs)[1:]
+
+    def weights_of(chunk, other):
+        parts = [weights[chunk * CHUNK + expert] for expert in range(CHUNK)]
+        return gather([after(part, other) for part in parts], chunk)
+
+    arrived = [dispatched(0)]
+    gathered = [weights_of(0, arrived[0][1])]
+    for chunk in range(1, chunks):
+        if AG1_FIRST:
+            gathered.append(weights_of(chunk, sent[chunk][-1]))
+            arrived.append(dispatched(chunk))
+        else:
+            arrived.append(dispatched(chunk))
+            gathered.append(weights_of(chunk, arrived[chunk][1]))
+    block_sum = jax.ShapeDtypeStruct((CHUNK * local + PAD, out_channels), BF16)
     backs = []
     reduced = []
     for chunk in range(chunks):
         full, held = zip(*gathered[chunk])
+        arrived[chunk][0] = wait(arrived[chunk][0], K_AFTER[chunk])
         pair = jax.ShapeDtypeStruct((2 * ROWS, width), BF16)
-        outs = [pair] * far + [half] * (2 * CHUNK)
+        outs = [pair] * far + [block_sum] * shards_n
         outs = pl.pallas_call(
             functools.partial(chunk_kernel, devs, held, chunk),
             out_shape=outs,
@@ -407,12 +389,34 @@
             name="experts",
         )(me_dp, depth_filter, *arrived[chunk], *full)
         results, to_reduce = list(outs[:far]), outs[far:]
-        reduced += scatter(list(zip(to_reduce[::2], to_reduce[1::2])))
-        if LATE and chunk + 1 == chunks:
-            results[1] = after(results[1], *reduced)
+        steps[f"sums{chunk}"] = [
+            flip(to_reduce[r], "dp", r) for r in sorted(range(1, shards_n), reverse=True)
+        ]
+        summed = to_reduce[0].astype(F32)
+        for value in steps[f"sums{chunk}"]:
+            summed = summed + value.astype(F32)
+        for expert in range(CHUNK):
+            lanes = slice(expert * channels, (expert + 1) * channels)
+            taps = summed[CHUNK * local : CHUNK * local + KERNEL_TAPS, lanes]
+            reduced.append((summed[expert * local : (expert + 1) * local], taps))
+        results = [wait(value, R_AFTER[chunk]) for value in results]
+        results[order[-1]] = wait(results[order[-1]], R_LAST[chunk])
         near = along_line(results)
-        swapped = flip(jnp.concatenate([value[ROWS:] for value in near], axis=0), "expert", 1)
-        backs += near + [swapped]
+        backs.append(near)
+    point_grads = jnp.stack([value for value, _ in reduced], axis=1)
+    depth_grads = jnp.stack([value for _, value in reduced], axis=0)
+    lists, backs = backs, []
+    for chunk, near in enumerate(lists):
+        value = jnp.concatenate([value[ROWS:] for value in near], axis=0)
+        if LATE == 1 and chunk + 1 == chunks:
+            value, point_grads, depth_grads = lax.optimization_barrier(
+                (value, point_grads, depth_grads)
+            )
+        backs += near + [flip(value, "expert", 1)]
+    if LATE == 2:
+        backs[-1], point_grads, depth_grads = lax.optimization_barrier(
+            (backs[-1], point_grads, depth_grads)
+        )
 
     mixed, token_grads = pl.pallas_call(
         functools.partial(combine_kernel, chunks),
@@ -426,10 +430,6 @@
         cost_estimate=cost(COSTS[2]),
         name="combine",
     )(route_weights, *tables, *backs)
-    point_grads = jnp.stack([value[:local] for value in reduced], axis=1)
-    depth_grads = jnp.stack(
-        [value[local : local + KERNEL_TAPS, :channels] for value in reduced], axis=0
-    )
     return (mixed, token_grads, point_grads, depth_grads)
 
 

time: 148 us -> 123 us (0.83)
  waiting for transfers between devices: 69.4 us -> 28.2 us
  starting transfers between devices: 43.1 us -> 61.3 us
  local copies, waits for them, and re-layouts: 9.82 us -> 7.71 us
    ppermute x32 -> x30, waiting for transfers between devices: 69.4 us -> 28.2 us  [flip(): lax.ppermute(value, axis, [(k, k ^ bits) for k in range(lax.axis_size(axi...]
    ppermute x32 -> x30, starting transfers between devices: 43.1 us -> 61.3 us  [flip(): lax.ppermute(value, axis, [(k, k ^ bits) for k in range(lax.axis_size(axi...]
    unnamed x83 -> x87, local copies, waits for them, and re-layouts: 7.27 us -> 6.08 us
  transfers between devices with their start and end apart: 32 -> 30, of which waited for: 10 -> 9; matrix products, arithmetic and copies ran while one was open for 3% -> 6% of each run, Pallas kernels for 14% -> 13%
where the time goes in v2:
time: 123 us
  starting transfers between devices  61.3 us (50%)
  waiting for transfers between devices  28.2 us (23%)
  Pallas kernels  23 us (19%)
  local copies, waits for them, and re-layouts  7.71 us (6%)
  between operations  1.35 us (1%)
    ppermute x30, starting transfers between devices, flip(): lax.ppermute(value, axis, [(k, k ^ bits) for k in range(lax.axis_size(axi...  61.3 us
    ppermute x30, waiting for transfers between devices, flip(): lax.ppermute(value, axis, [(k, k ^ bits) for k in range(lax.axis_size(axi...  28.2 us
    pallas_call x2, Pallas kernels, shards(): pl.pallas_call(functools.partial(chunk_kernel, devs, held, chunk), out_sh...  13.5 us
    unnamed x87, local copies, waits for them, and re-layouts  6.08 us
    pallas_call x2, Pallas kernels, shards(): pl.pallas_call(functools.partial(dispatch_kernel, devs, chunks, chunk), g...  5.97 us
    pallas_call x1, Pallas kernels, shards(): pl.pallas_call(functools.partial(combine_kernel, chunks), grid=(1,), out_...  3.54 us
  transfers between devices with their start and end apart: 30, of which 9 were waited for; matrix products, arithmetic and copies ran while one was open for 6% of the time, Pallas kernels for 13%

profile of v2, /device:TPU:0, one launch (start us, length us, event | category | flops | bytes accessed | tf_op | source)
XLA Modules:
  0.0 122.7 jit_solution(17700706356458445503)
XLA Ops:
  0.6 3.0 %dispatch.2 = (bf16[192,128]{1,0:T(8,128)(2,1)}, bf16[16,4096]{1,0:T(8,128)(2,1)}, bf16[16,4096]{1,0:T(8,128)(2,1)}, bf16[16,4096]{1,0:T(8,128)(2,1)}, bf16[16,4...) custom-call(s32[1]{0:T(128)} %bitcast.1.me_ref, s32[2,64]{1,0:T(2,128)} %bitcast.32, f32[2,64]{1,0:T(2,128)} %bitcast.34, ...), custom_call_target="tpu_custom_call" | custom-call | flops 2000000000 | bytes 8388608 | tf_op jit(solution)/shard_map/dispatch/pallas_call | solution.py:269
  4.1 3.0 %dispatch.3 = (bf16[192,128]{1,0:T(8,128)(2,1)}, bf16[16,4096]{1,0:T(8,128)(2,1)}, bf16[16,4096]{1,0:T(8,128)(2,1)}, bf16[16,4096]{1,0:T(8,128)(2,1)}, bf16[16,4...) custom-call(s32[1]{0:T(128)} %bitcast.1.me_ref, s32[2,64]{1,0:T(2,128)} %bitcast.33, f32[2,64]{1,0:T(2,128)} %bitcast.35, ...), custom_call_target="tpu_custom_call" | custom-call | flops 2000000000 | bytes 8388608 | tf_op jit(solution)/shard_map/dispatch/pallas_call | solution.py:269
  8.4 2.9 %collective-permute-start.1 = (bf16[128,1024]{1,0:T(8,128)(2,1)S(1)}, bf16[128,1024]{1,0:T(8,128)(2,1)S(1)}, u32[]{:S(2)}, u32[]{:S(2)}) collective-permute-start(bf16[128,1024]{1,0:T(8,128)(2,1)S(1)} %get-tuple-element.76), channel_id=1, source_target_pairs={{0,8},{8,0},{16,24},{24,16},{1,9},{9,1},{17,25},{25,17},{2,10},{10... | collective-permute-start | bytes 786440 | tf_op jit(solution)/shard_map/ppermute | solution.py:240
  11.3 1.5 %collective-permute-start.4 = (bf16[128,1024]{1,0:T(8,128)(2,1)S(1)}, bf16[128,1024]{1,0:T(8,128)(2,1)S(1)}, u32[]{:S(2)}, u32[]{:S(2)}) collective-permute-start(bf16[128,1024]{1,0:T(8,128)(2,1)S(1)} %get-tuple-element.80), channel_id=1, source_target_pairs={{0,16},{8,24},{16,0},{24,8},{1,17},{9,25},{17,1},{25,9},{2,18},{10... | collective-permute-start | bytes 786440 | tf_op jit(solution)/shard_map/ppermute | solution.py:240
  12.9 1.6 %collective-permute-start.7 = (bf16[32,4096]{1,0:T(8,128)(2,1)S(1)}, bf16[32,4096]{1,0:T(8,128)(2,1)S(1)}, u32[]{:S(2)}, u32[]{:S(2)}) collective-permute-start(bf16[32,4096]{1,0:T(8,128)(2,1)S(1)} %pad_maximum_fusion.3), channel_id=1, source_target_pairs={{0,2},{1,3},{2,0},{3,1},{4,6},{5,7},{6,4},{7,5},{8,10},{9,11},{10,... | collective-permute-start | bytes 786440 | tf_op jit(solution)/shard_map/ppermute | solution.py:240
  14.6 2.7 %collective-permute-start.8 = (bf16[32,4096]{1,0:T(8,128)(2,1)S(1)}, bf16[32,4096]{1,0:T(8,128)(2,1)S(1)}, u32[]{:S(2)}, u32[]{:S(2)}) collective-permute-start(bf16[32,4096]{1,0:T(8,128)(2,1)S(1)} %pad_maximum_fusion.4), channel_id=1, source_target_pairs={{0,4},{1,5},{2,6},{3,7},{4,0},{5,1},{6,2},{7,3},{8,12},{9,13},{10,... | collective-permute-start | bytes 786440 | tf_op jit(solution)/shard_map/ppermute | solution.py:240
  17.9 3.9 %collective-permute-start.9 = (bf16[32,4096]{1,0:T(8,128)(2,1)S(1)}, bf16[32,4096]{1,0:T(8,128)(2,1)S(1)}, u32[]{:S(2)}, u32[]{:S(2)}) collective-permute-start(bf16[32,4096]{1,0:T(8,128)(2,1)S(1)} %pad_maximum_fusion.5), channel_id=1, source_target_pairs={{0,6},{1,7},{2,4},{3,5},{4,2},{5,3},{6,0},{7,1},{8,14},{9,15},{10,... | collective-permute-start | bytes 786440 | tf_op jit(solution)/shard_map/ppermute | solution.py:240
  21.8 1.6 %collective-permute-start.2 = (bf16[256,1024]{1,0:T(8,128)(2,1)S(1)}, bf16[256,1024]{1,0:T(8,128)(2,1)S(1)}, u32[]{:S(2)}, u32[]{:S(2)}) collective-permute-start(bf16[256,1024]{1,0:T(8,128)(2,1)S(1)} %constant_dynamic-update-slice_fusion.refs_7_), channel_id=1, source_target_pairs={{0,16},{8,24},{16,0},{24,8},{1,17},{9,25},{17,1},{25,9},{2,18},{10... | collective-permute-start | bytes 1572872 | tf_op jit(solution)/shard_map/ppermute | solution.py:240
  23.4 1.6 %collective-permute-start.5 = (bf16[256,1024]{1,0:T(8,128)(2,1)S(1)}, bf16[256,1024]{1,0:T(8,128)(2,1)S(1)}, u32[]{:S(2)}, u32[]{:S(2)}) collective-permute-start(bf16[256,1024]{1,0:T(8,128)(2,1)S(1)} %constant_dynamic-update-slice_fusion.2.refs_9_), channel_id=1, source_target_pairs={{0,8},{8,0},{16,24},{24,16},{1,9},{9,1},{17,25},{25,17},{2,10},{10... | collective-permute-start | bytes 1572872 | tf_op jit(solution)/shard_map/ppermute | solution.py:240
  25.0 9.7 %collective-permute-done.2.refs_8_ = bf16[256,1024]{1,0:T(8,128)(2,1)S(1)} collective-permute-done((bf16[256,1024]{1,0:T(8,128)(2,1)S(1)}, bf16[256,1024]{1,0:T(8,128)(2,1)S(1)}, u32[]{:S(2)}, u32[]{:S(2)}) %collective-permute-start.2) | collective-permute-done | bytes 524320 | tf_op jit(solution)/shard_map/ppermute | solution.py:240
  34.7 1.5 %collective-permute-start.3 = (bf16[128,1024]{1,0:T(8,128)(2,1)S(1)}, bf16[128,1024]{1,0:T(8,128)(2,1)S(1)}, u32[]{:S(2)}, u32[]{:S(2)}) collective-permute-start(bf16[128,1024]{1,0:T(8,128)(2,1)S(1)} %get-tuple-element.78), channel_id=1, source_target_pairs={{0,8},{8,0},{16,24},{24,16},{1,9},{9,1},{17,25},{25,17},{2,10},{10... | collective-permute-start | bytes 786440 | tf_op jit(solution)/shard_map/ppermute | solution.py:240
  36.6 1.1 collective-permute-start.6
  37.7 3.9 %collective-permute-done.3 = bf16[128,1024]{1,0:T(8,128)(2,1)S(1)} collective-permute-done((bf16[128,1024]{1,0:T(8,128)(2,1)S(1)}, bf16[128,1024]{1,0:T(8,128)(2,1)S(1)}, u32[]{:S(2)}, u32[]{:S(2)}) %collective-permute-start.3) | collective-permute-done | bytes 262176 | tf_op jit(solution)/shard_map/ppermute | solution.py:240
  42.7 1.1 collective-permute-done.6
  43.8 1.6 %collective-permute-start.11 = (bf16[256,1024]{1,0:T(8,128)(2,1)S(1)}, bf16[256,1024]{1,0:T(8,128)(2,1)S(1)}, u32[]{:S(2)}, u32[]{:S(2)}) collective-permute-start(bf16[256,1024]{1,0:T(8,128)(2,1)S(1)} %constant_dynamic-update-slice_fusion.6.refs_9_), channel_id=1, source_target_pairs={{0,8},{8,0},{16,24},{24,16},{1,9},{9,1},{17,25},{25,17},{2,10},{10... | collective-permute-start | bytes 1572872 | tf_op jit(solution)/shard_map/ppermute | solution.py:240
  46.2 3.7 %collective-permute-start.17 = (bf16[32,4096]{1,0:T(8,128)(2,1)S(1)}, bf16[32,4096]{1,0:T(8,128)(2,1)S(1)}, u32[]{:S(2)}, u32[]{:S(2)}) collective-permute-start(bf16[32,4096]{1,0:T(8,128)(2,1)S(1)} %pad_maximum_fusion.8), channel_id=1, source_target_pairs={{0,6},{1,7},{2,4},{3,5},{4,2},{5,3},{6,0},{7,1},{8,14},{9,15},{10,... | collective-permute-start | bytes 786440 | tf_op jit(solution)/shard_map/ppermute | solution.py:240
  49.9 6.6 %experts.2 = (bf16[32,4096]{1,0:T(8,128)(2,1)}, bf16[32,4096]{1,0:T(8,128)(2,1)}, bf16[32,4096]{1,0:T(8,128)(2,1)}, bf16[32,4096]{1,0:T(8,128)(2,1)}, bf16[264,1...) custom-call(s32[1]{0:T(128)} %bitcast.3.refs_0_, ...), custom_call_target="tpu_custom_call" | custom-call | flops 3000000000 | bytes 8388608 | tf_op jit(solution)/shard_map/experts/pallas_call | solution.py:369
  56.8 1.6 %collective-permute-start.20 = (bf16[264,1024]{1,0:T(8,128)(2,1)}, bf16[264,1024]{1,0:T(8,128)(2,1)S(1)}, u32[]{:S(2)}, u32[]{:S(2)}) collective-permute-start(bf16[264,1024]{1,0:T(8,128)(2,1)} %get-tuple-element.111), channel_id=1, source_target_pairs={{0,24},{8,16},{16,8},{24,0},{1,25},{9,17},{17,9},{25,1},{2,26},{10... | collective-permute-start | bytes 1622024 | tf_op jit(solution)/shard_map/ppermute | solution.py:240
  59.2 1.1 collective-permute-start.22
  60.3 3.5 %collective-permute-done.15.refs_5_ = bf16[32,4096]{1,0:T(8,128)(2,1)S(1)} collective-permute-done((bf16[32,4096]{1,0:T(8,128)(2,1)S(1)}, bf16[32,4096]{1,0:T(8,128)(2,1)S(1)}, u32[]{:S(2)}, u32[]{:S(2)}) %collective-permute-start.15) | collective-permute-done | bytes 262176 | tf_op jit(solution)/shard_map/ppermute | solution.py:240
  63.8 4.1 %collective-permute-start.16 = (bf16[32,4096]{1,0:T(8,128)(2,1)}, bf16[32,4096]{1,0:T(8,128)(2,1)S(1)}, u32[]{:S(2)}, u32[]{:S(2)}) collective-permute-start(bf16[32,4096]{1,0:T(8,128)(2,1)} %get-tuple-element.102), channel_id=1, source_target_pairs={{0,4},{1,5},{2,6},{3,7},{4,0},{5,1},{6,2},{7,3},{8,12},{9,13},{10,... | collective-permute-start | bytes 786440 | tf_op jit(solution)/shard_map/ppermute | solution.py:240
  68.9 6.8 %experts.3 = (bf16[32,4096]{1,0:T(8,128)(2,1)}, bf16[32,4096]{1,0:T(8,128)(2,1)}, bf16[32,4096]{1,0:T(8,128)(2,1)}, bf16[32,4096]{1,0:T(8,128)(2,1)}, bf16[264,1...) custom-call(s32[1]{0:T(128)} %bitcast.3.refs_0_, ...), custom_call_target="tpu_custom_call" | custom-call | flops 3000000000 | bytes 8388608 | tf_op jit(solution)/shard_map/experts/pallas_call | solution.py:369
  75.8 3.4 %collective-permute-start.18 = (bf16[32,4096]{1,0:T(8,128)(2,1)S(1)}, bf16[32,4096]{1,0:T(8,128)(2,1)S(1)}, u32[]{:S(2)}, u32[]{:S(2)}) collective-permute-start(bf16[32,4096]{1,0:T(8,128)(2,1)S(1)} %copy-done.33), channel_id=1, source_target_pairs={{0,6},{1,7},{2,4},{3,5},{4,2},{5,3},{6,0},{7,1},{8,14},{9,15},{10,... | collective-permute-start | bytes 786440 | tf_op jit(solution)/shard_map/ppermute | solution.py:240
  79.8 1.6 %collective-permute-start.27 = (bf16[264,1024]{1,0:T(8,128)(2,1)}, bf16[264,1024]{1,0:T(8,128)(2,1)S(1)}, u32[]{:S(2)}, u32[]{:S(2)}) collective-permute-start(bf16[264,1024]{1,0:T(8,128)(2,1)} %get-tuple-element.127), channel_id=1, source_target_pairs={{0,16},{8,24},{16,0},{24,8},{1,17},{9,25},{17,1},{25,9},{2,18},{10... | collective-permute-start | bytes 1622024 | tf_op jit(solution)/shard_map/ppermute | solution.py:240
  82.4 1.7 %collective-permute-done.18.refs_5_ = bf16[32,4096]{1,0:T(8,128)(2,1)S(1)} collective-permute-done((bf16[32,4096]{1,0:T(8,128)(2,1)S(1)}, bf16[32,4096]{1,0:T(8,128)(2,1)S(1)}, u32[]{:S(2)}, u32[]{:S(2)}) %collective-permute-start.18) | collective-permute-done | bytes 262176 | tf_op jit(solution)/shard_map/ppermute | solution.py:240
  84.1 3.5 %collective-permute-start.25 = (bf16[32,4096]{1,0:T(8,128)(2,1)S(1)}, bf16[32,4096]{1,0:T(8,128)(2,1)S(1)}, u32[]{:S(2)}, u32[]{:S(2)}) collective-permute-start(bf16[32,4096]{1,0:T(8,128)(2,1)S(1)} %copy-done.38), channel_id=1, source_target_pairs={{0,6},{1,7},{2,4},{3,5},{4,2},{5,3},{6,0},{7,1},{8,14},{9,15},{10,... | collective-permute-start | bytes 786440 | tf_op jit(solution)/shard_map/ppermute | solution.py:240
  87.7 2.2 %collective-permute-start.26 = (bf16[264,1024]{1,0:T(8,128)(2,1)S(1)}, bf16[264,1024]{1,0:T(8,128)(2,1)S(1)}, u32[]{:S(2)}, u32[]{:S(2)}) collective-permute-start(bf16[264,1024]{1,0:T(8,128)(2,1)S(1)} %copy-done.23), channel_id=1, source_target_pairs={{0,24},{8,16},{16,8},{24,0},{1,25},{9,17},{17,9},{25,1},{2,26},{10... | collective-permute-start | bytes 1622024 | tf_op jit(solution)/shard_map/ppermute | solution.py:240
  89.9 8.3 %collective-permute-start.23 = (bf16[32,4096]{1,0:T(8,128)(2,1)S(1)}, bf16[32,4096]{1,0:T(8,128)(2,1)S(1)}, u32[]{:S(2)}, u32[]{:S(2)}) collective-permute-start(bf16[32,4096]{1,0:T(8,128)(2,1)S(1)} %copy-done.34), channel_id=1, source_target_pairs={{0,2},{1,3},{2,0},{3,1},{4,6},{5,7},{6,4},{7,5},{8,10},{9,11},{10,... | collective-permute-start | bytes 786440 | tf_op jit(solution)/shard_map/ppermute | solution.py:240
  98.3 7.7 %collective-permute-start.24 = (bf16[32,4096]{1,0:T(8,128)(2,1)S(1)}, bf16[32,4096]{1,0:T(8,128)(2,1)S(1)}, u32[]{:S(2)}, u32[]{:S(2)}) collective-permute-start(bf16[32,4096]{1,0:T(8,128)(2,1)S(1)} %copy-done.35), channel_id=1, source_target_pairs={{0,4},{1,5},{2,6},{3,7},{4,0},{5,1},{6,2},{7,3},{8,12},{9,13},{10,... | collective-permute-start | bytes 786440 | tf_op jit(solution)/shard_map/ppermute | solution.py:240
  106.0 7.1 %collective-permute-done.24.refs_9_ = bf16[32,4096]{1,0:T(8,128)(2,1)S(1)} collective-permute-done((bf16[32,4096]{1,0:T(8,128)(2,1)S(1)}, bf16[32,4096]{1,0:T(8,128)(2,1)S(1)}, u32[]{:S(2)}, u32[]{:S(2)}) %collective-permute-start.24) | collective-permute-done | bytes 262176 | tf_op jit(solution)/shard_map/ppermute | solution.py:240
  114.9 2.7 %copy.13 = f32[128,4,1024]{2,1,0:T(4,128)} copy(f32[128,4,1024]{2,0,1:T(8,128)S(1)} %pad_maximum_fusion) | data formatting | bytes 4194304
  119.2 3.5 %combine.1 = (bf16[64,4096]{1,0:T(8,128)(2,1)}, bf16[64,4096]{1,0:T(8,128)(2,1)}) custom-call(f32[2,64]{1,0:T(2,128)} %bitcast.36, bf16[192,128]{1,0:T(8,128)(2,1)} %get-tuple-element.69.refs_0_, bf16[192,128]{1,0:T(8,128)(2,1)} %get-tuple-element.70.refs_1_, bf16[32,4096]{1,0:T(8,128)(2,1)} %get-tuple-element.90.refs_2_, bf16[32,4096]{1,0:T(8,128)(2,1)} %copy-done.15, ...), custom_call_target="tpu_custom_call" | custom-call | flops 2000000000 | bytes 8388608 | tf_op jit(solution)/shard_map/combine/pallas_call | solution.py:421
  (151 shorter events, 11.7 us)
Async XLA Ops:
  3.6 4.7 %collective-permute-start = (bf16[64,4096]{1,0:T(8,128)(2,1)}, bf16[64,4096]{1,0:T(8,128)(2,1)S(1)}, u32[]{:S(2)}, u32[]{:S(2)}) collective-permute-start(bf16[64,4096]{1,0:T(8,128)(2,1)} %get-tuple-element.75), channel_id=1, source_target_pairs={{0,1},{1,0},{2,3},{3,2},{4,5},{5,4},{6,7},{7,6},{8,9},{9,8},{10,11... | collective-permute-start | bytes 1572872 | tf_op jit(solution)/shard_map/ppermute | solution.py:240
  7.1 16.3 %collective-permute-start.12 = (bf16[64,4096]{1,0:T(8,128)(2,1)}, bf16[64,4096]{1,0:T(8,128)(2,1)S(1)}, u32[]{:S(2)}, u32[]{:S(2)}) collective-permute-start(bf16[64,4096]{1,0:T(8,128)(2,1)} %get-tuple-element.73), channel_id=1, source_target_pairs={{0,1},{1,0},{2,3},{3,2},{4,5},{5,4},{6,7},{7,6},{8,9},{9,8},{10,11... | collective-permute-start | bytes 1572872 | tf_op jit(solution)/shard_map/ppermute | solution.py:240
  8.4 9.5 %collective-permute-start.1 = (bf16[128,1024]{1,0:T(8,128)(2,1)S(1)}, bf16[128,1024]{1,0:T(8,128)(2,1)S(1)}, u32[]{:S(2)}, u32[]{:S(2)}) collective-permute-start(bf16[128,1024]{1,0:T(8,128)(2,1)S(1)} %get-tuple-element.76), channel_id=1, source_target_pairs={{0,8},{8,0},{16,24},{24,16},{1,9},{9,1},{17,25},{25,17},{2,10},{10... | collective-permute-start | bytes 786440 | tf_op jit(solution)/shard_map/ppermute | solution.py:240
  11.3 10.5 %collective-permute-start.4 = (bf16[128,1024]{1,0:T(8,128)(2,1)S(1)}, bf16[128,1024]{1,0:T(8,128)(2,1)S(1)}, u32[]{:S(2)}, u32[]{:S(2)}) collective-permute-start(bf16[128,1024]{1,0:T(8,128)(2,1)S(1)} %get-tuple-element.80), channel_id=1, source_target_pairs={{0,16},{8,24},{16,0},{24,8},{1,17},{9,25},{17,1},{25,9},{2,18},{10... | collective-permute-start | bytes 786440 | tf_op jit(solution)/shard_map/ppermute | solution.py:240
  12.9 32.5 %collective-permute-start.7 = (bf16[32,4096]{1,0:T(8,128)(2,1)S(1)}, bf16[32,4096]{1,0:T(8,128)(2,1)S(1)}, u32[]{:S(2)}, u32[]{:S(2)}) collective-permute-start(bf16[32,4096]{1,0:T(8,128)(2,1)S(1)} %pad_maximum_fusion.3), channel_id=1, source_target_pairs={{0,2},{1,3},{2,0},{3,1},{4,6},{5,7},{6,4},{7,5},{8,10},{9,11},{10,... | collective-permute-start | bytes 786440 | tf_op jit(solution)/shard_map/ppermute | solution.py:240
  14.6 31.0 %collective-permute-start.8 = (bf16[32,4096]{1,0:T(8,128)(2,1)S(1)}, bf16[32,4096]{1,0:T(8,128)(2,1)S(1)}, u32[]{:S(2)}, u32[]{:S(2)}) collective-permute-start(bf16[32,4096]{1,0:T(8,128)(2,1)S(1)} %pad_maximum_fusion.4), channel_id=1, source_target_pairs={{0,4},{1,5},{2,6},{3,7},{4,0},{5,1},{6,2},{7,3},{8,12},{9,13},{10,... | collective-permute-start | bytes 786440 | tf_op jit(solution)/shard_map/ppermute | solution.py:240
  17.9 28.4 %collective-permute-start.9 = (bf16[32,4096]{1,0:T(8,128)(2,1)S(1)}, bf16[32,4096]{1,0:T(8,128)(2,1)S(1)}, u32[]{:S(2)}, u32[]{:S(2)}) collective-permute-start(bf16[32,4096]{1,0:T(8,128)(2,1)S(1)} %pad_maximum_fusion.5), channel_id=1, source_target_pairs={{0,6},{1,7},{2,4},{3,5},{4,2},{5,3},{6,0},{7,1},{8,14},{9,15},{10,... | collective-permute-start | bytes 786440 | tf_op jit(solution)/shard_map/ppermute | solution.py:240
  21.8 12.9 %collective-permute-start.2 = (bf16[256,1024]{1,0:T(8,128)(2,1)S(1)}, bf16[256,1024]{1,0:T(8,128)(2,1)S(1)}, u32[]{:S(2)}, u32[]{:S(2)}) collective-permute-start(bf16[256,1024]{1,0:T(8,128)(2,1)S(1)} %constant_dynamic-update-slice_fusion.refs_7_), channel_id=1, source_target_pairs={{0,16},{8,24},{16,0},{24,8},{1,17},{9,25},{17,1},{25,9},{2,18},{10... | collective-permute-start | bytes 1572872 | tf_op jit(solution)/shard_map/ppermute | solution.py:240
  23.4 13.2 %collective-permute-start.5 = (bf16[256,1024]{1,0:T(8,128)(2,1)S(1)}, bf16[256,1024]{1,0:T(8,128)(2,1)S(1)}, u32[]{:S(2)}, u32[]{:S(2)}) collective-permute-start(bf16[256,1024]{1,0:T(8,128)(2,1)S(1)} %constant_dynamic-update-slice_fusion.2.refs_9_), channel_id=1, source_target_pairs={{0,8},{8,0},{16,24},{24,16},{1,9},{9,1},{17,25},{25,17},{2,10},{10... | collective-permute-start | bytes 1572872 | tf_op jit(solution)/shard_map/ppermute | solution.py:240
  34.7 7.0 %collective-permute-start.3 = (bf16[128,1024]{1,0:T(8,128)(2,1)S(1)}, bf16[128,1024]{1,0:T(8,128)(2,1)S(1)}, u32[]{:S(2)}, u32[]{:S(2)}) collective-permute-start(bf16[128,1024]{1,0:T(8,128)(2,1)S(1)} %get-tuple-element.78), channel_id=1, source_target_pairs={{0,8},{8,0},{16,24},{24,16},{1,9},{9,1},{17,25},{25,17},{2,10},{10... | collective-permute-start | bytes 786440 | tf_op jit(solution)/shard_map/ppermute | solution.py:240
  36.6 7.1 %collective-permute-start.6 = (bf16[128,1024]{1,0:T(8,128)(2,1)S(1)}, bf16[128,1024]{1,0:T(8,128)(2,1)S(1)}, u32[]{:S(2)}, u32[]{:S(2)}) collective-permute-start(bf16[128,1024]{1,0:T(8,128)(2,1)S(1)} %get-tuple-element.82), channel_id=1, source_target_pairs={{0,16},{8,24},{16,0},{24,8},{1,17},{9,25},{17,1},{25,9},{2,18},{10... | collective-permute-start | bytes 786440 | tf_op jit(solution)/shard_map/ppermute | solution.py:240
  41.7 16.8 %collective-permute-start.10 = (bf16[256,1024]{1,0:T(8,128)(2,1)S(1)}, bf16[256,1024]{1,0:T(8,128)(2,1)S(1)}, u32[]{:S(2)}, u32[]{:S(2)}) collective-permute-start(bf16[256,1024]{1,0:T(8,128)(2,1)S(1)} %constant_dynamic-update-slice_fusion.4.refs_7_), channel_id=1, source_target_pairs={{0,16},{8,24},{16,0},{24,8},{1,17},{9,25},{17,1},{25,9},{2,18},{10... | collective-permute-start | bytes 1572872 | tf_op jit(solution)/shard_map/ppermute | solution.py:240
  43.8 15.4 %collective-permute-start.11 = (bf16[256,1024]{1,0:T(8,128)(2,1)S(1)}, bf16[256,1024]{1,0:T(8,128)(2,1)S(1)}, u32[]{:S(2)}, u32[]{:S(2)}) collective-permute-start(bf16[256,1024]{1,0:T(8,128)(2,1)S(1)} %constant_dynamic-update-slice_fusion.6.refs_9_), channel_id=1, source_target_pairs={{0,8},{8,0},{16,24},{24,16},{1,9},{9,1},{17,25},{25,17},{2,10},{10... | collective-permute-start | bytes 1572872 | tf_op jit(solution)/shard_map/ppermute | solution.py:240
  45.4 11.4 %collective-permute-start.13 = (bf16[32,4096]{1,0:T(8,128)(2,1)S(1)}, bf16[32,4096]{1,0:T(8,128)(2,1)S(1)}, u32[]{:S(2)}, u32[]{:S(2)}) collective-permute-start(bf16[32,4096]{1,0:T(8,128)(2,1)S(1)} %get-tuple-element.95), channel_id=1, source_target_pairs={{0,2},{1,3},{2,0},{3,1},{4,6},{5,7},{6,4},{7,5},{8,10},{9,11},{10,... | collective-permute-start | bytes 786440 | tf_op jit(solution)/shard_map/ppermute | solution.py:240
  45.5 18.2 %collective-permute-start.15 = (bf16[32,4096]{1,0:T(8,128)(2,1)S(1)}, bf16[32,4096]{1,0:T(8,128)(2,1)S(1)}, u32[]{:S(2)}, u32[]{:S(2)}) collective-permute-start(bf16[32,4096]{1,0:T(8,128)(2,1)S(1)} %get-tuple-element.101), channel_id=1, source_target_pairs={{0,4},{1,5},{2,6},{3,7},{4,0},{5,1},{6,2},{7,3},{8,12},{9,13},{10,... | collective-permute-start | bytes 786440 | tf_op jit(solution)/shard_map/ppermute | solution.py:240
  46.2 17.6 %collective-permute-start.17 = (bf16[32,4096]{1,0:T(8,128)(2,1)S(1)}, bf16[32,4096]{1,0:T(8,128)(2,1)S(1)}, u32[]{:S(2)}, u32[]{:S(2)}) collective-permute-start(bf16[32,4096]{1,0:T(8,128)(2,1)S(1)} %pad_maximum_fusion.8), channel_id=1, source_target_pairs={{0,6},{1,7},{2,4},{3,5},{4,2},{5,3},{6,0},{7,1},{8,14},{9,15},{10,... | collective-permute-start | bytes 786440 | tf_op jit(solution)/shard_map/ppermute | solution.py:240
  56.8 18.9 %collective-permute-start.20 = (bf16[264,1024]{1,0:T(8,128)(2,1)}, bf16[264,1024]{1,0:T(8,128)(2,1)S(1)}, u32[]{:S(2)}, u32[]{:S(2)}) collective-permute-start(bf16[264,1024]{1,0:T(8,128)(2,1)} %get-tuple-element.111), channel_id=1, source_target_pairs={{0,24},{8,16},{16,8},{24,0},{1,25},{9,17},{17,9},{25,1},{2,26},{10... | collective-permute-start | bytes 1622024 | tf_op jit(solution)/shard_map/ppermute | solution.py:240
  58.5 20.7 %collective-permute-start.21 = (bf16[264,1024]{1,0:T(8,128)(2,1)}, bf16[264,1024]{1,0:T(8,128)(2,1)S(1)}, u32[]{:S(2)}, u32[]{:S(2)}) collective-permute-start(bf16[264,1024]{1,0:T(8,128)(2,1)} %get-tuple-element.112), channel_id=1, source_target_pairs={{0,16},{8,24},{16,0},{24,8},{1,17},{9,25},{17,1},{25,9},{2,18},{10... | collective-permute-start | bytes 1622024 | tf_op jit(solution)/shard_map/ppermute | solution.py:240
  59.2 20.6 %collective-permute-start.22 = (bf16[264,1024]{1,0:T(8,128)(2,1)}, bf16[264,1024]{1,0:T(8,128)(2,1)S(1)}, u32[]{:S(2)}, u32[]{:S(2)}) collective-permute-start(bf16[264,1024]{1,0:T(8,128)(2,1)} %get-tuple-element.113), channel_id=1, source_target_pairs={{0,8},{8,0},{16,24},{24,16},{1,9},{9,1},{17,25},{25,17},{2,10},{10... | collective-permute-start | bytes 1622024 | tf_op jit(solution)/shard_map/ppermute | solution.py:240
  63.8 23.9 %collective-permute-start.14 = (bf16[32,4096]{1,0:T(8,128)(2,1)}, bf16[32,4096]{1,0:T(8,128)(2,1)S(1)}, u32[]{:S(2)}, u32[]{:S(2)}) collective-permute-start(bf16[32,4096]{1,0:T(8,128)(2,1)} %get-tuple-element.96), channel_id=1, source_target_pairs={{0,2},{1,3},{2,0},{3,1},{4,6},{5,7},{6,4},{7,5},{8,10},{9,11},{10,... | collective-permute-start | bytes 786440 | tf_op jit(solution)/shard_map/ppermute | solution.py:240
  63.8 26.1 %collective-permute-start.16 = (bf16[32,4096]{1,0:T(8,128)(2,1)}, bf16[32,4096]{1,0:T(8,128)(2,1)S(1)}, u32[]{:S(2)}, u32[]{:S(2)}) collective-permute-start(bf16[32,4096]{1,0:T(8,128)(2,1)} %get-tuple-element.102), channel_id=1, source_target_pairs={{0,4},{1,5},{2,6},{3,7},{4,0},{5,1},{6,2},{7,3},{8,12},{9,13},{10,... | collective-permute-start | bytes 786440 | tf_op jit(solution)/shard_map/ppermute | solution.py:240
  75.8 8.3 %collective-permute-start.18 = (bf16[32,4096]{1,0:T(8,128)(2,1)S(1)}, bf16[32,4096]{1,0:T(8,128)(2,1)S(1)}, u32[]{:S(2)}, u32[]{:S(2)}) collective-permute-start(bf16[32,4096]{1,0:T(8,128)(2,1)S(1)} %copy-done.33), channel_id=1, source_target_pairs={{0,6},{1,7},{2,4},{3,5},{4,2},{5,3},{6,0},{7,1},{8,14},{9,15},{10,... | collective-permute-start | bytes 786440 | tf_op jit(solution)/shard_map/ppermute | solution.py:240
  79.2 34.1 %collective-permute-start.28 = (bf16[264,1024]{1,0:T(8,128)(2,1)}, bf16[264,1024]{1,0:T(8,128)(2,1)S(1)}, u32[]{:S(2)}, u32[]{:S(2)}) collective-permute-start(bf16[264,1024]{1,0:T(8,128)(2,1)} %get-tuple-element.128), channel_id=1, source_target_pairs={{0,8},{8,0},{16,24},{24,16},{1,9},{9,1},{17,25},{25,17},{2,10},{10... | collective-permute-start | bytes 1622024 | tf_op jit(solution)/shard_map/ppermute | solution.py:240
  79.8 33.5 %collective-permute-start.27 = (bf16[264,1024]{1,0:T(8,128)(2,1)}, bf16[264,1024]{1,0:T(8,128)(2,1)S(1)}, u32[]{:S(2)}, u32[]{:S(2)}) collective-permute-start(bf16[264,1024]{1,0:T(8,128)(2,1)} %get-tuple-element.127), channel_id=1, source_target_pairs={{0,16},{8,24},{16,0},{24,8},{1,17},{9,25},{17,1},{25,9},{2,18},{10... | collective-permute-start | bytes 1622024 | tf_op jit(solution)/shard_map/ppermute | solution.py:240
  84.1 14.2 %collective-permute-start.25 = (bf16[32,4096]{1,0:T(8,128)(2,1)S(1)}, bf16[32,4096]{1,0:T(8,128)(2,1)S(1)}, u32[]{:S(2)}, u32[]{:S(2)}) collective-permute-start(bf16[32,4096]{1,0:T(8,128)(2,1)S(1)} %copy-done.38), channel_id=1, source_target_pairs={{0,6},{1,7},{2,4},{3,5},{4,2},{5,3},{6,0},{7,1},{8,14},{9,15},{10,... | collective-permute-start | bytes 786440 | tf_op jit(solution)/shard_map/ppermute | solution.py:240
  87.7 25.4 %copy-start.15 = (bf16[32,4096]{1,0:T(8,128)(2,1)}, bf16[32,4096]{1,0:T(8,128)(2,1)S(1)}, u32[]{:S(2)}) copy-start(bf16[32,4096]{1,0:T(8,128)(2,1)S(1)} %collective-permute-done.14.refs_3_) | copy-start | bytes 786436
  87.7 25.5 %collective-permute-start.26 = (bf16[264,1024]{1,0:T(8,128)(2,1)S(1)}, bf16[264,1024]{1,0:T(8,128)(2,1)S(1)}, u32[]{:S(2)}, u32[]{:S(2)}) collective-permute-start(bf16[264,1024]{1,0:T(8,128)(2,1)S(1)} %copy-done.23), channel_id=1, source_target_pairs={{0,24},{8,16},{16,8},{24,0},{1,25},{9,17},{17,9},{25,1},{2,26},{10... | collective-permute-start | bytes 1622024 | tf_op jit(solution)/shard_map/ppermute | solution.py:240
  89.9 23.2 %copy-start.16 = (bf16[32,4096]{1,0:T(8,128)(2,1)}, bf16[32,4096]{1,0:T(8,128)(2,1)S(1)}, u32[]{:S(2)}) copy-start(bf16[32,4096]{1,0:T(8,128)(2,1)S(1)} %collective-permute-done.16.refs_4_) | copy-start | bytes 786436
  89.9 23.2 %collective-permute-start.23 = (bf16[32,4096]{1,0:T(8,128)(2,1)S(1)}, bf16[32,4096]{1,0:T(8,128)(2,1)S(1)}, u32[]{:S(2)}, u32[]{:S(2)}) collective-permute-start(bf16[32,4096]{1,0:T(8,128)(2,1)S(1)} %copy-done.34), channel_id=1, source_target_pairs={{0,2},{1,3},{2,0},{3,1},{4,6},{5,7},{6,4},{7,5},{8,10},{9,11},{10,... | collective-permute-start | bytes 786440 | tf_op jit(solution)/shard_map/ppermute | solution.py:240
  98.3 14.9 %collective-permute-start.24 = (bf16[32,4096]{1,0:T(8,128)(2,1)S(1)}, bf16[32,4096]{1,0:T(8,128)(2,1)S(1)}, u32[]{:S(2)}, u32[]{:S(2)}) collective-permute-start(bf16[32,4096]{1,0:T(8,128)(2,1)S(1)} %copy-done.35), channel_id=1, source_target_pairs={{0,4},{1,5},{2,6},{3,7},{4,0},{5,1},{6,2},{7,3},{8,12},{9,13},{10,... | collective-permute-start | bytes 786440 | tf_op jit(solution)/shard_map/ppermute | solution.py:240
  113.1 5.0 %collective-permute-start.19 = (bf16[64,4096]{1,0:T(8,128)(2,1)S(1)}, bf16[64,4096]{1,0:T(8,128)(2,1)S(1)}, u32[]{:S(2)}, u32[]{:S(2)}) collective-permute-start(bf16[64,4096]{1,0:T(8,128)(2,1)S(1)} %pad_maximum_fusion.1), channel_id=1, source_target_pairs={{0,1},{1,0},{2,3},{3,2},{4,5},{5,4},{6,7},{7,6},{8,9},{9,8},{10,11... | collective-permute-start | bytes 1572872 | tf_op jit(solution)/shard_map/ppermute | solution.py:240
  114.3 3.8 %collective-permute-start.29 = (bf16[64,4096]{1,0:T(8,128)(2,1)S(1)}, bf16[64,4096]{1,0:T(8,128)(2,1)S(1)}, u32[]{:S(2)}, u32[]{:S(2)}) collective-permute-start(bf16[64,4096]{1,0:T(8,128)(2,1)S(1)} %pad_maximum_fusion.2), channel_id=1, source_target_pairs={{0,1},{1,0},{2,3},{3,2},{4,5},{5,4},{6,7},{7,6},{8,9},{9,8},{10,11... | collective-permute-start | bytes 1572872 | tf_op jit(solution)/shard_map/ppermute | solution.py:240
  (38 other events, 343.7 us)

commit v3 on v2

--- a/solution.py
+++ b/solution.py
@@ -60,8 +60,7 @@
         lane = lax.broadcasted_iota(jnp.int32, (1, slots), 1)
         piece = lane // ROWS
         within = lane % ROWS
-        far = devs // 2
-        relative = jnp.where(piece < far, 2 * piece, 2 * (piece - far) + 1)
+        relative = piece
         is_frame = within // (CHUNK * CAP) == 0
         wanted = ((me ^ relative) * chunks + chunk) * (CHUNK * CAP) + within % (CHUNK * CAP)
         one = lambda mask: jnp.where(mask, 1.0, 0.0).astype(BF16)
@@ -74,9 +73,8 @@
         table_ref[0:toks] = frame_first
         table_ref[toks : 2 * toks] = frame_second
         table_ref[2 * toks : 3 * toks] = cotan_first + cotan_second
-        select_ref[0:toks] = frame_first + frame_second
-        select_ref[toks : 2 * toks] = cotan_first
-        select_ref[2 * toks : 3 * toks] = cotan_second
+        select = jnp.concatenate([frame_first + frame_second, cotan_first, cotan_second], axis=0)
+        select_ref[...] = select.astype(F32).T.astype(BF16)
 
     weight_first = column(weights_ref[0:1, :])
     weight_second = column(weights_ref[1:2, :])
@@ -92,12 +90,17 @@
             ],
             axis=0,
         )
-        placed = dot(select_ref[...], stacked, ((0,), (0,)))
-        begin_row = 0
-        for ref in pieces:
-            rows = ref.shape[0]
-            ref[:, lanes] = placed[begin_row : begin_row + rows].astype(BF16)
-            begin_row += rows
+        placed = dot(select_ref[...], stacked)
+        if chunk < NEAR_SWAPS:
+            for r, ref in enumerate(pieces):
+                ref[:, lanes] = placed[2 * r * ROWS : 2 * (r + 1) * ROWS].astype(BF16)
+        else:
+            for r, ref in enumerate(pieces[:-1]):
+                begin_row = 2 * r * ROWS
+                ref[:, lanes] = placed[begin_row : begin_row + ROWS].astype(BF16)
+                pieces[-1][r * ROWS : (r + 1) * ROWS, lanes] = placed[
+                    begin_row + ROWS : begin_row + 2 * ROWS
+                ].astype(BF16)
 
 
 def sorting(devs, side):
@@ -117,17 +120,17 @@
     return bits if expert % 2 == 0 else bits[::-1]
 
 
-def chunk_kernel(devs, held, chunk, *refs):
+def chunk_kernel(devs, held, chunk, parts, *refs):
     me_ref, filter_ref = refs[0], refs[1]
     refs = refs[2:]
     far = devs // 2
-    (own_ref, swapped_ref, *far_refs), refs = refs[: far + 1], refs[far + 1 :]
+    pieces, refs = refs[: far + 1], refs[far + 1 :]
     weight_refs, refs = refs[: len(held)], refs[len(held) :]
     backs, refs = refs[:far], refs[far:]
     shards_n = sum(map(len, held)) // CHUNK
     reduce_refs, refs = refs[:shards_n], refs[shards_n:]
     matrix, rows_f32, hidden, preact, dpre, dhidden, grad, results = refs
-    width = own_ref.shape[1]
+    width = pieces[0].shape[1]
     channels = matrix.shape[1]
     bins = width // channels
     block = devs * CAP
@@ -141,7 +144,7 @@
     sort = sorting(devs, 0)
     for p in range(bins):
         lanes = slice(p * channels, (p + 1) * channels)
-        stacked = [ref[:, lanes] for ref in (own_ref, swapped_ref, *far_refs)]
+        stacked = [pieces[i][begin : begin + rows, lanes] for i, begin, rows in parts]
         rows_f32[:, lanes] = dot(sort, jnp.concatenate(stacked, axis=0))
 
     for expert in range(CHUNK):
@@ -202,17 +205,19 @@
 def combine_kernel(chunks, weights_ref, *refs):
     tables, pieces, (mixed_ref, grads_ref) = refs[:chunks], refs[chunks:-2], refs[-2:]
     each = len(pieces) // chunks
+    table = jnp.concatenate([ref[...] for ref in tables], axis=1)
     toks, width = mixed_ref.shape
     weight_first = column(weights_ref[0:1, :])
     weight_second = column(weights_ref[1:2, :])
     step = min(512, width)
     for begin in range(0, width, step):
         lanes = slice(begin, begin + step)
-        placed = None
-        for index, table_ref in enumerate(tables):
-            stacked = [ref[:, lanes] for ref in pieces[index * each : (index + 1) * each]]
-            part = dot(table_ref[...], jnp.concatenate(stacked, axis=0))
-            placed = part if placed is None else placed + part
+        stacked = []
+        for index in range(chunks):
+            *near, swapped = pieces[index * each : (index + 1) * each]
+            for r, ref in enumerate(near):
+                stacked += [ref[:, lanes], swapped[r * ROWS : (r + 1) * ROWS, lanes]]
+        placed = dot(table, jnp.concatenate(stacked, axis=0))
         mixed_ref[:, lanes] = (
             weight_first * placed[0:toks] + weight_second * placed[toks : 2 * toks]
         ).astype(BF16)
@@ -224,7 +229,12 @@
 COSTS = (2, 3, 2)
 LATE = 1
 PLANE = 2
-AG1_FIRST = True
+GATHER_AFTER = False
+NEAR_SWAPS = 1
+ORDER = lambda s: -s
+SUMS_AFTER = False
+WEIGHTS_AFTER = 0
+SWAP_AFTER = 2
 D1_AFTER = "gather0last"
 K_AFTER = ["gather1first", ""]
 R_AFTER = ['gather1last', 'sums0']
@@ -256,7 +266,7 @@
     block = devs * CAP
     total = devs * ROWS
     far = devs // 2
-    order = sorted(range(1, far), reverse=True)
+    order = sorted(range(1, far), key=ORDER)
     me = lax.axis_index("expert").astype(jnp.int32).reshape(1)
     me_dp = lax.axis_index("dp").astype(jnp.int32).reshape(1)
     routes = routes.T
@@ -265,18 +275,19 @@
     whole = lambda *shape: pl.BlockSpec(shape, lambda i: (0,) * len(shape))
     piece = jax.ShapeDtypeStruct((ROWS, width), BF16)
     tables, sent = [], []
+    pair = jax.ShapeDtypeStruct((2 * ROWS, width), BF16)
     for chunk in range(chunks):
+        if chunk < NEAR_SWAPS:
+            shapes = [pair] * far
+        else:
+            shapes = [piece] * far + [jax.ShapeDtypeStruct((far * ROWS, width), BF16)]
         table, *pieces = pl.pallas_call(
             functools.partial(dispatch_kernel, devs, chunks, chunk),
             grid=(1,),
-            out_shape=[jax.ShapeDtypeStruct((3 * toks, total), BF16)]
-            + [piece] * far
-            + [jax.ShapeDtypeStruct((far * ROWS, width), BF16)],
+            out_shape=[jax.ShapeDtypeStruct((3 * toks, total), BF16)] + shapes,
             in_specs=[SMEM, whole(2, toks), whole(2, toks), whole(toks, width), whole(toks, width)],
-            out_specs=[whole(3 * toks, total)]
-            + [whole(ROWS, width)] * far
-            + [whole(far * ROWS, width)],
-            scratch_shapes=[pltpu.VMEM((3 * toks, total), BF16)],
+            out_specs=[whole(3 * toks, total)] + [whole(*value.shape) for value in shapes],
+            scratch_shapes=[pltpu.VMEM((total, 3 * toks), BF16)],
             compiler_params=params(),
             cost_estimate=cost(COSTS[0]),
             name="dispatch",
@@ -333,9 +344,19 @@
                 for (old, places), (other, more) in zip(held, new)
             ]
 
-    weights = jnp.transpose(after(point_weight, tables[0]), (1, 0, 2))
+    weights = jnp.transpose(after(point_weight, tables[WEIGHTS_AFTER]), (1, 0, 2))
     def dispatched(chunk):
+        if chunk < NEAR_SWAPS:
+            near = [sent[chunk][0]] + [
+                wait(value, D1_AFTER) if chunk > 0 else value for value in sent[chunk][1:]
+            ]
+            near = along_line(near)
+            value = jnp.concatenate([value[ROWS:] for value in near], axis=0)
+            parts = [p for r in range(far) for p in ((r, 0, ROWS), (far, r * ROWS, ROWS))]
+            return near + [flip(value, "expert", 1)], parts
         *own, relayed = sent[chunk]
+        if SWAP_AFTER is not None:
+            relayed = after(relayed, line[SWAP_AFTER])
         relayed = flip(relayed, "expert", 1)
         pairs = [
             jnp.concatenate([own[r], relayed[r * ROWS : (r + 1) * ROWS]], axis=0)
@@ -343,36 +364,36 @@
         ]
         if chunk > 0:
             pairs = [wait(value, D1_AFTER) for value in pairs]
-        return [own[0], relayed] + along_line([own[0]] + pairs)[1:]
+        parts = [(0, 0, ROWS), (1, 0, ROWS)] + [(r + 1, 0, 2 * ROWS) for r in range(1, far)]
+        return [own[0], relayed] + along_line([own[0]] + pairs)[1:], parts
 
     def weights_of(chunk, other):
         parts = [weights[chunk * CHUNK + expert] for expert in range(CHUNK)]
-        return gather([after(part, other) for part in parts], chunk)
+        return gather(parts if other is False else [after(part, other) for part in parts], chunk)
 
     arrived = [dispatched(0)]
-    gathered = [weights_of(0, arrived[0][1])]
+    gathered = [weights_of(0, GATHER_AFTER and flip(sent[1][-1], "expert", 1))]
     for chunk in range(1, chunks):
-        if AG1_FIRST:
-            gathered.append(weights_of(chunk, sent[chunk][-1]))
-            arrived.append(dispatched(chunk))
-        else:
-            arrived.append(dispatched(chunk))
-            gathered.append(weights_of(chunk, arrived[chunk][1]))
+        gathered.append(weights_of(chunk, sent[chunk][-1]))
+        arrived.append(dispatched(chunk))
     block_sum = jax.ShapeDtypeStruct((CHUNK * local + PAD, out_channels), BF16)
     backs = []
     reduced = []
     for chunk in range(chunks):
         full, held = zip(*gathered[chunk])
-        arrived[chunk][0] = wait(arrived[chunk][0], K_AFTER[chunk])
-        pair = jax.ShapeDtypeStruct((2 * ROWS, width), BF16)
+        came, parts = arrived[chunk]
+        came[0] = wait(came[0], K_AFTER[chunk])
         outs = [pair] * far + [block_sum] * shards_n
         outs = pl.pallas_call(
-            functools.partial(chunk_kernel, devs, held, chunk),
+            functools.partial(chunk_kernel, devs, held, chunk, parts),
             out_shape=outs,
             grid=(1,),
             in_specs=[SMEM, whole(*depth_filter.shape)]
-            + [whole(ROWS, width)] * 2
-            + [whole(*value.shape) for value in (*arrived[chunk][2:], *full)],
+            + [
+                whole(max(begin + n for i, begin, n in parts if i == index), width)
+                for index in range(len(came))
+            ]
+            + [whole(*value.shape) for value in full],
             out_specs=[whole(*value.shape) for value in outs],
             scratch_shapes=[
                 pltpu.VMEM((CHUNK, channels, out_channels), BF16),
@@ -387,8 +408,10 @@
             compiler_params=params(),
             cost_estimate=cost(COSTS[1]),
             name="experts",
-        )(me_dp, depth_filter, *arrived[chunk], *full)
+        )(me_dp, depth_filter, *came, *full)
         results, to_reduce = list(outs[:far]), outs[far:]
+        if chunk + 1 < chunks and SUMS_AFTER:
+            to_reduce = [after(value, arrived[chunk + 1][0][-1]) for value in to_reduce]
         steps[f"sums{chunk}"] = [
             flip(to_reduce[r], "dp", r) for r in sorted(range(1, shards_n), reverse=True)
         ]

time: 123 us -> 121 us (0.984)
  starting transfers between devices: 61.3 us -> 57.4 us
  waiting for transfers between devices: 28.2 us -> 30 us
    ppermute x30, starting transfers between devices: 61.3 us -> 57.4 us  [flip(): lax.ppermute(value, axis, [(k, k ^ bits) for k in range(lax.axis_size(axi...]
    ppermute x30, waiting for transfers between devices: 28.2 us -> 30 us  [flip(): lax.ppermute(value, axis, [(k, k ^ bits) for k in range(lax.axis_size(axi...]
    unnamed x87 -> x85, local copies, waits for them, and re-layouts: 6.08 us -> 6.05 us
  transfers between devices with their start and end apart: 30 -> 30, of which waited for: 9 -> 9; matrix products, arithmetic and copies ran while one was open for 6% -> 5% of each run, Pallas kernels for 13% -> 14%
where the time goes in v3:
time: 121 us; the launch traced here: 120 us
  starting transfers between devices  57.4 us (47%)
  waiting for transfers between devices  30 us (25%)
  Pallas kernels  22.8 us (19%)
  local copies, waits for them, and re-layouts  7.66 us (6%)
  between operations  1.36 us (1%)
    ppermute x30, starting transfers between devices, flip(): lax.ppermute(value, axis, [(k, k ^ bits) for k in range(lax.axis_size(axi...  57.4 us
    ppermute x30, waiting for transfers between devices, flip(): lax.ppermute(value, axis, [(k, k ^ bits) for k in range(lax.axis_size(axi...  30 us
    pallas_call x2, Pallas kernels, shards(): pl.pallas_call(functools.partial(chunk_kernel, devs, held, chunk, parts),...  13.5 us
    pallas_call x2, Pallas kernels, shards(): pl.pallas_call(functools.partial(dispatch_kernel, devs, chunks, chunk), g...  6.06 us
    unnamed x85, local copies, waits for them, and re-layouts  6.05 us
    pallas_call x1, Pallas kernels, shards(): pl.pallas_call(functools.partial(combine_kernel, chunks), grid=(1,), out_...  3.16 us
  transfers between devices with their start and end apart: 30, of which 9 were waited for; matrix products, arithmetic and copies ran while one was open for 5% of the time, Pallas kernels for 14%

profile of v3, /device:TPU:0, one launch (start us, length us, event | category | flops | bytes accessed | tf_op | source)
XLA Modules:
  0.0 120.4 jit_solution(7416908705243130936)
XLA Ops:
  0.6 3.1 %dispatch.2 = (bf16[192,128]{1,0:T(8,128)(2,1)}, bf16[32,4096]{1,0:T(8,128)(2,1)}, bf16[32,4096]{1,0:T(8,128)(2,1)}, bf16[32,4096]{1,0:T(8,128)(2,1)}, bf16[32,4096]{1,0:T(8,128)(2,1)}) custom-call(s32[1]{0:T(128)} %bitcast.1.me_ref, s32[2,64]{1,0:T(2,128)} %bitcast.32, f32[2,64]{1,0:T(2,128)} %bitcast.34, bf16[64,4096]{1,0:T(8,128)(2,1)} %tokens_ref.3, ...), custom_call_target="tpu_custom_call" | custom-call | flops 2000000000 | bytes 8388608 | tf_op jit(solution)/shard_map/dispatch/pallas_call | solution.py:284
  4.1 3.0 %collective-permute-start = (bf16[128,1024]{1,0:T(8,128)(2,1)S(1)}, bf16[128,1024]{1,0:T(8,128)(2,1)S(1)}, u32[]{:S(2)}, u32[]{:S(2)}) collective-permute-start(bf16[128,1024]{1,0:T(8,128)(2,1)S(1)} %get-tuple-element.144), channel_id=1, source_target_pairs={{0,8},{8,0},{16,24},{24,16},{1,9},{9,1},{17,25},{25,17},{2,10},{10... | collective-permute-start | bytes 786440 | tf_op jit(solution)/shard_map/ppermute | solution.py:250
  7.1 1.5 %collective-permute-start.3 = (bf16[128,1024]{1,0:T(8,128)(2,1)S(1)}, bf16[128,1024]{1,0:T(8,128)(2,1)S(1)}, u32[]{:S(2)}, u32[]{:S(2)}) collective-permute-start(bf16[128,1024]{1,0:T(8,128)(2,1)S(1)} %get-tuple-element.142), channel_id=1, source_target_pairs={{0,16},{8,24},{16,0},{24,8},{1,17},{9,25},{17,1},{25,9},{2,18},{10... | collective-permute-start | bytes 786440 | tf_op jit(solution)/shard_map/ppermute | solution.py:250
  8.7 1.6 %collective-permute-start.6 = (bf16[32,4096]{1,0:T(8,128)(2,1)}, bf16[32,4096]{1,0:T(8,128)(2,1)S(1)}, u32[]{:S(2)}, u32[]{:S(2)}) collective-permute-start(bf16[32,4096]{1,0:T(8,128)(2,1)} %get-tuple-element.79), channel_id=1, source_target_pairs={{0,2},{1,3},{2,0},{3,1},{4,6},{5,7},{6,4},{7,5},{8,10},{9,11},{10,... | collective-permute-start | bytes 786440 | tf_op jit(solution)/shard_map/ppermute | solution.py:250
  10.2 2.6 %collective-permute-start.7 = (bf16[32,4096]{1,0:T(8,128)(2,1)S(1)}, bf16[32,4096]{1,0:T(8,128)(2,1)S(1)}, u32[]{:S(2)}, u32[]{:S(2)}) collective-permute-start(bf16[32,4096]{1,0:T(8,128)(2,1)S(1)} %copy-done.37), channel_id=1, source_target_pairs={{0,4},{1,5},{2,6},{3,7},{4,0},{5,1},{6,2},{7,3},{8,12},{9,13},{10,... | collective-permute-start | bytes 786440 | tf_op jit(solution)/shard_map/ppermute | solution.py:250
  13.1 3.0 %dispatch.3 = (bf16[192,128]{1,0:T(8,128)(2,1)}, bf16[16,4096]{1,0:T(8,128)(2,1)}, bf16[16,4096]{1,0:T(8,128)(2,1)}, bf16[16,4096]{1,0:T(8,128)(2,1)}, bf16[16,4...) custom-call(s32[1]{0:T(128)} %bitcast.1.me_ref, s32[2,64]{1,0:T(2,128)} %bitcast.33, f32[2,64]{1,0:T(2,128)} %bitcast.35, ...), custom_call_target="tpu_custom_call" | custom-call | flops 2000000000 | bytes 8388608 | tf_op jit(solution)/shard_map/dispatch/pallas_call | solution.py:284
  17.9 3.1 %collective-permute-done.6.refs_3_ = bf16[32,4096]{1,0:T(8,128)(2,1)S(1)} collective-permute-done((bf16[32,4096]{1,0:T(8,128)(2,1)}, bf16[32,4096]{1,0:T(8,128)(2,1)S(1)}, u32[]{:S(2)}, u32[]{:S(2)}) %collective-permute-start.6) | collective-permute-done | bytes 262176 | tf_op jit(solution)/shard_map/ppermute | solution.py:250
  21.1 8.6 %collective-permute-done.8.refs_5_ = bf16[32,4096]{1,0:T(8,128)(2,1)S(1)} collective-permute-done((bf16[32,4096]{1,0:T(8,128)(2,1)}, bf16[32,4096]{1,0:T(8,128)(2,1)S(1)}, u32[]{:S(2)}, u32[]{:S(2)}) %collective-permute-start.8) | collective-permute-done | bytes 262176 | tf_op jit(solution)/shard_map/ppermute | solution.py:250
  29.8 1.9 %collective-permute-done.7.refs_4_ = bf16[32,4096]{1,0:T(8,128)(2,1)S(1)} collective-permute-done((bf16[32,4096]{1,0:T(8,128)(2,1)S(1)}, bf16[32,4096]{1,0:T(8,128)(2,1)S(1)}, u32[]{:S(2)}, u32[]{:S(2)}) %collective-permute-start.7) | collective-permute-done | bytes 262176 | tf_op jit(solution)/shard_map/ppermute | solution.py:250
  33.0 4.3 %collective-permute-start.13 = (bf16[32,4096]{1,0:T(8,128)(2,1)S(1)}, bf16[32,4096]{1,0:T(8,128)(2,1)S(1)}, u32[]{:S(2)}, u32[]{:S(2)}) collective-permute-start(bf16[32,4096]{1,0:T(8,128)(2,1)S(1)} %get-tuple-element.91), channel_id=1, source_target_pairs={{0,2},{1,3},{2,0},{3,1},{4,6},{5,7},{6,4},{7,5},{8,10},{9,11},{10,... | collective-permute-start | bytes 786440 | tf_op jit(solution)/shard_map/ppermute | solution.py:250
  37.4 1.2 %collective-permute-start.15 = (bf16[32,4096]{1,0:T(8,128)(2,1)S(1)}, bf16[32,4096]{1,0:T(8,128)(2,1)S(1)}, u32[]{:S(2)}, u32[]{:S(2)}) collective-permute-start(bf16[32,4096]{1,0:T(8,128)(2,1)S(1)} %get-tuple-element.97), channel_id=1, source_target_pairs={{0,4},{1,5},{2,6},{3,7},{4,0},{5,1},{6,2},{7,3},{8,12},{9,13},{10,... | collective-permute-start | bytes 786440 | tf_op jit(solution)/shard_map/ppermute | solution.py:250
  38.6 1.9 %collective-permute-done.2 = bf16[128,1024]{1,0:T(8,128)(2,1)S(1)} collective-permute-done((bf16[128,1024]{1,0:T(8,128)(2,1)S(1)}, bf16[128,1024]{1,0:T(8,128)(2,1)S(1)}, u32[]{:S(2)}, u32[]{:S(2)}) %collective-permute-start.2) | collective-permute-done | bytes 262176 | tf_op jit(solution)/shard_map/ppermute | solution.py:250
  41.2 1.2 collective-permute-start.11
  42.4 2.5 %collective-permute-start.17 = (bf16[32,4096]{1,0:T(8,128)(2,1)S(1)}, bf16[32,4096]{1,0:T(8,128)(2,1)S(1)}, u32[]{:S(2)}, u32[]{:S(2)}) collective-permute-start(bf16[32,4096]{1,0:T(8,128)(2,1)S(1)} %pad_maximum_fusion.8), channel_id=1, source_target_pairs={{0,6},{1,7},{2,4},{3,5},{4,2},{5,3},{6,0},{7,1},{8,14},{9,15},{10,... | collective-permute-start | bytes 786440 | tf_op jit(solution)/shard_map/ppermute | solution.py:250
  45.0 6.7 %experts.2 = (bf16[32,4096]{1,0:T(8,128)(2,1)}, bf16[32,4096]{1,0:T(8,128)(2,1)}, bf16[32,4096]{1,0:T(8,128)(2,1)}, bf16[32,4096]{1,0:T(8,128)(2,1)}, bf16[264,1...) custom-call(s32[1]{0:T(128)} %bitcast.3.refs_0_, ...), custom_call_target="tpu_custom_call" | custom-call | flops 3000000000 | bytes 8388608 | tf_op jit(solution)/shard_map/experts/pallas_call | solution.py:387
  51.7 1.9 %collective-permute-start.20 = (bf16[264,1024]{1,0:T(8,128)(2,1)}, bf16[264,1024]{1,0:T(8,128)(2,1)S(1)}, u32[]{:S(2)}, u32[]{:S(2)}) collective-permute-start(bf16[264,1024]{1,0:T(8,128)(2,1)} %get-tuple-element.107), channel_id=1, source_target_pairs={{0,24},{8,16},{16,8},{24,0},{1,25},{9,17},{17,9},{25,1},{2,26},{10... | collective-permute-start | bytes 1622024 | tf_op jit(solution)/shard_map/ppermute | solution.py:250
  55.8 5.2 %collective-permute-start.14 = (bf16[32,4096]{1,0:T(8,128)(2,1)}, bf16[32,4096]{1,0:T(8,128)(2,1)S(1)}, u32[]{:S(2)}, u32[]{:S(2)}) collective-permute-start(bf16[32,4096]{1,0:T(8,128)(2,1)} %get-tuple-element.92), channel_id=1, source_target_pairs={{0,2},{1,3},{2,0},{3,1},{4,6},{5,7},{6,4},{7,5},{8,10},{9,11},{10,... | collective-permute-start | bytes 786440 | tf_op jit(solution)/shard_map/ppermute | solution.py:250
  60.9 3.8 %collective-permute-start.16 = (bf16[32,4096]{1,0:T(8,128)(2,1)}, bf16[32,4096]{1,0:T(8,128)(2,1)S(1)}, u32[]{:S(2)}, u32[]{:S(2)}) collective-permute-start(bf16[32,4096]{1,0:T(8,128)(2,1)} %get-tuple-element.98), channel_id=1, source_target_pairs={{0,4},{1,5},{2,6},{3,7},{4,0},{5,1},{6,2},{7,3},{8,12},{9,13},{10,... | collective-permute-start | bytes 786440 | tf_op jit(solution)/shard_map/ppermute | solution.py:250
  64.7 0.9 slice.92
  65.7 6.9 %experts.3 = (bf16[32,4096]{1,0:T(8,128)(2,1)}, bf16[32,4096]{1,0:T(8,128)(2,1)}, bf16[32,4096]{1,0:T(8,128)(2,1)}, bf16[32,4096]{1,0:T(8,128)(2,1)}, bf16[264,1...) custom-call(s32[1]{0:T(128)} %bitcast.3.refs_0_, ...), custom_call_target="tpu_custom_call" | custom-call | flops 3000000000 | bytes 8388608 | tf_op jit(solution)/shard_map/experts/pallas_call | solution.py:387
  72.6 1.3 %collective-permute-start.18 = (bf16[32,4096]{1,0:T(8,128)(2,1)S(1)}, bf16[32,4096]{1,0:T(8,128)(2,1)S(1)}, u32[]{:S(2)}, u32[]{:S(2)}) collective-permute-start(bf16[32,4096]{1,0:T(8,128)(2,1)S(1)} %copy-done.34), channel_id=1, source_target_pairs={{0,6},{1,7},{2,4},{3,5},{4,2},{5,3},{6,0},{7,1},{8,14},{9,15},{10,... | collective-permute-start | bytes 786440 | tf_op jit(solution)/shard_map/ppermute | solution.py:250
  73.8 4.3 %collective-permute-done.21 = bf16[264,1024]{1,0:T(8,128)(2,1)S(1)} collective-permute-done((bf16[264,1024]{1,0:T(8,128)(2,1)}, bf16[264,1024]{1,0:T(8,128)(2,1)S(1)}, u32[]{:S(2)}, u32[]{:S(2)}) %collective-permute-start.21) | collective-permute-done | bytes 540704 | tf_op jit(solution)/shard_map/ppermute | solution.py:250
  78.1 0.7 collective-permute-start.28
  78.9 1.0 collective-permute-start.27
  81.2 2.5 %collective-permute-start.25 = (bf16[32,4096]{1,0:T(8,128)(2,1)S(1)}, bf16[32,4096]{1,0:T(8,128)(2,1)S(1)}, u32[]{:S(2)}, u32[]{:S(2)}) collective-permute-start(bf16[32,4096]{1,0:T(8,128)(2,1)S(1)} %copy-done.38), channel_id=1, source_target_pairs={{0,6},{1,7},{2,4},{3,5},{4,2},{5,3},{6,0},{7,1},{8,14},{9,15},{10,... | collective-permute-start | bytes 786440 | tf_op jit(solution)/shard_map/ppermute | solution.py:250
  83.8 2.5 %collective-permute-start.26 = (bf16[264,1024]{1,0:T(8,128)(2,1)S(1)}, bf16[264,1024]{1,0:T(8,128)(2,1)S(1)}, u32[]{:S(2)}, u32[]{:S(2)}) collective-permute-start(bf16[264,1024]{1,0:T(8,128)(2,1)S(1)} %copy-done.23), channel_id=1, source_target_pairs={{0,24},{8,16},{16,8},{24,0},{1,25},{9,17},{17,9},{25,1},{2,26},{10... | collective-permute-start | bytes 1622024 | tf_op jit(solution)/shard_map/ppermute | solution.py:250
  86.3 11.2 %collective-permute-start.23 = (bf16[32,4096]{1,0:T(8,128)(2,1)S(1)}, bf16[32,4096]{1,0:T(8,128)(2,1)S(1)}, u32[]{:S(2)}, u32[]{:S(2)}) collective-permute-start(bf16[32,4096]{1,0:T(8,128)(2,1)S(1)} %copy-done.35), channel_id=1, source_target_pairs={{0,2},{1,3},{2,0},{3,1},{4,6},{5,7},{6,4},{7,5},{8,10},{9,11},{10,... | collective-permute-start | bytes 786440 | tf_op jit(solution)/shard_map/ppermute | solution.py:250
  97.6 4.8 %collective-permute-start.24 = (bf16[32,4096]{1,0:T(8,128)(2,1)S(1)}, bf16[32,4096]{1,0:T(8,128)(2,1)S(1)}, u32[]{:S(2)}, u32[]{:S(2)}) collective-permute-start(bf16[32,4096]{1,0:T(8,128)(2,1)S(1)} %copy-done.36), channel_id=1, source_target_pairs={{0,4},{1,5},{2,6},{3,7},{4,0},{5,1},{6,2},{7,3},{8,12},{9,13},{10,... | collective-permute-start | bytes 786440 | tf_op jit(solution)/shard_map/ppermute | solution.py:250
  102.4 8.7 %collective-permute-done.24.refs_9_ = bf16[32,4096]{1,0:T(8,128)(2,1)S(1)} collective-permute-done((bf16[32,4096]{1,0:T(8,128)(2,1)S(1)}, bf16[32,4096]{1,0:T(8,128)(2,1)S(1)}, u32[]{:S(2)}, u32[]{:S(2)}) %collective-permute-start.24) | collective-permute-done | bytes 262176 | tf_op jit(solution)/shard_map/ppermute | solution.py:250
  112.9 2.7 %copy.13 = f32[128,4,1024]{2,1,0:T(4,128)} copy(f32[128,4,1024]{2,0,1:T(8,128)S(1)} %pad_maximum_fusion) | data formatting | bytes 4194304
  116.2 0.8 copy-done.30
  117.2 3.2 %combine.1 = (bf16[64,4096]{1,0:T(8,128)(2,1)}, bf16[64,4096]{1,0:T(8,128)(2,1)}) custom-call(f32[2,64]{1,0:T(2,128)} %bitcast.36, bf16[192,128]{1,0:T(8,128)(2,1)} %get-tuple-element.67.refs_0_, bf16[192,128]{1,0:T(8,128)(2,1)} %get-tuple-element.68.refs_1_, bf16[32,4096]{1,0:T(8,128)(2,1)} %get-tuple-element.85.refs_2_, bf16[32,4096]{1,0:T(8,128)(2,1)} %copy-done.11, ...), custom_call_target="tpu_custom_call" | custom-call | flops 2000000000 | bytes 8388608 | tf_op jit(solution)/shard_map/combine/pallas_call | solution.py:444
  (150 shorter events, 10.5 us)
Async XLA Ops:
  4.1 12.6 %collective-permute-start = (bf16[128,1024]{1,0:T(8,128)(2,1)S(1)}, bf16[128,1024]{1,0:T(8,128)(2,1)S(1)}, u32[]{:S(2)}, u32[]{:S(2)}) collective-permute-start(bf16[128,1024]{1,0:T(8,128)(2,1)S(1)} %get-tuple-element.144), channel_id=1, source_target_pairs={{0,8},{8,0},{16,24},{24,16},{1,9},{9,1},{17,25},{25,17},{2,10},{10... | collective-permute-start | bytes 786440 | tf_op jit(solution)/shard_map/ppermute | solution.py:250
  7.1 10.3 %collective-permute-start.3 = (bf16[128,1024]{1,0:T(8,128)(2,1)S(1)}, bf16[128,1024]{1,0:T(8,128)(2,1)S(1)}, u32[]{:S(2)}, u32[]{:S(2)}) collective-permute-start(bf16[128,1024]{1,0:T(8,128)(2,1)S(1)} %get-tuple-element.142), channel_id=1, source_target_pairs={{0,16},{8,24},{16,0},{24,8},{1,17},{9,25},{17,1},{25,9},{2,18},{10... | collective-permute-start | bytes 786440 | tf_op jit(solution)/shard_map/ppermute | solution.py:250
  8.7 12.4 %collective-permute-start.6 = (bf16[32,4096]{1,0:T(8,128)(2,1)}, bf16[32,4096]{1,0:T(8,128)(2,1)S(1)}, u32[]{:S(2)}, u32[]{:S(2)}) collective-permute-start(bf16[32,4096]{1,0:T(8,128)(2,1)} %get-tuple-element.79), channel_id=1, source_target_pairs={{0,2},{1,3},{2,0},{3,1},{4,6},{5,7},{6,4},{7,5},{8,10},{9,11},{10,... | collective-permute-start | bytes 786440 | tf_op jit(solution)/shard_map/ppermute | solution.py:250
  10.2 21.4 %collective-permute-start.7 = (bf16[32,4096]{1,0:T(8,128)(2,1)S(1)}, bf16[32,4096]{1,0:T(8,128)(2,1)S(1)}, u32[]{:S(2)}, u32[]{:S(2)}) collective-permute-start(bf16[32,4096]{1,0:T(8,128)(2,1)S(1)} %copy-done.37), channel_id=1, source_target_pairs={{0,4},{1,5},{2,6},{3,7},{4,0},{5,1},{6,2},{7,3},{8,12},{9,13},{10,... | collective-permute-start | bytes 786440 | tf_op jit(solution)/shard_map/ppermute | solution.py:250
  12.8 16.9 %collective-permute-start.8 = (bf16[32,4096]{1,0:T(8,128)(2,1)}, bf16[32,4096]{1,0:T(8,128)(2,1)S(1)}, u32[]{:S(2)}, u32[]{:S(2)}) collective-permute-start(bf16[32,4096]{1,0:T(8,128)(2,1)} %get-tuple-element.81), channel_id=1, source_target_pairs={{0,6},{1,7},{2,4},{3,5},{4,2},{5,3},{6,0},{7,1},{8,14},{9,15},{10,... | collective-permute-start | bytes 786440 | tf_op jit(solution)/shard_map/ppermute | solution.py:250
  16.8 15.0 %collective-permute-start.1 = (bf16[256,1024]{1,0:T(8,128)(2,1)S(1)}, bf16[256,1024]{1,0:T(8,128)(2,1)S(1)}, u32[]{:S(2)}, u32[]{:S(2)}) collective-permute-start(bf16[256,1024]{1,0:T(8,128)(2,1)S(1)} %pad_maximum_fusion.1.refs_7_), channel_id=1, source_target_pairs={{0,16},{8,24},{16,0},{24,8},{1,17},{9,25},{17,1},{25,9},{2,18},{10... | collective-permute-start | bytes 1572872 | tf_op jit(solution)/shard_map/ppermute | solution.py:250
  17.4 15.0 %collective-permute-start.4 = (bf16[256,1024]{1,0:T(8,128)(2,1)S(1)}, bf16[256,1024]{1,0:T(8,128)(2,1)S(1)}, u32[]{:S(2)}, u32[]{:S(2)}) collective-permute-start(bf16[256,1024]{1,0:T(8,128)(2,1)S(1)} %pad_maximum_fusion.2.refs_9_), channel_id=1, source_target_pairs={{0,8},{8,0},{16,24},{24,16},{1,9},{9,1},{17,25},{25,17},{2,10},{10... | collective-permute-start | bytes 1572872 | tf_op jit(solution)/shard_map/ppermute | solution.py:250
  21.0 11.9 %collective-permute-start.12 = (bf16[64,4096]{1,0:T(8,128)(2,1)S(1)}, bf16[64,4096]{1,0:T(8,128)(2,1)S(1)}, u32[]{:S(2)}, u32[]{:S(2)}) collective-permute-start(bf16[64,4096]{1,0:T(8,128)(2,1)S(1)} %copy-done.29), channel_id=1, source_target_pairs={{0,1},{1,0},{2,3},{3,2},{4,5},{5,4},{6,7},{7,6},{8,9},{9,8},{10,11... | collective-permute-start | bytes 1572872 | tf_op jit(solution)/shard_map/ppermute | solution.py:250
  31.7 10.7 %collective-permute-start.9 = (bf16[64,4096]{1,0:T(8,128)(2,1)S(1)}, bf16[64,4096]{1,0:T(8,128)(2,1)S(1)}, u32[]{:S(2)}, u32[]{:S(2)}) collective-permute-start(bf16[64,4096]{1,0:T(8,128)(2,1)S(1)} %pad_maximum_fusion.3), channel_id=1, source_target_pairs={{0,1},{1,0},{2,3},{3,2},{4,5},{5,4},{6,7},{7,6},{8,9},{9,8},{10,11... | collective-permute-start | bytes 1572872 | tf_op jit(solution)/shard_map/ppermute | solution.py:250
  31.8 8.7 %collective-permute-start.2 = (bf16[128,1024]{1,0:T(8,128)(2,1)S(1)}, bf16[128,1024]{1,0:T(8,128)(2,1)S(1)}, u32[]{:S(2)}, u32[]{:S(2)}) collective-permute-start(bf16[128,1024]{1,0:T(8,128)(2,1)S(1)} %get-tuple-element.74), channel_id=1, source_target_pairs={{0,8},{8,0},{16,24},{24,16},{1,9},{9,1},{17,25},{25,17},{2,10},{10... | collective-permute-start | bytes 786440 | tf_op jit(solution)/shard_map/ppermute | solution.py:250
  32.4 8.7 %collective-permute-start.5 = (bf16[128,1024]{1,0:T(8,128)(2,1)S(1)}, bf16[128,1024]{1,0:T(8,128)(2,1)S(1)}, u32[]{:S(2)}, u32[]{:S(2)}) collective-permute-start(bf16[128,1024]{1,0:T(8,128)(2,1)S(1)} %get-tuple-element.77), channel_id=1, source_target_pairs={{0,16},{8,24},{16,0},{24,8},{1,17},{9,25},{17,1},{25,9},{2,18},{10... | collective-permute-start | bytes 786440 | tf_op jit(solution)/shard_map/ppermute | solution.py:250
  33.0 18.6 %collective-permute-start.13 = (bf16[32,4096]{1,0:T(8,128)(2,1)S(1)}, bf16[32,4096]{1,0:T(8,128)(2,1)S(1)}, u32[]{:S(2)}, u32[]{:S(2)}) collective-permute-start(bf16[32,4096]{1,0:T(8,128)(2,1)S(1)} %get-tuple-element.91), channel_id=1, source_target_pairs={{0,2},{1,3},{2,0},{3,1},{4,6},{5,7},{6,4},{7,5},{8,10},{9,11},{10,... | collective-permute-start | bytes 786440 | tf_op jit(solution)/shard_map/ppermute | solution.py:250
  37.4 18.4 %collective-permute-start.15 = (bf16[32,4096]{1,0:T(8,128)(2,1)S(1)}, bf16[32,4096]{1,0:T(8,128)(2,1)S(1)}, u32[]{:S(2)}, u32[]{:S(2)}) collective-permute-start(bf16[32,4096]{1,0:T(8,128)(2,1)S(1)} %get-tuple-element.97), channel_id=1, source_target_pairs={{0,4},{1,5},{2,6},{3,7},{4,0},{5,1},{6,2},{7,3},{8,12},{9,13},{10,... | collective-permute-start | bytes 786440 | tf_op jit(solution)/shard_map/ppermute | solution.py:250
  40.6 13.5 %collective-permute-start.10 = (bf16[256,1024]{1,0:T(8,128)(2,1)S(1)}, bf16[256,1024]{1,0:T(8,128)(2,1)S(1)}, u32[]{:S(2)}, u32[]{:S(2)}) collective-permute-start(bf16[256,1024]{1,0:T(8,128)(2,1)S(1)} %constant_dynamic-update-slice_fusion.refs_7_), channel_id=1, source_target_pairs={{0,16},{8,24},{16,0},{24,8},{1,17},{9,25},{17,1},{25,9},{2,18},{10... | collective-permute-start | bytes 1572872 | tf_op jit(solution)/shard_map/ppermute | solution.py:250
  41.2 13.9 %collective-permute-start.11 = (bf16[256,1024]{1,0:T(8,128)(2,1)S(1)}, bf16[256,1024]{1,0:T(8,128)(2,1)S(1)}, u32[]{:S(2)}, u32[]{:S(2)}) collective-permute-start(bf16[256,1024]{1,0:T(8,128)(2,1)S(1)} %constant_dynamic-update-slice_fusion.2.refs_9_), channel_id=1, source_target_pairs={{0,8},{8,0},{16,24},{24,16},{1,9},{9,1},{17,25},{25,17},{2,10},{10... | collective-permute-start | bytes 1572872 | tf_op jit(solution)/shard_map/ppermute | solution.py:250
  42.4 18.5 %collective-permute-start.17 = (bf16[32,4096]{1,0:T(8,128)(2,1)S(1)}, bf16[32,4096]{1,0:T(8,128)(2,1)S(1)}, u32[]{:S(2)}, u32[]{:S(2)}) collective-permute-start(bf16[32,4096]{1,0:T(8,128)(2,1)S(1)} %pad_maximum_fusion.8), channel_id=1, source_target_pairs={{0,6},{1,7},{2,4},{3,5},{4,2},{5,3},{6,0},{7,1},{8,14},{9,15},{10,... | collective-permute-start | bytes 786440 | tf_op jit(solution)/shard_map/ppermute | solution.py:250
  51.7 20.9 %collective-permute-start.20 = (bf16[264,1024]{1,0:T(8,128)(2,1)}, bf16[264,1024]{1,0:T(8,128)(2,1)S(1)}, u32[]{:S(2)}, u32[]{:S(2)}) collective-permute-start(bf16[264,1024]{1,0:T(8,128)(2,1)} %get-tuple-element.107), channel_id=1, source_target_pairs={{0,24},{8,16},{16,8},{24,0},{1,25},{9,17},{17,9},{25,1},{2,26},{10... | collective-permute-start | bytes 1622024 | tf_op jit(solution)/shard_map/ppermute | solution.py:250
  54.1 24.0 %collective-permute-start.21 = (bf16[264,1024]{1,0:T(8,128)(2,1)}, bf16[264,1024]{1,0:T(8,128)(2,1)S(1)}, u32[]{:S(2)}, u32[]{:S(2)}) collective-permute-start(bf16[264,1024]{1,0:T(8,128)(2,1)} %get-tuple-element.108), channel_id=1, source_target_pairs={{0,16},{8,24},{16,0},{24,8},{1,17},{9,25},{17,1},{25,9},{2,18},{10... | collective-permute-start | bytes 1622024 | tf_op jit(solution)/shard_map/ppermute | solution.py:250
  55.1 23.8 %collective-permute-start.22 = (bf16[264,1024]{1,0:T(8,128)(2,1)}, bf16[264,1024]{1,0:T(8,128)(2,1)S(1)}, u32[]{:S(2)}, u32[]{:S(2)}) collective-permute-start(bf16[264,1024]{1,0:T(8,128)(2,1)} %get-tuple-element.109), channel_id=1, source_target_pairs={{0,8},{8,0},{16,24},{24,16},{1,9},{9,1},{17,25},{25,17},{2,10},{10... | collective-permute-start | bytes 1622024 | tf_op jit(solution)/shard_map/ppermute | solution.py:250
  55.8 28.1 %collective-permute-start.14 = (bf16[32,4096]{1,0:T(8,128)(2,1)}, bf16[32,4096]{1,0:T(8,128)(2,1)S(1)}, u32[]{:S(2)}, u32[]{:S(2)}) collective-permute-start(bf16[32,4096]{1,0:T(8,128)(2,1)} %get-tuple-element.92), channel_id=1, source_target_pairs={{0,2},{1,3},{2,0},{3,1},{4,6},{5,7},{6,4},{7,5},{8,10},{9,11},{10,... | collective-permute-start | bytes 786440 | tf_op jit(solution)/shard_map/ppermute | solution.py:250
  60.9 25.4 %collective-permute-start.16 = (bf16[32,4096]{1,0:T(8,128)(2,1)}, bf16[32,4096]{1,0:T(8,128)(2,1)S(1)}, u32[]{:S(2)}, u32[]{:S(2)}) collective-permute-start(bf16[32,4096]{1,0:T(8,128)(2,1)} %get-tuple-element.98), channel_id=1, source_target_pairs={{0,4},{1,5},{2,6},{3,7},{4,0},{5,1},{6,2},{7,3},{8,12},{9,13},{10,... | collective-permute-start | bytes 786440 | tf_op jit(solution)/shard_map/ppermute | solution.py:250
  72.6 8.7 %collective-permute-start.18 = (bf16[32,4096]{1,0:T(8,128)(2,1)S(1)}, bf16[32,4096]{1,0:T(8,128)(2,1)S(1)}, u32[]{:S(2)}, u32[]{:S(2)}) collective-permute-start(bf16[32,4096]{1,0:T(8,128)(2,1)S(1)} %copy-done.34), channel_id=1, source_target_pairs={{0,6},{1,7},{2,4},{3,5},{4,2},{5,3},{6,0},{7,1},{8,14},{9,15},{10,... | collective-permute-start | bytes 786440 | tf_op jit(solution)/shard_map/ppermute | solution.py:250
  78.1 33.2 %collective-permute-start.28 = (bf16[264,1024]{1,0:T(8,128)(2,1)}, bf16[264,1024]{1,0:T(8,128)(2,1)S(1)}, u32[]{:S(2)}, u32[]{:S(2)}) collective-permute-start(bf16[264,1024]{1,0:T(8,128)(2,1)} %get-tuple-element.124), channel_id=1, source_target_pairs={{0,8},{8,0},{16,24},{24,16},{1,9},{9,1},{17,25},{25,17},{2,10},{10... | collective-permute-start | bytes 1622024 | tf_op jit(solution)/shard_map/ppermute | solution.py:250
  78.9 32.4 %collective-permute-start.27 = (bf16[264,1024]{1,0:T(8,128)(2,1)}, bf16[264,1024]{1,0:T(8,128)(2,1)S(1)}, u32[]{:S(2)}, u32[]{:S(2)}) collective-permute-start(bf16[264,1024]{1,0:T(8,128)(2,1)} %get-tuple-element.123), channel_id=1, source_target_pairs={{0,16},{8,24},{16,0},{24,8},{1,17},{9,25},{17,1},{25,9},{2,18},{10... | collective-permute-start | bytes 1622024 | tf_op jit(solution)/shard_map/ppermute | solution.py:250
  81.2 16.3 %collective-permute-start.25 = (bf16[32,4096]{1,0:T(8,128)(2,1)S(1)}, bf16[32,4096]{1,0:T(8,128)(2,1)S(1)}, u32[]{:S(2)}, u32[]{:S(2)}) collective-permute-start(bf16[32,4096]{1,0:T(8,128)(2,1)S(1)} %copy-done.38), channel_id=1, source_target_pairs={{0,6},{1,7},{2,4},{3,5},{4,2},{5,3},{6,0},{7,1},{8,14},{9,15},{10,... | collective-permute-start | bytes 786440 | tf_op jit(solution)/shard_map/ppermute | solution.py:250
  83.8 27.4 %copy-start.11 = (bf16[32,4096]{1,0:T(8,128)(2,1)}, bf16[32,4096]{1,0:T(8,128)(2,1)S(1)}, u32[]{:S(2)}) copy-start(bf16[32,4096]{1,0:T(8,128)(2,1)S(1)} %collective-permute-done.14.refs_3_) | copy-start | bytes 786436
  83.8 27.5 %collective-permute-start.26 = (bf16[264,1024]{1,0:T(8,128)(2,1)S(1)}, bf16[264,1024]{1,0:T(8,128)(2,1)S(1)}, u32[]{:S(2)}, u32[]{:S(2)}) collective-permute-start(bf16[264,1024]{1,0:T(8,128)(2,1)S(1)} %copy-done.23), channel_id=1, source_target_pairs={{0,24},{8,16},{16,8},{24,0},{1,25},{9,17},{17,9},{25,1},{2,26},{10... | collective-permute-start | bytes 1622024 | tf_op jit(solution)/shard_map/ppermute | solution.py:250
  86.3 24.9 %copy-start.12 = (bf16[32,4096]{1,0:T(8,128)(2,1)}, bf16[32,4096]{1,0:T(8,128)(2,1)S(1)}, u32[]{:S(2)}) copy-start(bf16[32,4096]{1,0:T(8,128)(2,1)S(1)} %collective-permute-done.16.refs_4_) | copy-start | bytes 786436
  86.3 24.9 %collective-permute-start.23 = (bf16[32,4096]{1,0:T(8,128)(2,1)S(1)}, bf16[32,4096]{1,0:T(8,128)(2,1)S(1)}, u32[]{:S(2)}, u32[]{:S(2)}) collective-permute-start(bf16[32,4096]{1,0:T(8,128)(2,1)S(1)} %copy-done.35), channel_id=1, source_target_pairs={{0,2},{1,3},{2,0},{3,1},{4,6},{5,7},{6,4},{7,5},{8,10},{9,11},{10,... | collective-permute-start | bytes 786440 | tf_op jit(solution)/shard_map/ppermute | solution.py:250
  97.6 13.6 %collective-permute-start.24 = (bf16[32,4096]{1,0:T(8,128)(2,1)S(1)}, bf16[32,4096]{1,0:T(8,128)(2,1)S(1)}, u32[]{:S(2)}, u32[]{:S(2)}) collective-permute-start(bf16[32,4096]{1,0:T(8,128)(2,1)S(1)} %copy-done.36), channel_id=1, source_target_pairs={{0,4},{1,5},{2,6},{3,7},{4,0},{5,1},{6,2},{7,3},{8,12},{9,13},{10,... | collective-permute-start | bytes 786440 | tf_op jit(solution)/shard_map/ppermute | solution.py:250
  111.2 5.0 %collective-permute-start.19 = (bf16[64,4096]{1,0:T(8,128)(2,1)S(1)}, bf16[64,4096]{1,0:T(8,128)(2,1)S(1)}, u32[]{:S(2)}, u32[]{:S(2)}) collective-permute-start(bf16[64,4096]{1,0:T(8,128)(2,1)S(1)} %pad_maximum_fusion.4), channel_id=1, source_target_pairs={{0,1},{1,0},{2,3},{3,2},{4,5},{5,4},{6,7},{7,6},{8,9},{9,8},{10,11... | collective-permute-start | bytes 1572872 | tf_op jit(solution)/shard_map/ppermute | solution.py:250
  112.4 3.8 %collective-permute-start.29 = (bf16[64,4096]{1,0:T(8,128)(2,1)S(1)}, bf16[64,4096]{1,0:T(8,128)(2,1)S(1)}, u32[]{:S(2)}, u32[]{:S(2)}) collective-permute-start(bf16[64,4096]{1,0:T(8,128)(2,1)S(1)} %pad_maximum_fusion.5), channel_id=1, source_target_pairs={{0,1},{1,0},{2,3},{3,2},{4,5},{5,4},{6,7},{7,6},{8,9},{9,8},{10,11... | collective-permute-start | bytes 1572872 | tf_op jit(solution)/shard_map/ppermute | solution.py:250
  (38 other events, 271.1 us)

commit v4 on v3

--- a/solution.py
+++ b/solution.py
@@ -226,7 +226,7 @@
 
 VMEM = pl.BlockSpec(memory_space=pltpu.VMEM)
 SMEM = pl.BlockSpec(memory_space=pltpu.SMEM)
-COSTS = (2, 3, 2)
+COSTS = (2, 8, 2)
 LATE = 1
 PLANE = 2
 GATHER_AFTER = False

time: 121 us -> 120 us (level)
  starting transfers between devices: 57.4 us -> 49.3 us
  waiting for transfers between devices: 30 us -> 36.2 us
    ppermute x30, starting transfers between devices: 57.4 us -> 49.3 us  [flip(): lax.ppermute(value, axis, [(k, k ^ bits) for k in range(lax.axis_size(axi...]
    ppermute x30, waiting for transfers between devices: 30 us -> 36.2 us  [flip(): lax.ppermute(value, axis, [(k, k ^ bits) for k in range(lax.axis_size(axi...]
where the time goes in v4:
time: 120 us; the launch traced here: 119 us
  starting transfers between devices  49.3 us (41%)
  waiting for transfers between devices  36.2 us (30%)
  Pallas kernels  22.8 us (19%)
  local copies, waits for them, and re-layouts  8.49 us (7%)
  between operations  1.35 us (1%)
    ppermute x30, starting transfers between devices, flip(): lax.ppermute(value, axis, [(k, k ^ bits) for k in range(lax.axis_size(axi...  49.3 us
    ppermute x30, waiting for transfers between devices, flip(): lax.ppermute(value, axis, [(k, k ^ bits) for k in range(lax.axis_size(axi...  36.2 us
    pallas_call x2, Pallas kernels, shards(): pl.pallas_call(functools.partial(chunk_kernel, devs, held, chunk, parts),...  13.5 us
    unnamed x85, local copies, waits for them, and re-layouts  6.88 us
    pallas_call x2, Pallas kernels, shards(): pl.pallas_call(functools.partial(dispatch_kernel, devs, chunks, chunk), g...  6.06 us
    pallas_call x1, Pallas kernels, shards(): pl.pallas_call(functools.partial(combine_kernel, chunks), grid=(1,), out_...  3.17 us
  transfers between devices with their start and end apart: 30, of which 9 were waited for; matrix products, arithmetic and copies ran while one was open for 5% of the time, Pallas kernels for 14%

profile of v4, /device:TPU:0, one launch (start us, length us, event | category | flops | bytes accessed | tf_op | source)
XLA Modules:
  0.0 119.3 jit_solution(14537194482176713731)
XLA Ops:
  0.6 3.1 %dispatch.2 = (bf16[192,128]{1,0:T(8,128)(2,1)}, bf16[32,4096]{1,0:T(8,128)(2,1)}, bf16[32,4096]{1,0:T(8,128)(2,1)}, bf16[32,4096]{1,0:T(8,128)(2,1)}, bf16[32,4096]{1,0:T(8,128)(2,1)}) custom-call(s32[1]{0:T(128)} %bitcast.1.me_ref, s32[2,64]{1,0:T(2,128)} %bitcast.32, f32[2,64]{1,0:T(2,128)} %bitcast.34, bf16[64,4096]{1,0:T(8,128)(2,1)} %tokens_ref.3, ...), custom_call_target="tpu_custom_call" | custom-call | flops 2000000000 | bytes 8388608 | tf_op jit(solution)/shard_map/dispatch/pallas_call | solution.py:284
  4.1 3.0 %collective-permute-start = (bf16[128,1024]{1,0:T(8,128)(2,1)S(1)}, bf16[128,1024]{1,0:T(8,128)(2,1)S(1)}, u32[]{:S(2)}, u32[]{:S(2)}) collective-permute-start(bf16[128,1024]{1,0:T(8,128)(2,1)S(1)} %get-tuple-element.144), channel_id=1, source_target_pairs={{0,8},{8,0},{16,24},{24,16},{1,9},{9,1},{17,25},{25,17},{2,10},{10... | collective-permute-start | bytes 786440 | tf_op jit(solution)/shard_map/ppermute | solution.py:250
  7.1 1.5 %collective-permute-start.3 = (bf16[128,1024]{1,0:T(8,128)(2,1)S(1)}, bf16[128,1024]{1,0:T(8,128)(2,1)S(1)}, u32[]{:S(2)}, u32[]{:S(2)}) collective-permute-start(bf16[128,1024]{1,0:T(8,128)(2,1)S(1)} %get-tuple-element.142), channel_id=1, source_target_pairs={{0,16},{8,24},{16,0},{24,8},{1,17},{9,25},{17,1},{25,9},{2,18},{10... | collective-permute-start | bytes 786440 | tf_op jit(solution)/shard_map/ppermute | solution.py:250
  8.7 1.6 %collective-permute-start.6 = (bf16[32,4096]{1,0:T(8,128)(2,1)}, bf16[32,4096]{1,0:T(8,128)(2,1)S(1)}, u32[]{:S(2)}, u32[]{:S(2)}) collective-permute-start(bf16[32,4096]{1,0:T(8,128)(2,1)} %get-tuple-element.79), channel_id=1, source_target_pairs={{0,2},{1,3},{2,0},{3,1},{4,6},{5,7},{6,4},{7,5},{8,10},{9,11},{10,... | collective-permute-start | bytes 786440 | tf_op jit(solution)/shard_map/ppermute | solution.py:250
  10.2 2.6 %collective-permute-start.7 = (bf16[32,4096]{1,0:T(8,128)(2,1)S(1)}, bf16[32,4096]{1,0:T(8,128)(2,1)S(1)}, u32[]{:S(2)}, u32[]{:S(2)}) collective-permute-start(bf16[32,4096]{1,0:T(8,128)(2,1)S(1)} %copy-done.38), channel_id=1, source_target_pairs={{0,4},{1,5},{2,6},{3,7},{4,0},{5,1},{6,2},{7,3},{8,12},{9,13},{10,... | collective-permute-start | bytes 786440 | tf_op jit(solution)/shard_map/ppermute | solution.py:250
  13.1 3.0 %dispatch.3 = (bf16[192,128]{1,0:T(8,128)(2,1)}, bf16[16,4096]{1,0:T(8,128)(2,1)}, bf16[16,4096]{1,0:T(8,128)(2,1)}, bf16[16,4096]{1,0:T(8,128)(2,1)}, bf16[16,4...) custom-call(s32[1]{0:T(128)} %bitcast.1.me_ref, s32[2,64]{1,0:T(2,128)} %bitcast.33, f32[2,64]{1,0:T(2,128)} %bitcast.35, ...), custom_call_target="tpu_custom_call" | custom-call | flops 2000000000 | bytes 8388608 | tf_op jit(solution)/shard_map/dispatch/pallas_call | solution.py:284
  17.9 3.1 %collective-permute-done.6.refs_3_ = bf16[32,4096]{1,0:T(8,128)(2,1)S(1)} collective-permute-done((bf16[32,4096]{1,0:T(8,128)(2,1)}, bf16[32,4096]{1,0:T(8,128)(2,1)S(1)}, u32[]{:S(2)}, u32[]{:S(2)}) %collective-permute-start.6) | collective-permute-done | bytes 262176 | tf_op jit(solution)/shard_map/ppermute | solution.py:250
  21.1 8.6 %collective-permute-done.8.refs_5_ = bf16[32,4096]{1,0:T(8,128)(2,1)S(1)} collective-permute-done((bf16[32,4096]{1,0:T(8,128)(2,1)}, bf16[32,4096]{1,0:T(8,128)(2,1)S(1)}, u32[]{:S(2)}, u32[]{:S(2)}) %collective-permute-start.8) | collective-permute-done | bytes 262176 | tf_op jit(solution)/shard_map/ppermute | solution.py:250
  29.8 1.9 %collective-permute-done.7.refs_4_ = bf16[32,4096]{1,0:T(8,128)(2,1)S(1)} collective-permute-done((bf16[32,4096]{1,0:T(8,128)(2,1)S(1)}, bf16[32,4096]{1,0:T(8,128)(2,1)S(1)}, u32[]{:S(2)}, u32[]{:S(2)}) %collective-permute-start.7) | collective-permute-done | bytes 262176 | tf_op jit(solution)/shard_map/ppermute | solution.py:250
  33.0 4.3 %collective-permute-start.13 = (bf16[32,4096]{1,0:T(8,128)(2,1)S(1)}, bf16[32,4096]{1,0:T(8,128)(2,1)S(1)}, u32[]{:S(2)}, u32[]{:S(2)}) collective-permute-start(bf16[32,4096]{1,0:T(8,128)(2,1)S(1)} %get-tuple-element.91), channel_id=1, source_target_pairs={{0,2},{1,3},{2,0},{3,1},{4,6},{5,7},{6,4},{7,5},{8,10},{9,11},{10,... | collective-permute-start | bytes 786440 | tf_op jit(solution)/shard_map/ppermute | solution.py:250
  37.4 1.2 %collective-permute-start.15 = (bf16[32,4096]{1,0:T(8,128)(2,1)S(1)}, bf16[32,4096]{1,0:T(8,128)(2,1)S(1)}, u32[]{:S(2)}, u32[]{:S(2)}) collective-permute-start(bf16[32,4096]{1,0:T(8,128)(2,1)S(1)} %get-tuple-element.97), channel_id=1, source_target_pairs={{0,4},{1,5},{2,6},{3,7},{4,0},{5,1},{6,2},{7,3},{8,12},{9,13},{10,... | collective-permute-start | bytes 786440 | tf_op jit(solution)/shard_map/ppermute | solution.py:250
  38.6 1.9 %collective-permute-done.2 = bf16[128,1024]{1,0:T(8,128)(2,1)S(1)} collective-permute-done((bf16[128,1024]{1,0:T(8,128)(2,1)S(1)}, bf16[128,1024]{1,0:T(8,128)(2,1)S(1)}, u32[]{:S(2)}, u32[]{:S(2)}) %collective-permute-start.2) | collective-permute-done | bytes 262176 | tf_op jit(solution)/shard_map/ppermute | solution.py:250
  40.5 2.5 %collective-permute-start.17 = (bf16[32,4096]{1,0:T(8,128)(2,1)S(1)}, bf16[32,4096]{1,0:T(8,128)(2,1)S(1)}, u32[]{:S(2)}, u32[]{:S(2)}) collective-permute-start(bf16[32,4096]{1,0:T(8,128)(2,1)S(1)} %pad_maximum_fusion.8), channel_id=1, source_target_pairs={{0,6},{1,7},{2,4},{3,5},{4,2},{5,3},{6,0},{7,1},{8,14},{9,15},{10,... | collective-permute-start | bytes 786440 | tf_op jit(solution)/shard_map/ppermute | solution.py:250
  43.7 0.8 copy-done.26
  45.0 6.7 %experts.2 = (bf16[32,4096]{1,0:T(8,128)(2,1)}, bf16[32,4096]{1,0:T(8,128)(2,1)}, bf16[32,4096]{1,0:T(8,128)(2,1)}, bf16[32,4096]{1,0:T(8,128)(2,1)}, bf16[264,1...) custom-call(s32[1]{0:T(128)} %bitcast.3.refs_0_, ...), custom_call_target="tpu_custom_call" | custom-call | flops 8000000000 | bytes 8388608 | tf_op jit(solution)/shard_map/experts/pallas_call | solution.py:387
  51.7 4.6 %collective-permute-done.10.refs_8_ = bf16[256,1024]{1,0:T(8,128)(2,1)S(1)} collective-permute-done((bf16[256,1024]{1,0:T(8,128)(2,1)S(1)}, bf16[256,1024]{1,0:T(8,128)(2,1)S(1)}, u32[]{:S(2)}, u32[]{:S(2)}) %collective-permute-start.10) | collective-permute-done | bytes 524320 | tf_op jit(solution)/shard_map/ppermute | solution.py:250
  57.4 1.5 %collective-permute-start.21 = (bf16[264,1024]{1,0:T(8,128)(2,1)}, bf16[264,1024]{1,0:T(8,128)(2,1)S(1)}, u32[]{:S(2)}, u32[]{:S(2)}) collective-permute-start(bf16[264,1024]{1,0:T(8,128)(2,1)} %get-tuple-element.108), channel_id=1, source_target_pairs={{0,16},{8,24},{16,0},{24,8},{1,17},{9,25},{17,1},{25,9},{2,18},{10... | collective-permute-start | bytes 1622024 | tf_op jit(solution)/shard_map/ppermute | solution.py:250
  58.9 0.9 collective-permute-start.22
  59.8 3.4 %collective-permute-start.14 = (bf16[32,4096]{1,0:T(8,128)(2,1)}, bf16[32,4096]{1,0:T(8,128)(2,1)S(1)}, u32[]{:S(2)}, u32[]{:S(2)}) collective-permute-start(bf16[32,4096]{1,0:T(8,128)(2,1)} %get-tuple-element.92), channel_id=1, source_target_pairs={{0,2},{1,3},{2,0},{3,1},{4,6},{5,7},{6,4},{7,5},{8,10},{9,11},{10,... | collective-permute-start | bytes 786440 | tf_op jit(solution)/shard_map/ppermute | solution.py:250
  63.2 1.5 %collective-permute-start.16 = (bf16[32,4096]{1,0:T(8,128)(2,1)}, bf16[32,4096]{1,0:T(8,128)(2,1)S(1)}, u32[]{:S(2)}, u32[]{:S(2)}) collective-permute-start(bf16[32,4096]{1,0:T(8,128)(2,1)} %get-tuple-element.98), channel_id=1, source_target_pairs={{0,4},{1,5},{2,6},{3,7},{4,0},{5,1},{6,2},{7,3},{8,12},{9,13},{10,... | collective-permute-start | bytes 786440 | tf_op jit(solution)/shard_map/ppermute | solution.py:250
  64.7 0.9 slice.92
  65.7 6.9 %experts.3 = (bf16[32,4096]{1,0:T(8,128)(2,1)}, bf16[32,4096]{1,0:T(8,128)(2,1)}, bf16[32,4096]{1,0:T(8,128)(2,1)}, bf16[32,4096]{1,0:T(8,128)(2,1)}, bf16[264,1...) custom-call(s32[1]{0:T(128)} %bitcast.3.refs_0_, ...), custom_call_target="tpu_custom_call" | custom-call | flops 8000000000 | bytes 8388608 | tf_op jit(solution)/shard_map/experts/pallas_call | solution.py:387
  72.6 1.3 %collective-permute-start.18 = (bf16[32,4096]{1,0:T(8,128)(2,1)S(1)}, bf16[32,4096]{1,0:T(8,128)(2,1)S(1)}, u32[]{:S(2)}, u32[]{:S(2)}) collective-permute-start(bf16[32,4096]{1,0:T(8,128)(2,1)S(1)} %copy-done.34), channel_id=1, source_target_pairs={{0,6},{1,7},{2,4},{3,5},{4,2},{5,3},{6,0},{7,1},{8,14},{9,15},{10,... | collective-permute-start | bytes 786440 | tf_op jit(solution)/shard_map/ppermute | solution.py:250
  74.0 7.6 %collective-permute-done.21 = bf16[264,1024]{1,0:T(8,128)(2,1)S(1)} collective-permute-done((bf16[264,1024]{1,0:T(8,128)(2,1)}, bf16[264,1024]{1,0:T(8,128)(2,1)S(1)}, u32[]{:S(2)}, u32[]{:S(2)}) %collective-permute-start.21) | collective-permute-done | bytes 540704 | tf_op jit(solution)/shard_map/ppermute | solution.py:250
  83.7 1.4 %collective-permute-start.25 = (bf16[32,4096]{1,0:T(8,128)(2,1)S(1)}, bf16[32,4096]{1,0:T(8,128)(2,1)S(1)}, u32[]{:S(2)}, u32[]{:S(2)}) collective-permute-start(bf16[32,4096]{1,0:T(8,128)(2,1)S(1)} %copy-done.39), channel_id=1, source_target_pairs={{0,6},{1,7},{2,4},{3,5},{4,2},{5,3},{6,0},{7,1},{8,14},{9,15},{10,... | collective-permute-start | bytes 786440 | tf_op jit(solution)/shard_map/ppermute | solution.py:250
  85.2 2.5 %collective-permute-start.26 = (bf16[264,1024]{1,0:T(8,128)(2,1)S(1)}, bf16[264,1024]{1,0:T(8,128)(2,1)S(1)}, u32[]{:S(2)}, u32[]{:S(2)}) collective-permute-start(bf16[264,1024]{1,0:T(8,128)(2,1)S(1)} %copy-done.23), channel_id=1, source_target_pairs={{0,24},{8,16},{16,8},{24,0},{1,25},{9,17},{17,9},{25,1},{2,26},{10... | collective-permute-start | bytes 1622024 | tf_op jit(solution)/shard_map/ppermute | solution.py:250
  87.6 7.2 %collective-permute-start.23 = (bf16[32,4096]{1,0:T(8,128)(2,1)S(1)}, bf16[32,4096]{1,0:T(8,128)(2,1)S(1)}, u32[]{:S(2)}, u32[]{:S(2)}) collective-permute-start(bf16[32,4096]{1,0:T(8,128)(2,1)S(1)} %copy-done.35), channel_id=1, source_target_pairs={{0,2},{1,3},{2,0},{3,1},{4,6},{5,7},{6,4},{7,5},{8,10},{9,11},{10,... | collective-permute-start | bytes 786440 | tf_op jit(solution)/shard_map/ppermute | solution.py:250
  94.9 7.3 %collective-permute-start.24 = (bf16[32,4096]{1,0:T(8,128)(2,1)S(1)}, bf16[32,4096]{1,0:T(8,128)(2,1)S(1)}, u32[]{:S(2)}, u32[]{:S(2)}) collective-permute-start(bf16[32,4096]{1,0:T(8,128)(2,1)S(1)} %copy-done.36), channel_id=1, source_target_pairs={{0,4},{1,5},{2,6},{3,7},{4,0},{5,1},{6,2},{7,3},{8,12},{9,13},{10,... | collective-permute-start | bytes 786440 | tf_op jit(solution)/shard_map/ppermute | solution.py:250
  102.3 7.8 %collective-permute-done.24.refs_9_ = bf16[32,4096]{1,0:T(8,128)(2,1)S(1)} collective-permute-done((bf16[32,4096]{1,0:T(8,128)(2,1)S(1)}, bf16[32,4096]{1,0:T(8,128)(2,1)S(1)}, u32[]{:S(2)}, u32[]{:S(2)}) %collective-permute-start.24) | collective-permute-done | bytes 262176 | tf_op jit(solution)/shard_map/ppermute | solution.py:250
  111.8 2.7 %copy.13 = f32[128,4,1024]{2,1,0:T(4,128)} copy(f32[128,4,1024]{2,0,1:T(8,128)S(1)} %pad_maximum_fusion) | data formatting | bytes 4194304
  115.1 0.8 copy-done.29
  116.1 3.2 %combine.1 = (bf16[64,4096]{1,0:T(8,128)(2,1)}, bf16[64,4096]{1,0:T(8,128)(2,1)}) custom-call(f32[2,64]{1,0:T(2,128)} %bitcast.36, bf16[192,128]{1,0:T(8,128)(2,1)} %get-tuple-element.67.refs_0_, bf16[192,128]{1,0:T(8,128)(2,1)} %get-tuple-element.68.refs_1_, bf16[32,4096]{1,0:T(8,128)(2,1)} %get-tuple-element.85.refs_2_, bf16[32,4096]{1,0:T(8,128)(2,1)} %copy-done.11, ...), custom_call_target="tpu_custom_call" | custom-call | flops 2000000000 | bytes 8388608 | tf_op jit(solution)/shard_map/combine/pallas_call | solution.py:444
  (150 shorter events, 10.8 us)
Async XLA Ops:
  4.1 12.6 %collective-permute-start = (bf16[128,1024]{1,0:T(8,128)(2,1)S(1)}, bf16[128,1024]{1,0:T(8,128)(2,1)S(1)}, u32[]{:S(2)}, u32[]{:S(2)}) collective-permute-start(bf16[128,1024]{1,0:T(8,128)(2,1)S(1)} %get-tuple-element.144), channel_id=1, source_target_pairs={{0,8},{8,0},{16,24},{24,16},{1,9},{9,1},{17,25},{25,17},{2,10},{10... | collective-permute-start | bytes 786440 | tf_op jit(solution)/shard_map/ppermute | solution.py:250
  7.1 10.3 %collective-permute-start.3 = (bf16[128,1024]{1,0:T(8,128)(2,1)S(1)}, bf16[128,1024]{1,0:T(8,128)(2,1)S(1)}, u32[]{:S(2)}, u32[]{:S(2)}) collective-permute-start(bf16[128,1024]{1,0:T(8,128)(2,1)S(1)} %get-tuple-element.142), channel_id=1, source_target_pairs={{0,16},{8,24},{16,0},{24,8},{1,17},{9,25},{17,1},{25,9},{2,18},{10... | collective-permute-start | bytes 786440 | tf_op jit(solution)/shard_map/ppermute | solution.py:250
  8.7 12.4 %collective-permute-start.6 = (bf16[32,4096]{1,0:T(8,128)(2,1)}, bf16[32,4096]{1,0:T(8,128)(2,1)S(1)}, u32[]{:S(2)}, u32[]{:S(2)}) collective-permute-start(bf16[32,4096]{1,0:T(8,128)(2,1)} %get-tuple-element.79), channel_id=1, source_target_pairs={{0,2},{1,3},{2,0},{3,1},{4,6},{5,7},{6,4},{7,5},{8,10},{9,11},{10,... | collective-permute-start | bytes 786440 | tf_op jit(solution)/shard_map/ppermute | solution.py:250
  10.2 21.4 %collective-permute-start.7 = (bf16[32,4096]{1,0:T(8,128)(2,1)S(1)}, bf16[32,4096]{1,0:T(8,128)(2,1)S(1)}, u32[]{:S(2)}, u32[]{:S(2)}) collective-permute-start(bf16[32,4096]{1,0:T(8,128)(2,1)S(1)} %copy-done.38), channel_id=1, source_target_pairs={{0,4},{1,5},{2,6},{3,7},{4,0},{5,1},{6,2},{7,3},{8,12},{9,13},{10,... | collective-permute-start | bytes 786440 | tf_op jit(solution)/shard_map/ppermute | solution.py:250
  12.8 16.9 %collective-permute-start.8 = (bf16[32,4096]{1,0:T(8,128)(2,1)}, bf16[32,4096]{1,0:T(8,128)(2,1)S(1)}, u32[]{:S(2)}, u32[]{:S(2)}) collective-permute-start(bf16[32,4096]{1,0:T(8,128)(2,1)} %get-tuple-element.81), channel_id=1, source_target_pairs={{0,6},{1,7},{2,4},{3,5},{4,2},{5,3},{6,0},{7,1},{8,14},{9,15},{10,... | collective-permute-start | bytes 786440 | tf_op jit(solution)/shard_map/ppermute | solution.py:250
  16.8 15.0 %collective-permute-start.1 = (bf16[256,1024]{1,0:T(8,128)(2,1)S(1)}, bf16[256,1024]{1,0:T(8,128)(2,1)S(1)}, u32[]{:S(2)}, u32[]{:S(2)}) collective-permute-start(bf16[256,1024]{1,0:T(8,128)(2,1)S(1)} %pad_maximum_fusion.1.refs_7_), channel_id=1, source_target_pairs={{0,16},{8,24},{16,0},{24,8},{1,17},{9,25},{17,1},{25,9},{2,18},{10... | collective-permute-start | bytes 1572872 | tf_op jit(solution)/shard_map/ppermute | solution.py:250
  17.4 15.0 %collective-permute-start.4 = (bf16[256,1024]{1,0:T(8,128)(2,1)S(1)}, bf16[256,1024]{1,0:T(8,128)(2,1)S(1)}, u32[]{:S(2)}, u32[]{:S(2)}) collective-permute-start(bf16[256,1024]{1,0:T(8,128)(2,1)S(1)} %pad_maximum_fusion.2.refs_9_), channel_id=1, source_target_pairs={{0,8},{8,0},{16,24},{24,16},{1,9},{9,1},{17,25},{25,17},{2,10},{10... | collective-permute-start | bytes 1572872 | tf_op jit(solution)/shard_map/ppermute | solution.py:250
  21.0 11.9 %collective-permute-start.12 = (bf16[64,4096]{1,0:T(8,128)(2,1)S(1)}, bf16[64,4096]{1,0:T(8,128)(2,1)S(1)}, u32[]{:S(2)}, u32[]{:S(2)}) collective-permute-start(bf16[64,4096]{1,0:T(8,128)(2,1)S(1)} %copy-done.28), channel_id=1, source_target_pairs={{0,1},{1,0},{2,3},{3,2},{4,5},{5,4},{6,7},{7,6},{8,9},{9,8},{10,11... | collective-permute-start | bytes 1572872 | tf_op jit(solution)/shard_map/ppermute | solution.py:250
  31.7 11.9 %collective-permute-start.9 = (bf16[64,4096]{1,0:T(8,128)(2,1)S(1)}, bf16[64,4096]{1,0:T(8,128)(2,1)S(1)}, u32[]{:S(2)}, u32[]{:S(2)}) collective-permute-start(bf16[64,4096]{1,0:T(8,128)(2,1)S(1)} %pad_maximum_fusion.3), channel_id=1, source_target_pairs={{0,1},{1,0},{2,3},{3,2},{4,5},{5,4},{6,7},{7,6},{8,9},{9,8},{10,11... | collective-permute-start | bytes 1572872 | tf_op jit(solution)/shard_map/ppermute | solution.py:250
  31.8 8.7 %collective-permute-start.2 = (bf16[128,1024]{1,0:T(8,128)(2,1)S(1)}, bf16[128,1024]{1,0:T(8,128)(2,1)S(1)}, u32[]{:S(2)}, u32[]{:S(2)}) collective-permute-start(bf16[128,1024]{1,0:T(8,128)(2,1)S(1)} %get-tuple-element.74), channel_id=1, source_target_pairs={{0,8},{8,0},{16,24},{24,16},{1,9},{9,1},{17,25},{25,17},{2,10},{10... | collective-permute-start | bytes 786440 | tf_op jit(solution)/shard_map/ppermute | solution.py:250
  32.4 10.6 %collective-permute-start.5 = (bf16[128,1024]{1,0:T(8,128)(2,1)S(1)}, bf16[128,1024]{1,0:T(8,128)(2,1)S(1)}, u32[]{:S(2)}, u32[]{:S(2)}) collective-permute-start(bf16[128,1024]{1,0:T(8,128)(2,1)S(1)} %get-tuple-element.77), channel_id=1, source_target_pairs={{0,16},{8,24},{16,0},{24,8},{1,17},{9,25},{17,1},{25,9},{2,18},{10... | collective-permute-start | bytes 786440 | tf_op jit(solution)/shard_map/ppermute | solution.py:250
  33.0 25.9 %collective-permute-start.13 = (bf16[32,4096]{1,0:T(8,128)(2,1)S(1)}, bf16[32,4096]{1,0:T(8,128)(2,1)S(1)}, u32[]{:S(2)}, u32[]{:S(2)}) collective-permute-start(bf16[32,4096]{1,0:T(8,128)(2,1)S(1)} %get-tuple-element.91), channel_id=1, source_target_pairs={{0,2},{1,3},{2,0},{3,1},{4,6},{5,7},{6,4},{7,5},{8,10},{9,11},{10,... | collective-permute-start | bytes 786440 | tf_op jit(solution)/shard_map/ppermute | solution.py:250
  37.4 22.4 %collective-permute-start.15 = (bf16[32,4096]{1,0:T(8,128)(2,1)S(1)}, bf16[32,4096]{1,0:T(8,128)(2,1)S(1)}, u32[]{:S(2)}, u32[]{:S(2)}) collective-permute-start(bf16[32,4096]{1,0:T(8,128)(2,1)S(1)} %get-tuple-element.97), channel_id=1, source_target_pairs={{0,4},{1,5},{2,6},{3,7},{4,0},{5,1},{6,2},{7,3},{8,12},{9,13},{10,... | collective-permute-start | bytes 786440 | tf_op jit(solution)/shard_map/ppermute | solution.py:250
  40.5 22.6 %collective-permute-start.17 = (bf16[32,4096]{1,0:T(8,128)(2,1)S(1)}, bf16[32,4096]{1,0:T(8,128)(2,1)S(1)}, u32[]{:S(2)}, u32[]{:S(2)}) collective-permute-start(bf16[32,4096]{1,0:T(8,128)(2,1)S(1)} %pad_maximum_fusion.8), channel_id=1, source_target_pairs={{0,6},{1,7},{2,4},{3,5},{4,2},{5,3},{6,0},{7,1},{8,14},{9,15},{10,... | collective-permute-start | bytes 786440 | tf_op jit(solution)/shard_map/ppermute | solution.py:250
  43.0 13.3 %collective-permute-start.10 = (bf16[256,1024]{1,0:T(8,128)(2,1)S(1)}, bf16[256,1024]{1,0:T(8,128)(2,1)S(1)}, u32[]{:S(2)}, u32[]{:S(2)}) collective-permute-start(bf16[256,1024]{1,0:T(8,128)(2,1)S(1)} %constant_dynamic-update-slice_fusion.refs_7_), channel_id=1, source_target_pairs={{0,16},{8,24},{16,0},{24,8},{1,17},{9,25},{17,1},{25,9},{2,18},{10... | collective-permute-start | bytes 1572872 | tf_op jit(solution)/shard_map/ppermute | solution.py:250
  44.5 12.9 %collective-permute-start.11 = (bf16[256,1024]{1,0:T(8,128)(2,1)S(1)}, bf16[256,1024]{1,0:T(8,128)(2,1)S(1)}, u32[]{:S(2)}, u32[]{:S(2)}) collective-permute-start(bf16[256,1024]{1,0:T(8,128)(2,1)S(1)} %constant_dynamic-update-slice_fusion.2.refs_9_), channel_id=1, source_target_pairs={{0,8},{8,0},{16,24},{24,16},{1,9},{9,1},{17,25},{25,17},{2,10},{10... | collective-permute-start | bytes 1572872 | tf_op jit(solution)/shard_map/ppermute | solution.py:250
  56.3 16.3 %collective-permute-start.20 = (bf16[264,1024]{1,0:T(8,128)(2,1)}, bf16[264,1024]{1,0:T(8,128)(2,1)S(1)}, u32[]{:S(2)}, u32[]{:S(2)}) collective-permute-start(bf16[264,1024]{1,0:T(8,128)(2,1)} %get-tuple-element.107), channel_id=1, source_target_pairs={{0,24},{8,16},{16,8},{24,0},{1,25},{9,17},{17,9},{25,1},{2,26},{10... | collective-permute-start | bytes 1622024 | tf_op jit(solution)/shard_map/ppermute | solution.py:250
  57.4 24.1 %collective-permute-start.21 = (bf16[264,1024]{1,0:T(8,128)(2,1)}, bf16[264,1024]{1,0:T(8,128)(2,1)S(1)}, u32[]{:S(2)}, u32[]{:S(2)}) collective-permute-start(bf16[264,1024]{1,0:T(8,128)(2,1)} %get-tuple-element.108), channel_id=1, source_target_pairs={{0,16},{8,24},{16,0},{24,8},{1,17},{9,25},{17,1},{25,9},{2,18},{10... | collective-permute-start | bytes 1622024 | tf_op jit(solution)/shard_map/ppermute | solution.py:250
  58.9 23.2 %collective-permute-start.22 = (bf16[264,1024]{1,0:T(8,128)(2,1)}, bf16[264,1024]{1,0:T(8,128)(2,1)S(1)}, u32[]{:S(2)}, u32[]{:S(2)}) collective-permute-start(bf16[264,1024]{1,0:T(8,128)(2,1)} %get-tuple-element.109), channel_id=1, source_target_pairs={{0,8},{8,0},{16,24},{24,16},{1,9},{9,1},{17,25},{25,17},{2,10},{10... | collective-permute-start | bytes 1622024 | tf_op jit(solution)/shard_map/ppermute | solution.py:250
  59.8 25.3 %collective-permute-start.14 = (bf16[32,4096]{1,0:T(8,128)(2,1)}, bf16[32,4096]{1,0:T(8,128)(2,1)S(1)}, u32[]{:S(2)}, u32[]{:S(2)}) collective-permute-start(bf16[32,4096]{1,0:T(8,128)(2,1)} %get-tuple-element.92), channel_id=1, source_target_pairs={{0,2},{1,3},{2,0},{3,1},{4,6},{5,7},{6,4},{7,5},{8,10},{9,11},{10,... | collective-permute-start | bytes 786440 | tf_op jit(solution)/shard_map/ppermute | solution.py:250
  63.2 24.5 %collective-permute-start.16 = (bf16[32,4096]{1,0:T(8,128)(2,1)}, bf16[32,4096]{1,0:T(8,128)(2,1)S(1)}, u32[]{:S(2)}, u32[]{:S(2)}) collective-permute-start(bf16[32,4096]{1,0:T(8,128)(2,1)} %get-tuple-element.98), channel_id=1, source_target_pairs={{0,4},{1,5},{2,6},{3,7},{4,0},{5,1},{6,2},{7,3},{8,12},{9,13},{10,... | collective-permute-start | bytes 786440 | tf_op jit(solution)/shard_map/ppermute | solution.py:250
  72.6 11.0 %collective-permute-start.18 = (bf16[32,4096]{1,0:T(8,128)(2,1)S(1)}, bf16[32,4096]{1,0:T(8,128)(2,1)S(1)}, u32[]{:S(2)}, u32[]{:S(2)}) collective-permute-start(bf16[32,4096]{1,0:T(8,128)(2,1)S(1)} %copy-done.34), channel_id=1, source_target_pairs={{0,6},{1,7},{2,4},{3,5},{4,2},{5,3},{6,0},{7,1},{8,14},{9,15},{10,... | collective-permute-start | bytes 786440 | tf_op jit(solution)/shard_map/ppermute | solution.py:250
  81.5 28.7 %collective-permute-start.28 = (bf16[264,1024]{1,0:T(8,128)(2,1)}, bf16[264,1024]{1,0:T(8,128)(2,1)S(1)}, u32[]{:S(2)}, u32[]{:S(2)}) collective-permute-start(bf16[264,1024]{1,0:T(8,128)(2,1)} %get-tuple-element.124), channel_id=1, source_target_pairs={{0,8},{8,0},{16,24},{24,16},{1,9},{9,1},{17,25},{25,17},{2,10},{10... | collective-permute-start | bytes 1622024 | tf_op jit(solution)/shard_map/ppermute | solution.py:250
  82.1 28.1 %collective-permute-start.27 = (bf16[264,1024]{1,0:T(8,128)(2,1)}, bf16[264,1024]{1,0:T(8,128)(2,1)S(1)}, u32[]{:S(2)}, u32[]{:S(2)}) collective-permute-start(bf16[264,1024]{1,0:T(8,128)(2,1)} %get-tuple-element.123), channel_id=1, source_target_pairs={{0,16},{8,24},{16,0},{24,8},{1,17},{9,25},{17,1},{25,9},{2,18},{10... | collective-permute-start | bytes 1622024 | tf_op jit(solution)/shard_map/ppermute | solution.py:250
  83.7 11.2 %collective-permute-start.25 = (bf16[32,4096]{1,0:T(8,128)(2,1)S(1)}, bf16[32,4096]{1,0:T(8,128)(2,1)S(1)}, u32[]{:S(2)}, u32[]{:S(2)}) collective-permute-start(bf16[32,4096]{1,0:T(8,128)(2,1)S(1)} %copy-done.39), channel_id=1, source_target_pairs={{0,6},{1,7},{2,4},{3,5},{4,2},{5,3},{6,0},{7,1},{8,14},{9,15},{10,... | collective-permute-start | bytes 786440 | tf_op jit(solution)/shard_map/ppermute | solution.py:250
  85.1 24.9 %copy-start.11 = (bf16[32,4096]{1,0:T(8,128)(2,1)}, bf16[32,4096]{1,0:T(8,128)(2,1)S(1)}, u32[]{:S(2)}) copy-start(bf16[32,4096]{1,0:T(8,128)(2,1)S(1)} %collective-permute-done.14.refs_3_) | copy-start | bytes 786436
  85.2 25.1 %collective-permute-start.26 = (bf16[264,1024]{1,0:T(8,128)(2,1)S(1)}, bf16[264,1024]{1,0:T(8,128)(2,1)S(1)}, u32[]{:S(2)}, u32[]{:S(2)}) collective-permute-start(bf16[264,1024]{1,0:T(8,128)(2,1)S(1)} %copy-done.23), channel_id=1, source_target_pairs={{0,24},{8,16},{16,8},{24,0},{1,25},{9,17},{17,9},{25,1},{2,26},{10... | collective-permute-start | bytes 1622024 | tf_op jit(solution)/shard_map/ppermute | solution.py:250
  87.6 22.5 %copy-start.12 = (bf16[32,4096]{1,0:T(8,128)(2,1)}, bf16[32,4096]{1,0:T(8,128)(2,1)S(1)}, u32[]{:S(2)}) copy-start(bf16[32,4096]{1,0:T(8,128)(2,1)S(1)} %collective-permute-done.16.refs_4_) | copy-start | bytes 786436
  87.6 22.5 %collective-permute-start.23 = (bf16[32,4096]{1,0:T(8,128)(2,1)S(1)}, bf16[32,4096]{1,0:T(8,128)(2,1)S(1)}, u32[]{:S(2)}, u32[]{:S(2)}) collective-permute-start(bf16[32,4096]{1,0:T(8,128)(2,1)S(1)} %copy-done.35), channel_id=1, source_target_pairs={{0,2},{1,3},{2,0},{3,1},{4,6},{5,7},{6,4},{7,5},{8,10},{9,11},{10,... | collective-permute-start | bytes 786440 | tf_op jit(solution)/shard_map/ppermute | solution.py:250
  94.9 15.1 %collective-permute-start.24 = (bf16[32,4096]{1,0:T(8,128)(2,1)S(1)}, bf16[32,4096]{1,0:T(8,128)(2,1)S(1)}, u32[]{:S(2)}, u32[]{:S(2)}) collective-permute-start(bf16[32,4096]{1,0:T(8,128)(2,1)S(1)} %copy-done.36), channel_id=1, source_target_pairs={{0,4},{1,5},{2,6},{3,7},{4,0},{5,1},{6,2},{7,3},{8,12},{9,13},{10,... | collective-permute-start | bytes 786440 | tf_op jit(solution)/shard_map/ppermute | solution.py:250
  110.1 5.0 %collective-permute-start.19 = (bf16[64,4096]{1,0:T(8,128)(2,1)S(1)}, bf16[64,4096]{1,0:T(8,128)(2,1)S(1)}, u32[]{:S(2)}, u32[]{:S(2)}) collective-permute-start(bf16[64,4096]{1,0:T(8,128)(2,1)S(1)} %pad_maximum_fusion.4), channel_id=1, source_target_pairs={{0,1},{1,0},{2,3},{3,2},{4,5},{5,4},{6,7},{7,6},{8,9},{9,8},{10,11... | collective-permute-start | bytes 1572872 | tf_op jit(solution)/shard_map/ppermute | solution.py:250
  111.3 3.8 %collective-permute-start.29 = (bf16[64,4096]{1,0:T(8,128)(2,1)S(1)}, bf16[64,4096]{1,0:T(8,128)(2,1)S(1)}, u32[]{:S(2)}, u32[]{:S(2)}) collective-permute-start(bf16[64,4096]{1,0:T(8,128)(2,1)S(1)} %pad_maximum_fusion.5), channel_id=1, source_target_pairs={{0,1},{1,0},{2,3},{3,2},{4,5},{5,4},{6,7},{7,6},{8,9},{9,8},{10,11... | collective-permute-start | bytes 1572872 | tf_op jit(solution)/shard_map/ppermute | solution.py:250
  (38 other events, 227.9 us)
